TPU v7x, 256 devices: a whole 4x4x8 slice. The times are simulated.
256 devices in a mesh: grp: 32 (over x_hi, z, core), dist: 8 (over y, x_lo).
Axes of the slice: x: 4 (x_hi: 2, x_lo: 2; x = x_hi * 2 + x_lo), y: 4, z: 8, core: 2. Of those that a mesh axis runs over, the one named last changes fastest.
Arguments:
- orbitals: bfloat16 [32, 64, 4096], P('grp', 'dist'), may hold values from -6 to 6
- occupations: bfloat16 [32], P('grp'), may hold values from 0.19921875 to 1
Outputs:
- exchange_action: float32 [32, 64, 4096], P('grp', 'dist')
All inputs are finite; a program needn't handle non-finite values.
Results may differ from a plain program's by a relative error of at most 0.0003.
Values may be sent and summed in bfloat16 or wider, within the bound.
No kernel may reach another device: no remote copies, remote signals or barrier semaphores. Data moves between devices by JAX's collectives and lax.ppermute only.
A program may use at most 64 MiB of HBM per device.

v0:
```python
import functools
import math

import jax
import jax.numpy as jnp
import numpy as np
from jax import lax
from jax.experimental import pallas as pl
from jax.experimental.pallas import tpu as pltpu
from jax.sharding import PartitionSpec as P

GRID = 64
GF = 16
GM = 16
box_length = 7.0


def split(x):
    hi = x.astype(jnp.bfloat16)
    lo = (x - hi.astype(jnp.float32)).astype(jnp.bfloat16)
    return hi, lo


def tables():
    position = np.arange(GRID)
    angles = (position[:, None] * position[None, :] % GRID) * (2.0 * math.pi / GRID)
    t = np.cos(angles) + np.sin(angles)
    hi = t.astype(jnp.bfloat16)
    lo = (t - hi.astype(np.float64)).astype(jnp.bfloat16)
    hi, lo = jnp.asarray(hi), jnp.asarray(lo)
    left = jnp.concatenate([hi, hi, lo, lo], axis=1)
    zero = jnp.zeros_like(hi)
    two = lambda m: jnp.concatenate([jnp.concatenate([m, zero], 1), jnp.concatenate([zero, m], 1)], 0)
    wide = jnp.concatenate([two(hi), two(lo)], axis=1)
    right = jnp.concatenate([wide, wide], axis=0)
    return left, right


def green_table():
    p = jnp.arange(GRID, dtype=jnp.int32)
    f = jnp.minimum(p, GRID - p)
    sq = (f * f).astype(jnp.float32)
    tot = sq[:, None, None] + sq[None, :, None] + jnp.concatenate([sq, sq])[None, None, :]
    c = box_length**2 / (math.pi * GRID**3)
    return jnp.where(tot > 0.5, c / jnp.maximum(tot, 1.0), 0.0)


def dot(a, b):
    return jnp.dot(a, b, preferred_element_type=jnp.float32)


def along_lanes(x, right):
    hi, lo = split(x)
    y = dot(jnp.concatenate([hi, lo], axis=1), right)
    return y[:, :128] + y[:, 128:]


def along_rows(left, x):
    hi, lo = split(x)
    return dot(left, jnp.concatenate([hi, lo, hi, lo], axis=0))


def solve_kernel(first, place_ref, order_ref, row_ref, a_ref, b_ref, left_ref, right_ref, green_ref, *refs):
    if first:
        out_ref, f_ref = refs
    else:
        sum_ref, out_ref, f_ref = refs
    where = [order_ref[lax.rem(place_ref[0] - b + 8, 8)] for b in range(8)]
    left = left_ref[...]
    right = right_ref[...]
    low = lax.broadcasted_iota(jnp.int32, (GRID, 128), 1) < 64

    def column(ref, lanes):
        pieces = [ref[where[b], :, lanes] for b in range(8)]
        return jnp.concatenate(pieces, axis=0).astype(jnp.float32)

    def lanes_of(yh):
        return pl.ds(pl.multiple_of(yh * 128, 128), 128)

    def rows_of(step):
        return pl.ds(pl.multiple_of(step * (128 * GF), 128 * GF), 128 * GF)

    def forward(step, _):
        packed = []
        for i in range(GF):
            lanes = lanes_of(step * GF + i)
            row = row_ref[:, lanes].astype(jnp.float32)
            d1 = row * column(a_ref, lanes)
            d2 = row * column(b_ref, lanes)
            packed.append(jnp.where(low, d1, pltpu.roll(d2, 64, 1)))
            packed.append(jnp.where(low, pltpu.roll(d1, 64, 1), d2))
        g = along_lanes(jnp.concatenate(packed, axis=0), right)
        wide = jnp.concatenate([g[64 * i : 64 * i + 64] for i in range(2 * GF)], axis=1)
        h = along_rows(left, wide)
        tall = jnp.concatenate([h[:, 128 * i : 128 * i + 128] for i in range(2 * GF)], axis=0)
        f_ref[rows_of(step), :] = tall
        return 0

    lax.fori_loop(0, 32 // GF, forward, 0)

    def middle(step, _):
        kx = step * GM
        parts = [f_ref[pl.ds(kx + i, 64, stride=64), :] for i in range(GM)]
        h = along_rows(left, jnp.concatenate(parts, axis=1))
        h = h * jnp.concatenate([green_ref[kx + i] for i in range(GM)], axis=1)
        u = along_rows(left, h)
        for i in range(GM):
            f_ref[pl.ds(kx + i, 64, stride=64), :] = u[:, 128 * i : 128 * i + 128]
        return 0

    lax.fori_loop(0, 64 // GM, middle, 0)

    occ_a = -a_ref[0, :, 4096:4224].astype(jnp.float32)[0:1, :]
    occ_b = -b_ref[0, :, 4096:4224].astype(jnp.float32)[0:1, :]

    def backward(step, _):
        h = f_ref[rows_of(step), :]
        wide = jnp.concatenate([h[64 * i : 64 * i + 64] for i in range(2 * GF)], axis=1)
        g = along_rows(left, wide)
        tall = jnp.concatenate([g[:, 128 * i : 128 * i + 128] for i in range(2 * GF)], axis=0)
        p = along_lanes(tall, right)
        for i in range(GF):
            lanes = lanes_of(step * GF + i)
            p0, p1 = p[128 * i : 128 * i + 64], p[128 * i + 64 : 128 * i + 128]
            v1 = jnp.where(low, p0, pltpu.roll(p1, 64, 1))
            v2 = jnp.where(low, pltpu.roll(p0, 64, 1), p1)
            term = v1 * (column(a_ref, lanes) * occ_a) + v2 * (column(b_ref, lanes) * occ_b)
            if not first:
                term = sum_ref[:, lanes] + term
            out_ref[:, lanes] = term
        return 0

    lax.fori_loop(0, 32 // GF, backward, 0)
    if not first:
        level = jnp.zeros((GRID, 128), jnp.float32)
        for i in range(32):
            level = jnp.maximum(level, jnp.abs(out_ref[:, 128 * i : 128 * i + 128]))
        peak = jnp.maximum(jnp.max(level, axis=(0, 1), keepdims=True), 1e-30)
        power = jnp.ceil(jnp.log2(jnp.broadcast_to(peak, (8, 128)))) - 15.0
        factor = jnp.exp2(-power)[0:1]
        for i in range(32):
            lanes = slice(128 * i, 128 * i + 128)
            out_ref[:, lanes] = out_ref[:, lanes] * factor
        out_ref[:, 4096:4224] = jnp.broadcast_to(power[0:1], (GRID, 128))


def solve(place, row, a, b, left, right, green, *more):
    vm = pl.BlockSpec(memory_space=pltpu.VMEM)
    sm = pl.BlockSpec(memory_space=pltpu.SMEM)
    order = jnp.asarray(np.argsort(ORDER), jnp.int32)
    width = GRID * GRID + (128 if more else 0)
    return pl.pallas_call(
        functools.partial(solve_kernel, not more),
        out_shape=jax.ShapeDtypeStruct((GRID, width), jnp.float32),
        in_specs=[sm, sm] + [vm] * (6 + len(more)),
        out_specs=vm,
        scratch_shapes=[pltpu.VMEM((GRID * GRID, 128), jnp.float32)],
        cost_estimate=pl.CostEstimate(flops=10**10, bytes_accessed=10**7, transcendentals=0),
        compiler_params=pltpu.CompilerParams(vmem_limit_bytes=32 * 2**20),
        name="solve",
    )(place, order, row, a, b, left, right, green, *more)


AXES = ("grp", "dist")
ORDER = (0, 4, 3, 5, 2, 6, 1, 7)


def device(half, z, core, lane):
    return ((half * 8 + z) * 2 + core) * 8 + lane


def moved(x, rule):
    pairs = [
        (device(h, z, c, l), device(*rule(h, z, c, l)))
        for h in range(2)
        for z in range(8)
        for c in range(2)
        for l in range(8)
    ]
    return lax.ppermute(x, AXES, pairs)


def body(orbitals, occupations):
    return exchange(orbitals[0], occupations[0])


def exchange(mine, occupation):
    slice_out = jnp.concatenate([mine, jnp.broadcast_to(occupation, (8, 128))], axis=1)
    turned = moved(slice_out, lambda h, z, c, l: (h, l, c, z))
    copies = jnp.broadcast_to(mine, (8, *mine.shape))
    row = lax.all_to_all(copies, "dist", split_axis=0, concat_axis=0, tiled=True)
    row = row.reshape(GRID, GRID * GRID)
    pieces = []
    for k in ORDER:
        piece = turned
        if k:
            piece = moved(turned, lambda h, z, c, l, k=k: (h, (z + k) % 8, c, l))
        pieces.append(piece)
    col = jnp.stack(pieces)
    far = []
    for i in range(2):
        half = jnp.stack(pieces[4 * i : 4 * i + 4])
        far.append(moved(half, lambda h, z, c, l: (1 - h, z, c, l)))
    core_col = moved(col, lambda h, z, c, l: (h, z, 1 - c, l))
    place = ((lax.axis_index("grp") >> 1) & 7).astype(jnp.int32).reshape(1)
    left, right = tables()
    green = green_table()
    partial = solve(place, row, col, core_col, left, right, green)
    far, partial = lax.optimization_barrier((far, partial))
    far_col = jnp.concatenate(far)
    far_core_col = moved(far_col, lambda h, z, c, l: (h, z, 1 - c, l))
    partial = solve(place, row, far_col, far_core_col, left, right, green, partial)
    sent = partial.astype(jnp.float16).reshape(8, 8, GRID * GRID + 128)
    arrived = lax.all_to_all(sent, "dist", split_axis=0, concat_axis=0, tiled=True)
    power = lax.optimization_barrier(arrived[:, 0:1, GRID * GRID : GRID * GRID + 1])
    terms = arrived[:, :, : GRID * GRID].astype(jnp.float32) * jnp.exp2(power.astype(jnp.float32))
    return terms.sum(axis=0)[None]


def solution(mesh):
    in_specs = (P("grp", "dist", None), P("grp"))
    out_specs = P("grp", "dist", None)
    return jax.shard_map(body, mesh=mesh, in_specs=in_specs, out_specs=out_specs, check_vma=False)
```

profile of v0, /device:TPU:32, one launch (start us, length us, event | category | flops | bytes accessed | tf_op | source)
XLA Modules:
  0.0 80.2 jit_solution(14954723806166433339)
XLA Ops:
  0.7 0.8 %concatenate.36 = bf16[8,4224]{1,0:T(8,128)(2,1)S(1)} pad(bf16[8,4096]{1,0:T(8,128)(2,1)} %bitcast.34, bf16[]{:T(256)} %bitcast.23), padding=0_0x0_128 | pad | bytes 133122 | tf_op jit(solution)/shard_map/concatenate | solution.py:188
  1.5 2.9 %collective-permute-start = (bf16[8,4224]{1,0:T(8,128)(2,1)S(1)}, bf16[8,4224]{1,0:T(8,128)(2,1)S(1)}, u32[]{:S(2)}, u32[]{:S(2)}) collective-permute-start(bf16[8,4224]{1,0:T(8,128)(2,1)S(1)} %concatenate.36), channel_id=1, source_target_pairs={{0,0},{1,16},{2,32},{3,48},{4,64},{5,80},{6,96},{7,112},{8,8},{9,2... | collective-permute-start | bytes 202760 | tf_op jit(solution)/shard_map/ppermute | solution.py:180
  4.4 1.7 %broadcast_in_dim.8 = bf16[8,8,4096]{2,1,0:T(8,128)(2,1)} broadcast(bf16[8,4096]{1,0:T(8,128)(2,1)} %bitcast.35), dimensions={1,2} | broadcast | bytes 589824 | tf_op jit(solution)/shard_map/broadcast_in_dim | solution.py:190
  6.1 10.4 %all-to-all-start = ((bf16[8,8,4096]{2,1,0:T(8,128)(2,1)}), bf16[8,8,4096]{2,1,0:T(8,128)(2,1)S(1)}, u32[]{:S(2)}, u32[]{:S(2)}) async-start(bf16[8,8,4096]{2,1,0:T(8,128)(2,1)} %broadcast_in_dim.8), calls=%async_computation | async-start | bytes 1048576 | tf_op jit(solution)/shard_map/all_to_all | solution.py:191
  16.7 0.6 fusion.1.green_ref
  17.4 0.6 collective-permute-start.8
  18.0 1.5 %collective-permute-start.7 = (bf16[8,4224]{1,0:T(8,128)(2,1)S(1)}, bf16[8,4224]{1,0:T(8,128)(2,1)S(1)}, u32[]{:S(2)}, u32[]{:S(2)}) collective-permute-start(bf16[8,4224]{1,0:T(8,128)(2,1)S(1)} %collective-permute-done), channel_id=1, source_target_pairs={{0,16},{1,17},{2,18},{3,19},{4,20},{5,21},{6,22},{7,23},{8,24},{9,... | collective-permute-start | bytes 202760 | tf_op jit(solution)/shard_map/ppermute | solution.py:180
  19.5 5.2 %collective-permute-start.6 = (bf16[8,4224]{1,0:T(8,128)(2,1)S(1)}, bf16[8,4224]{1,0:T(8,128)(2,1)S(1)}, u32[]{:S(2)}, u32[]{:S(2)}) collective-permute-start(bf16[8,4224]{1,0:T(8,128)(2,1)S(1)} %collective-permute-done), channel_id=1, source_target_pairs={{0,96},{1,97},{2,98},{3,99},{4,100},{5,101},{6,102},{7,103},{8,104... | collective-permute-start | bytes 202760 | tf_op jit(solution)/shard_map/ppermute | solution.py:180
  24.7 2.4 %collective-permute-start.3 = (bf16[8,4224]{1,0:T(8,128)(2,1)S(1)}, bf16[8,4224]{1,0:T(8,128)(2,1)S(1)}, u32[]{:S(2)}, u32[]{:S(2)}) collective-permute-start(bf16[8,4224]{1,0:T(8,128)(2,1)S(1)} %collective-permute-done), channel_id=1, source_target_pairs={{0,80},{1,81},{2,82},{3,83},{4,84},{5,85},{6,86},{7,87},{8,88},{9,... | collective-permute-start | bytes 202760 | tf_op jit(solution)/shard_map/ppermute | solution.py:180
  27.1 2.8 %collective-permute-start.2 = (bf16[8,4224]{1,0:T(8,128)(2,1)S(1)}, bf16[8,4224]{1,0:T(8,128)(2,1)S(1)}, u32[]{:S(2)}, u32[]{:S(2)}) collective-permute-start(bf16[8,4224]{1,0:T(8,128)(2,1)S(1)} %collective-permute-done), channel_id=1, source_target_pairs={{0,48},{1,49},{2,50},{3,51},{4,52},{5,53},{6,54},{7,55},{8,56},{9,... | collective-permute-start | bytes 202760 | tf_op jit(solution)/shard_map/ppermute | solution.py:180
  29.8 2.4 %collective-permute-start.1 = (bf16[8,4224]{1,0:T(8,128)(2,1)S(1)}, bf16[8,4224]{1,0:T(8,128)(2,1)S(1)}, u32[]{:S(2)}, u32[]{:S(2)}) collective-permute-start(bf16[8,4224]{1,0:T(8,128)(2,1)S(1)} %collective-permute-done), channel_id=1, source_target_pairs={{0,64},{1,65},{2,66},{3,67},{4,68},{5,69},{6,70},{7,71},{8,72},{9,... | collective-permute-start | bytes 202760 | tf_op jit(solution)/shard_map/ppermute | solution.py:180
  32.2 5.8 %collective-permute-done.5 = bf16[8,4224]{1,0:T(8,128)(2,1)S(1)} collective-permute-done((bf16[8,4224]{1,0:T(8,128)(2,1)S(1)}, bf16[8,4224]{1,0:T(8,128)(2,1)S(1)}, u32[]{:S(2)}, u32[]{:S(2)}) %collective-permute-start.5) | collective-permute-done | bytes 67616 | tf_op jit(solution)/shard_map/ppermute | solution.py:180
  38.0 0.8 pad_maximum_fusion.1
  38.7 2.8 %collective-permute-start.9 = (bf16[4,8,4224]{2,1,0:T(8,128)(2,1)}, bf16[4,8,4224]{2,1,0:T(8,128)(2,1)}, u32[]{:S(2)}, u32[]{:S(2)}) collective-permute-start(bf16[4,8,4224]{2,1,0:T(8,128)(2,1)} %pad_maximum_fusion.1), channel_id=1, source_target_pairs={{0,128},{1,129},{2,130},{3,131},{4,132},{5,133},{6,134},{7,135},{8... | collective-permute-start | bytes 811016 | tf_op jit(solution)/shard_map/ppermute | solution.py:180
  41.8 0.8 pad_maximum_fusion
  42.6 0.7 collective-permute-start.4
  43.9 8.4 %solve.2.refs_0_ = f32[64,4096]{1,0:T(8,128)S(1)} custom-call(s32[1]{0:T(128)} %bitcast.place_ref, s32[8]{0:T(128)S(1)} %copy-done.2, bf16[64,4096]{1,0:T(8,128)(2,1)S(1)} %bitcast.24, bf16[8,8,4224]{2,1,0:T(8,128)(2,1)S(1)} %constant_dynamic-update-slice_fusion.a_ref, bf16[8,8,4224]{2,1,0:T(8,128)(2,1)} %collective-permute-done.10.b_ref, ...), custom_call_target="tpu_custom_call" | custom-call | flops 10000000000 | bytes 10000000 | tf_op jit(solution)/shard_map/solve/pallas_call | solution.py:152
  52.3 1.0 %collective-permute-done.4 = bf16[4,8,4224]{2,1,0:T(8,128)(2,1)} collective-permute-done((bf16[4,8,4224]{2,1,0:T(8,128)(2,1)}, bf16[4,8,4224]{2,1,0:T(8,128)(2,1)}, u32[]{:S(2)}, u32[]{:S(2)}) %collective-permute-start.4) | collective-permute-done | bytes 270368 | tf_op jit(solution)/shard_map/ppermute | solution.py:180
  53.3 1.0 %constant_dynamic-update-slice_fusion.9 = bf16[8,8,4224]{2,1,0:T(8,128)(2,1)S(1)} fusion(bf16[4,8,4224]{2,1,0:T(8,128)(2,1)} %collective-permute-done.4), kind=kLoop, calls=%fused_computation.17 | loop fusion | bytes 540672
  54.2 1.0 %constant_dynamic-update-slice_fusion.8.a_ref = bf16[8,8,4224]{2,1,0:T(8,128)(2,1)S(1)} fusion(bf16[8,8,4224]{2,1,0:T(8,128)(2,1)S(1)} %constant_dynamic-update-slice_fusion.9, bf16[4,8,4224]{2,1,0:T(8,128)(2,1)} %collective-permute-done.9), kind=kLoop, calls=%fused_computation.16 | loop fusion | bytes 540672 | tf_op jit(solution)/shard_map/concatenate | solution.py:210
  55.5 1.9 %collective-permute-done.11.b_ref = bf16[8,8,4224]{2,1,0:T(8,128)(2,1)S(1)} collective-permute-done((bf16[8,8,4224]{2,1,0:T(8,128)(2,1)S(1)}, bf16[8,8,4224]{2,1,0:T(8,128)(2,1)S(1)}, u32[]{:S(2)}, u32[]{:S(2)}) %collective-permute-start.11) | collective-permute-done | bytes 540704 | tf_op jit(solution)/shard_map/ppermute | solution.py:180
  57.4 8.2 %solve.3 = f32[64,4224]{1,0:T(8,128)S(1)} custom-call(s32[1]{0:T(128)} %bitcast.place_ref, s32[8]{0:T(128)S(1)} %copy-done.2, bf16[64,4096]{1,0:T(8,128)(2,1)S(1)} %bitcast.25, bf16[8,8,4224]{2,1,0:T(8,128)(2,1)S(1)} %constant_dynamic-update-slice_fusion.8.a_ref, bf16[8,8,4224]{2,1,0:T(8,128)(2,1)S(1)} %collective-permute-done.11.b_ref, ...), custom_call_target="tpu_custom_call" | custom-call | flops 10000000000 | bytes 10000000 | tf_op jit(solution)/shard_map/solve/pallas_call | solution.py:152
  65.7 13.5 %all_to_all.10 = f16[8,8,4224]{2,1,0:T(8,128)(2,1)S(1)} all-to-all(f16[8,8,4224]{2,1,0:T(8,128)(2,1)S(1)} %convert_bitcast_fusion), channel_id=1, replica_groups=mesh['grp'=32,'dist'=8] {'dist'}, dimensions={0} | all-to-all | bytes 1081344 | tf_op jit(solution)/shard_map/all_to_all | solution.py:214
  79.4 0.8 %multiply_reduce_fusion = f32[8,4096]{1,0:T(8,128)} fusion(f16[8,8,4224]{2,1,0:T(8,128)(2,1)S(1)} %all_to_all.10, f32[8]{0:T(128)S(1)} %exponential_reduce_fusion), kind=kLoop, calls=%fused_computation.4 | loop fusion | flops 753664 | bytes 655392 | tf_op jit(solution)/shard_map/reduce_sum | solution.py:217
  (33 shorter events, 1.5 us)
Async XLA Ops:
  1.5 15.8 %collective-permute-start = (bf16[8,4224]{1,0:T(8,128)(2,1)S(1)}, bf16[8,4224]{1,0:T(8,128)(2,1)S(1)}, u32[]{:S(2)}, u32[]{:S(2)}) collective-permute-start(bf16[8,4224]{1,0:T(8,128)(2,1)S(1)} %concatenate.36), channel_id=1, source_target_pairs={{0,0},{1,16},{2,32},{3,48},{4,64},{5,80},{6,96},{7,112},{8,8},{9,2... | collective-permute-start | bytes 202760 | tf_op jit(solution)/shard_map/ppermute | solution.py:180
  6.1 37.2 %all-to-all-start = ((bf16[8,8,4096]{2,1,0:T(8,128)(2,1)}), bf16[8,8,4096]{2,1,0:T(8,128)(2,1)S(1)}, u32[]{:S(2)}, u32[]{:S(2)}) async-start(bf16[8,8,4096]{2,1,0:T(8,128)(2,1)} %broadcast_in_dim.8), calls=%async_computation | async-start | bytes 1048576 | tf_op jit(solution)/shard_map/all_to_all | solution.py:191
  16.7 27.2 %copy-start = (bf16[256,256]{1,0:T(8,128)(2,1)S(1)}, bf16[256,256]{1,0:T(8,128)(2,1)}, u32[]{:S(2)}) copy-start(bf16[256,256]{1,0:T(8,128)(2,1)} %constant.53.right_ref) | copy-start | bytes 393220
  16.7 27.2 %copy-start.1 = (bf16[64,256]{1,0:T(8,128)(2,1)S(1)}, bf16[64,256]{1,0:T(8,128)(2,1)}, u32[]{:S(2)}) copy-start(bf16[64,256]{1,0:T(8,128)(2,1)} %constant.45.left_ref) | copy-start | bytes 98308
  16.7 27.2 %copy-start.2 = (s32[8]{0:T(128)S(1)}, s32[8]{0:T(128)}, u32[]{:S(2)}) copy-start(s32[8]{0:T(128)} %constant.32.clone.order_ref) | copy-start | bytes 100
  17.4 9.7 %collective-permute-start.8 = (bf16[8,4224]{1,0:T(8,128)(2,1)S(1)}, bf16[8,4224]{1,0:T(8,128)(2,1)S(1)}, u32[]{:S(2)}, u32[]{:S(2)}) collective-permute-start(bf16[8,4224]{1,0:T(8,128)(2,1)S(1)} %collective-permute-done), channel_id=1, source_target_pairs={{0,112},{1,113},{2,114},{3,115},{4,116},{5,117},{6,118},{7,119},{8... | collective-permute-start | bytes 202760 | tf_op jit(solution)/shard_map/ppermute | solution.py:180
  18.0 11.8 %collective-permute-start.7 = (bf16[8,4224]{1,0:T(8,128)(2,1)S(1)}, bf16[8,4224]{1,0:T(8,128)(2,1)S(1)}, u32[]{:S(2)}, u32[]{:S(2)}) collective-permute-start(bf16[8,4224]{1,0:T(8,128)(2,1)S(1)} %collective-permute-done), channel_id=1, source_target_pairs={{0,16},{1,17},{2,18},{3,19},{4,20},{5,21},{6,22},{7,23},{8,24},{9,... | collective-permute-start | bytes 202760 | tf_op jit(solution)/shard_map/ppermute | solution.py:180
  19.5 12.7 %collective-permute-start.6 = (bf16[8,4224]{1,0:T(8,128)(2,1)S(1)}, bf16[8,4224]{1,0:T(8,128)(2,1)S(1)}, u32[]{:S(2)}, u32[]{:S(2)}) collective-permute-start(bf16[8,4224]{1,0:T(8,128)(2,1)S(1)} %collective-permute-done), channel_id=1, source_target_pairs={{0,96},{1,97},{2,98},{3,99},{4,100},{5,101},{6,102},{7,103},{8,104... | collective-permute-start | bytes 202760 | tf_op jit(solution)/shard_map/ppermute | solution.py:180
  24.7 13.3 %collective-permute-start.5 = (bf16[8,4224]{1,0:T(8,128)(2,1)S(1)}, bf16[8,4224]{1,0:T(8,128)(2,1)S(1)}, u32[]{:S(2)}, u32[]{:S(2)}) collective-permute-start(bf16[8,4224]{1,0:T(8,128)(2,1)S(1)} %collective-permute-done), channel_id=1, source_target_pairs={{0,32},{1,33},{2,34},{3,35},{4,36},{5,37},{6,38},{7,39},{8,40},{9,... | collective-permute-start | bytes 202760 | tf_op jit(solution)/shard_map/ppermute | solution.py:180
  24.7 16.9 %collective-permute-start.3 = (bf16[8,4224]{1,0:T(8,128)(2,1)S(1)}, bf16[8,4224]{1,0:T(8,128)(2,1)S(1)}, u32[]{:S(2)}, u32[]{:S(2)}) collective-permute-start(bf16[8,4224]{1,0:T(8,128)(2,1)S(1)} %collective-permute-done), channel_id=1, source_target_pairs={{0,80},{1,81},{2,82},{3,83},{4,84},{5,85},{6,86},{7,87},{8,88},{9,... | collective-permute-start | bytes 202760 | tf_op jit(solution)/shard_map/ppermute | solution.py:180
  27.1 14.5 %collective-permute-start.2 = (bf16[8,4224]{1,0:T(8,128)(2,1)S(1)}, bf16[8,4224]{1,0:T(8,128)(2,1)S(1)}, u32[]{:S(2)}, u32[]{:S(2)}) collective-permute-start(bf16[8,4224]{1,0:T(8,128)(2,1)S(1)} %collective-permute-done), channel_id=1, source_target_pairs={{0,48},{1,49},{2,50},{3,51},{4,52},{5,53},{6,54},{7,55},{8,56},{9,... | collective-permute-start | bytes 202760 | tf_op jit(solution)/shard_map/ppermute | solution.py:180
  29.8 11.8 %collective-permute-start.1 = (bf16[8,4224]{1,0:T(8,128)(2,1)S(1)}, bf16[8,4224]{1,0:T(8,128)(2,1)S(1)}, u32[]{:S(2)}, u32[]{:S(2)}) collective-permute-start(bf16[8,4224]{1,0:T(8,128)(2,1)S(1)} %collective-permute-done), channel_id=1, source_target_pairs={{0,64},{1,65},{2,66},{3,67},{4,68},{5,69},{6,70},{7,71},{8,72},{9,... | collective-permute-start | bytes 202760 | tf_op jit(solution)/shard_map/ppermute | solution.py:180
  38.7 13.5 %collective-permute-start.9 = (bf16[4,8,4224]{2,1,0:T(8,128)(2,1)}, bf16[4,8,4224]{2,1,0:T(8,128)(2,1)}, u32[]{:S(2)}, u32[]{:S(2)}) collective-permute-start(bf16[4,8,4224]{2,1,0:T(8,128)(2,1)} %pad_maximum_fusion.1), channel_id=1, source_target_pairs={{0,128},{1,129},{2,130},{3,131},{4,132},{5,133},{6,134},{7,135},{8... | collective-permute-start | bytes 811016 | tf_op jit(solution)/shard_map/ppermute | solution.py:180
  41.7 2.2 %collective-permute-start.10 = (bf16[8,8,4224]{2,1,0:T(8,128)(2,1)S(1)}, bf16[8,8,4224]{2,1,0:T(8,128)(2,1)}, u32[]{:S(2)}, u32[]{:S(2)}) collective-permute-start(bf16[8,8,4224]{2,1,0:T(8,128)(2,1)S(1)} %constant_dynamic-update-slice_fusion.a_ref), channel_id=1, source_target_pairs={{0,8},{1,9},{2,10},{3,11},{4,12},{5,13},{6,14},{7,15},{8,0},{9,1},... | collective-permute-start | bytes 1622024 | tf_op jit(solution)/shard_map/ppermute | solution.py:180
  42.6 10.7 %collective-permute-start.4 = (bf16[4,8,4224]{2,1,0:T(8,128)(2,1)}, bf16[4,8,4224]{2,1,0:T(8,128)(2,1)}, u32[]{:S(2)}, u32[]{:S(2)}) collective-permute-start(bf16[4,8,4224]{2,1,0:T(8,128)(2,1)} %pad_maximum_fusion), channel_id=1, source_target_pairs={{0,128},{1,129},{2,130},{3,131},{4,132},{5,133},{6,134},{7,135},{8... | collective-permute-start | bytes 811016 | tf_op jit(solution)/shard_map/ppermute | solution.py:180
  55.2 2.2 %collective-permute-start.11 = (bf16[8,8,4224]{2,1,0:T(8,128)(2,1)S(1)}, bf16[8,8,4224]{2,1,0:T(8,128)(2,1)S(1)}, u32[]{:S(2)}, u32[]{:S(2)}) collective-permute-start(bf16[8,8,4224]{2,1,0:T(8,128)(2,1)S(1)} %constant_dynamic-update-slice_fusion.8.a_ref), channel_id=1, source_target_pairs={{0,8},{1,9},{2,10},{3,11},{4,12},{5,13},{6,14},{7,15},{8,0},{9,1},... | collective-permute-start | bytes 1622024 | tf_op jit(solution)/shard_map/ppermute | solution.py:180
where the time goes:
time: 80.6 us; the launch traced here: 80.2 us
  starting transfers between devices  32 us (40%)
  Pallas kernels  16.6 us (21%)
  blocking collectives  13.5 us (17%)
  waiting for transfers between devices  9.34 us (12%)
  local copies, waits for them, and re-layouts  4.59 us (6%)
  other arithmetic  3.33 us (4%)
  between operations  0.81 us (1%)
    ppermute x12, starting transfers between devices, moved(): return lax.ppermute(x, AXES, pairs)  21.6 us
    pallas_call x2, Pallas kernels, solve(): pl.pallas_call(functools.partial(solve_kernel, not more), out_shape=jax.S...  16.6 us
    all_to_all x1, blocking collectives, exchange(): lax.all_to_all(sent, 'dist', split_axis=0, concat_axis=0, tiled=True)  13.5 us
    all_to_all x1, starting transfers between devices, exchange(): lax.all_to_all(copies, 'dist', split_axis=0, concat_axis=0, tiled=True)  10.4 us
    ppermute x12, waiting for transfers between devices, moved(): return lax.ppermute(x, AXES, pairs)  9.33 us
    broadcast_in_dim x1, local copies, waits for them, and re-layouts, exchange(): copies = jnp.broadcast_to(mine, (8, *mine.shape))  1.67 us
  transfers between devices with their start and end apart: 13, of which 4 were waited for; matrix products, arithmetic and copies ran while one was open for 5% of the time, Pallas kernels for 10%

commit v1 on v0

v1 whole, which is shorter than its diff:
```python
import functools
import math

import jax
import jax.numpy as jnp
import numpy as np
from jax import lax
from jax.experimental import pallas as pl
from jax.experimental.pallas import tpu as pltpu
from jax.sharding import PartitionSpec as P

GRID = 64
GM = 32
PITCH = 65
box_length = 7.0


def split(x):
    hi = x.astype(jnp.bfloat16)
    lo = (x - hi.astype(jnp.float32)).astype(jnp.bfloat16)
    return hi, lo


def tables():
    position = np.arange(GRID)
    angles = (position[:, None] * position[None, :] % GRID) * (2.0 * math.pi / GRID)
    t = np.cos(angles) + np.sin(angles)
    hi = t.astype(jnp.bfloat16)
    lo = (t - hi.astype(np.float64)).astype(jnp.bfloat16)
    hi, lo = jnp.asarray(hi), jnp.asarray(lo)
    left = jnp.concatenate([hi, hi, lo], axis=1)
    zero = jnp.zeros_like(hi)
    two = lambda m: jnp.concatenate([jnp.concatenate([m, zero], 1), jnp.concatenate([zero, m], 1)], 0)
    wide = jnp.concatenate([two(hi), two(lo)], axis=1)
    right = jnp.concatenate([wide, wide], axis=0)
    return left, right


def green_table():
    p = jnp.arange(GRID, dtype=jnp.int32)
    f = jnp.minimum(p, GRID - p)
    sq = (f * f).astype(jnp.float32)
    tot = sq[:, None, None] + sq[None, :, None] + jnp.concatenate([sq, sq])[None, None, :]
    c = box_length**2 / (math.pi * GRID**3)
    return jnp.where(tot > 0.5, c / jnp.maximum(tot, 1.0), 0.0)


def dot(a, b):
    return jnp.dot(a, b, preferred_element_type=jnp.float32)


def along_lanes(x, right):
    hi, lo = split(x)
    y = dot(jnp.concatenate([hi, lo], axis=1), right)
    return y[:, :128] + y[:, 128:]


def along_rows(left, x):
    hi, lo = split(x)
    return dot(left, jnp.concatenate([hi, lo, hi], axis=0))


def solve_kernel(first, seat_ref, row_ref, *refs):
    sources = ((refs[0], refs[1]), (refs[2], refs[3]))
    left_ref, right_ref, green_ref = refs[4:7]
    col_ref, f_ref = refs[-2:]
    out_ref = refs[-3]
    group = seat_ref[0]
    core = jnp.bitwise_and(group, 1)
    z = jnp.bitwise_and(jnp.right_shift(group, 1), 7)

    for member in range(2):
        for block in range(8):
            away = jnp.bitwise_and(block - z + 8, 7)
            hops = jnp.where(away > 4, 8 - away, away)
            single = jnp.logical_or(away == 0, away == 4)
            holder = jnp.where(single, member, jnp.where(away > 4, 0, 1))
            paired = 8 - 2 * hops + jnp.bitwise_xor(holder, member)
            index = jnp.where(single, jnp.right_shift(away, 2), paired)
            rows = slice(8 * block, 8 * block + 8)
            for other in range(2):
                for half in range(2):
                    here = jnp.bitwise_xor(holder, core) == other
                    here = jnp.logical_and(here, jnp.right_shift(index, 2) == half)

                    @pl.when(here)
                    def _():
                        piece = sources[other][half][jnp.bitwise_and(index, 3)]
                        col_ref[member, rows, :] = piece.astype(jnp.float32)

    left = left_ref[...]
    right = right_ref[...]
    low = lax.broadcasted_iota(jnp.int32, (GRID, 128), 1) < 64

    packed = []
    for i in range(32):
        lanes = slice(128 * i, 128 * i + 128)
        row = row_ref[:, lanes].astype(jnp.float32)
        d1 = row * col_ref[0, :, lanes]
        d2 = row * col_ref[1, :, lanes]
        packed.append(jnp.where(low, d1, pltpu.roll(d2, 64, 1)))
        packed.append(jnp.where(low, pltpu.roll(d1, 64, 1), d2))
    g = along_lanes(jnp.concatenate(packed, axis=0), right)
    wide = jnp.concatenate([g[64 * i : 64 * i + 64] for i in range(64)], axis=1)
    h = along_rows(left, wide)
    for i in range(64):
        f_ref[PITCH * i : PITCH * i + 64, :] = h[:, 128 * i : 128 * i + 128]

    def middle(step, _):
        kx = step * GM
        parts = [f_ref[pl.ds(kx + i, 64, stride=PITCH), :] for i in range(GM)]
        h = along_rows(left, jnp.concatenate(parts, axis=1))
        h = h * jnp.concatenate([green_ref[kx + i] for i in range(GM)], axis=1)
        u = along_rows(left, h)
        for i in range(GM):
            f_ref[pl.ds(kx + i, 64, stride=PITCH), :] = u[:, 128 * i : 128 * i + 128]
        return 0

    lax.fori_loop(0, 64 // GM, middle, 0)

    occ = [-col_ref[member, 0:1, 4096:4224] for member in range(2)]
    wide = jnp.concatenate([f_ref[PITCH * i : PITCH * i + 64, :] for i in range(64)], axis=1)
    g = along_rows(left, wide)
    tall = jnp.concatenate([g[:, 128 * i : 128 * i + 128] for i in range(64)], axis=0)
    p = along_lanes(tall, right)
    for i in range(32):
        lanes = slice(128 * i, 128 * i + 128)
        p0, p1 = p[128 * i : 128 * i + 64], p[128 * i + 64 : 128 * i + 128]
        v1 = jnp.where(low, p0, pltpu.roll(p1, 64, 1))
        v2 = jnp.where(low, pltpu.roll(p0, 64, 1), p1)
        term = v1 * (col_ref[0, :, lanes] * occ[0]) + v2 * (col_ref[1, :, lanes] * occ[1])
        if not first:
            term = refs[7][:, lanes] + term
        out_ref[:, lanes] = term

    if not first:
        level = jnp.zeros((GRID, 128), jnp.float32)
        for i in range(32):
            level = jnp.maximum(level, jnp.abs(out_ref[:, 128 * i : 128 * i + 128]))
        peak = jnp.maximum(jnp.max(level, axis=(0, 1), keepdims=True), 1e-30)
        power = jnp.ceil(jnp.log2(jnp.broadcast_to(peak, (8, 128)))) - 15.0
        factor = jnp.exp2(-power)[0:1]
        for i in range(32):
            lanes = slice(128 * i, 128 * i + 128)
            out_ref[:, lanes] = out_ref[:, lanes] * factor
        out_ref[:, 4096:4224] = jnp.broadcast_to(power[0:1], (GRID, 128))


def solve(seat, row, mine, other, left, right, green, *more):
    vm = pl.BlockSpec(memory_space=pltpu.VMEM)
    sm = pl.BlockSpec(memory_space=pltpu.SMEM)
    width = GRID * GRID + (128 if more else 0)
    return pl.pallas_call(
        functools.partial(solve_kernel, not more),
        out_shape=jax.ShapeDtypeStruct((GRID, width), jnp.float32),
        in_specs=[sm] + [vm] * (8 + len(more)),
        out_specs=vm,
        scratch_shapes=[
            pltpu.VMEM((2, GRID, GRID * GRID + 128), jnp.float32),
            pltpu.VMEM((GRID * PITCH, 128), jnp.float32),
        ],
        cost_estimate=pl.CostEstimate(flops=10**10, bytes_accessed=10**7, transcendentals=0),
        compiler_params=pltpu.CompilerParams(vmem_limit_bytes=40 * 2**20),
        name="solve",
    )(seat, row, *mine, *other, left, right, green, *more)


AXES = ("grp", "dist")


def device(half, z, core, lane):
    return ((half * 8 + z) * 2 + core) * 8 + lane


def moved(x, rule):
    pairs = [
        (device(h, z, c, l), device(*rule(h, z, c, l)))
        for h in range(2)
        for z in range(8)
        for c in range(2)
        for l in range(8)
    ]
    return lax.ppermute(x, AXES, pairs)


def body(orbitals, occupations):
    return exchange(orbitals[0], occupations[0])


def cores(h, z, c, l):
    return (h, z, 1 - c, l)


def exchange(mine, occupation):
    slice_out = jnp.concatenate([mine, jnp.broadcast_to(occupation, (8, 128))], axis=1)
    kept = moved(slice_out, lambda h, z, c, l: (h, l, c, z))
    crossed = moved(slice_out, lambda h, z, c, l: (h, l, 1 - c, z))
    copies = jnp.broadcast_to(mine, (8, *mine.shape))
    row = lax.all_to_all(copies, "dist", split_axis=0, concat_axis=0, tiled=True)
    row = row.reshape(GRID, GRID * GRID)
    pair = jnp.stack([kept, crossed])
    fourth = moved(kept, lambda h, z, c, l: (h, (z + 4) % 8, c, l))
    shifted = {}
    for k in (3, 2, 1):
        rule = lambda h, z, c, l, k=k: (h, (z + (k if c == 0 else 8 - k)) % 8, c, l)
        shifted[k] = moved(pair, rule)
    halves = [
        jnp.concatenate([kept[None], fourth[None], shifted[3]]),
        jnp.concatenate([shifted[2], shifted[1]]),
    ]
    far, core = [], []
    for half in halves:
        far.append(moved(half, lambda h, z, c, l: (1 - h, z, c, l)))
        core.append(moved(half, cores))
    far_core = [moved(far[0], cores)]
    seat = lax.axis_index("grp").astype(jnp.int32).reshape(1)
    left, right = tables()
    green = green_table()
    partial = solve(seat, row, halves, core, left, right, green)
    last, partial = lax.optimization_barrier((far[1], partial))
    far[1] = last
    far_core.append(moved(last, cores))
    partial = solve(seat, row, far, far_core, left, right, green, partial)
    sent = partial.astype(jnp.float16).reshape(8, 8, GRID * GRID + 128)
    arrived = lax.all_to_all(sent, "dist", split_axis=0, concat_axis=0, tiled=True)
    power = lax.optimization_barrier(arrived[:, 0:1, GRID * GRID : GRID * GRID + 1])
    terms = arrived[:, :, : GRID * GRID].astype(jnp.float32) * jnp.exp2(power.astype(jnp.float32))
    return terms.sum(axis=0)[None]


def solution(mesh):
    in_specs = (P("grp", "dist", None), P("grp"))
    out_specs = P("grp", "dist", None)
    return jax.shard_map(body, mesh=mesh, in_specs=in_specs, out_specs=out_specs, check_vma=False)
```

time: 80.6 us -> 81.5 us (1.011)
  the two profiles are of different devices: /device:TPU:32 before, /device:TPU:4 now
where the time goes in v1:
time: 81.5 us; the launch traced here: 81.1 us
  starting transfers between devices  31.2 us (38%)
  blocking collectives  16.2 us (20%)
  waiting for transfers between devices  15.2 us (19%)
  Pallas kernels  12.4 us (15%)
  local copies, waits for them, and re-layouts  3.45 us (4%)
  other arithmetic  1.86 us (2%)
    ppermute x12, starting transfers between devices, moved(): return lax.ppermute(x, AXES, pairs)  17 us
    all_to_all x1, blocking collectives, exchange(): lax.all_to_all(sent, 'dist', split_axis=0, concat_axis=0, tiled=True)  16.2 us
    ppermute x12, waiting for transfers between devices, moved(): return lax.ppermute(x, AXES, pairs)  15.2 us
    all_to_all x1, starting transfers between devices, exchange(): lax.all_to_all(copies, 'dist', split_axis=0, concat_axis=0, tiled=True)  14.2 us
    pallas_call x2, Pallas kernels, solve(): pl.pallas_call(functools.partial(solve_kernel, not more), out_shape=jax.S...  12.4 us
    broadcast_in_dim x1, local copies, waits for them, and re-layouts, exchange(): copies = jnp.broadcast_to(mine, (8, *mine.shape))  1.67 us
  transfers between devices with their start and end apart: 13, of which 5 were waited for; matrix products, arithmetic and copies ran while one was open for 3% of the time, Pallas kernels for 7%

profile of v1, /device:TPU:4, one launch (start us, length us, event | category | flops | bytes accessed | tf_op | source)
XLA Modules:
  0.0 81.1 jit_solution(14639259327921844711)
XLA Ops:
  0.7 0.8 %concatenate.39 = bf16[8,4224]{1,0:T(8,128)(2,1)S(1)} pad(bf16[8,4096]{1,0:T(8,128)(2,1)} %bitcast.15, bf16[]{:T(256)} %bitcast.10), padding=0_0x0_128 | pad | bytes 133122 | tf_op jit(solution)/shard_map/concatenate | solution.py:195
  1.5 0.7 collective-permute-start
  2.2 1.7 %broadcast_in_dim.21 = bf16[8,8,4096]{2,1,0:T(8,128)(2,1)} broadcast(bf16[8,4096]{1,0:T(8,128)(2,1)} %bitcast.16), dimensions={1,2} | broadcast | bytes 589824 | tf_op jit(solution)/shard_map/broadcast_in_dim | solution.py:198
  3.8 14.2 %all-to-all-start = ((bf16[8,8,4096]{2,1,0:T(8,128)(2,1)}), bf16[8,8,4096]{2,1,0:T(8,128)(2,1)S(1)}, u32[]{:S(2)}, u32[]{:S(2)}) async-start(bf16[8,8,4096]{2,1,0:T(8,128)(2,1)} %broadcast_in_dim.21), calls=%async_computation | async-start | bytes 1048576 | tf_op jit(solution)/shard_map/all_to_all | solution.py:199
  18.2 4.5 %collective-permute-start.3 = (bf16[2,8,4224]{2,1,0:T(8,128)(2,1)S(1)}, bf16[2,8,4224]{2,1,0:T(8,128)(2,1)S(1)}, u32[]{:S(2)}, u32[]{:S(2)}) collective-permute-start(bf16[2,8,4224]{2,1,0:T(8,128)(2,1)S(1)} %pad_maximum_fusion.1), channel_id=1, source_target_pairs={{0,48},{1,49},{2,50},{3,51},{4,52},{5,53},{6,54},{7,55},{8,88},{9,... | collective-permute-start | bytes 405512 | tf_op jit(solution)/shard_map/ppermute | solution.py:183
  22.7 6.9 %collective-permute-start.1 = (bf16[8,4224]{1,0:T(8,128)(2,1)S(1)}, bf16[8,4224]{1,0:T(8,128)(2,1)S(1)}, u32[]{:S(2)}, u32[]{:S(2)}) collective-permute-start(bf16[8,4224]{1,0:T(8,128)(2,1)S(1)} %collective-permute-done), channel_id=1, source_target_pairs={{0,64},{1,65},{2,66},{3,67},{4,68},{5,69},{6,70},{7,71},{8,72},{9,... | collective-permute-start | bytes 202760 | tf_op jit(solution)/shard_map/ppermute | solution.py:183
  29.7 0.6 collective-permute-start.5
  30.3 6.1 %collective-permute-done.1 = bf16[8,4224]{1,0:T(8,128)(2,1)S(1)} collective-permute-done((bf16[8,4224]{1,0:T(8,128)(2,1)S(1)}, bf16[8,4224]{1,0:T(8,128)(2,1)S(1)}, u32[]{:S(2)}, u32[]{:S(2)}) %collective-permute-start.1) | collective-permute-done | bytes 67616 | tf_op jit(solution)/shard_map/ppermute | solution.py:183
  36.4 0.1 collective-permute-start.8
  36.5 1.8 %collective-permute-done.5 = bf16[2,8,4224]{2,1,0:T(8,128)(2,1)S(1)} collective-permute-done((bf16[2,8,4224]{2,1,0:T(8,128)(2,1)S(1)}, bf16[2,8,4224]{2,1,0:T(8,128)(2,1)S(1)}, u32[]{:S(2)}, u32[]{:S(2)}) %collective-permute-start.5) | collective-permute-done | bytes 135200 | tf_op jit(solution)/shard_map/ppermute | solution.py:183
  38.4 0.1 collective-permute-start.9
  38.5 0.6 fusion.1.refs_6_
  39.1 1.6 %collective-permute-start.4 = (bf16[4,8,4224]{2,1,0:T(8,128)(2,1)S(1)}, bf16[4,8,4224]{2,1,0:T(8,128)(2,1)S(1)}, u32[]{:S(2)}, u32[]{:S(2)}) collective-permute-start(bf16[4,8,4224]{2,1,0:T(8,128)(2,1)S(1)} %pad_maximum_fusion.refs_0_), channel_id=1, source_target_pairs={{0,128},{1,129},{2,130},{3,131},{4,132},{5,133},{6,134},{7,135},{8... | collective-permute-start | bytes 811016 | tf_op jit(solution)/shard_map/ppermute | solution.py:183
  40.6 2.1 %collective-permute-start.7 = (bf16[4,8,4224]{2,1,0:T(8,128)(2,1)S(1)}, bf16[4,8,4224]{2,1,0:T(8,128)(2,1)}, u32[]{:S(2)}, u32[]{:S(2)}) collective-permute-start(bf16[4,8,4224]{2,1,0:T(8,128)(2,1)S(1)} %constant_dynamic-update-slice_fusion.refs_1_), channel_id=1, source_target_pairs={{0,128},{1,129},{2,130},{3,131},{4,132},{5,133},{6,134},{7,135},{8... | collective-permute-start | bytes 811016 | tf_op jit(solution)/shard_map/ppermute | solution.py:183
  42.7 0.9 %copy-done = bf16[256,256]{1,0:T(8,128)(2,1)S(1)} copy-done((bf16[256,256]{1,0:T(8,128)(2,1)S(1)}, bf16[256,256]{1,0:T(8,128)(2,1)}, u32[]{:S(2)}) %copy-start) | copy-done | bytes 131096
  43.6 5.9 %solve.2.refs_7_ = f32[64,4096]{1,0:T(8,128)S(1)} custom-call(s32[1]{0:T(128)} %bitcast.seat_ref, bf16[64,4096]{1,0:T(8,128)(2,1)S(1)} %bitcast.11, bf16[4,8,4224]{2,1,0:T(8,128)(2,1)S(1)} %pad_maximum_fusion.refs_0_, bf16[4,8,4224]{2,1,0:T(8,128)(2,1)S(1)} %constant_dynamic-update-slice_fusion.refs_1_, bf16[4,8,4224]{2,1,0:T(8,128)(2,1)} %collective-permute-done.8.refs_2_, ...), custom_call_target="tpu_custom_call" | custom-call | flops 10000000000 | bytes 10000000 | tf_op jit(solution)/shard_map/solve/pallas_call | solution.py:153
  49.6 5.9 %collective-permute-done.7.refs_1_ = bf16[4,8,4224]{2,1,0:T(8,128)(2,1)} collective-permute-done((bf16[4,8,4224]{2,1,0:T(8,128)(2,1)S(1)}, bf16[4,8,4224]{2,1,0:T(8,128)(2,1)}, u32[]{:S(2)}, u32[]{:S(2)}) %collective-permute-start.7) | collective-permute-done | bytes 270368 | tf_op jit(solution)/shard_map/ppermute | solution.py:183
  55.5 0.5 collective-permute-start.11
  56.0 1.0 %collective-permute-done.10.refs_2_ = bf16[4,8,4224]{2,1,0:T(8,128)(2,1)S(1)} collective-permute-done((bf16[4,8,4224]{2,1,0:T(8,128)(2,1)S(1)}, bf16[4,8,4224]{2,1,0:T(8,128)(2,1)S(1)}, u32[]{:S(2)}, u32[]{:S(2)}) %collective-permute-start.10) | collective-permute-done | bytes 270368 | tf_op jit(solution)/shard_map/ppermute | solution.py:183
  57.0 0.4 collective-permute-done.11.refs_3_
  57.4 6.4 %solve.3 = f32[64,4224]{1,0:T(8,128)S(1)} custom-call(s32[1]{0:T(128)} %bitcast.seat_ref, bf16[64,4096]{1,0:T(8,128)(2,1)S(1)} %bitcast.12, bf16[4,8,4224]{2,1,0:T(8,128)(2,1)S(1)} %collective-permute-done.4.refs_0_, bf16[4,8,4224]{2,1,0:T(8,128)(2,1)} %collective-permute-done.7.refs_1_, bf16[4,8,4224]{2,1,0:T(8,128)(2,1)S(1)} %collective-permute-done.10.refs_2_, ...), custom_call_target="tpu_custom_call" | custom-call | flops 10000000000 | bytes 10000000 | tf_op jit(solution)/shard_map/solve/pallas_call | solution.py:153
  63.9 16.2 %all_to_all.10 = f16[8,8,4224]{2,1,0:T(8,128)(2,1)S(1)} all-to-all(f16[8,8,4224]{2,1,0:T(8,128)(2,1)S(1)} %convert_bitcast_fusion), channel_id=1, replica_groups=mesh['grp'=32,'dist'=8] {'dist'}, dimensions={0} | all-to-all | bytes 1081344 | tf_op jit(solution)/shard_map/all_to_all | solution.py:225
  80.1 0.2 exponential_reduce_fusion
  80.2 0.8 %multiply_reduce_fusion = f32[8,4096]{1,0:T(8,128)} fusion(f16[8,8,4224]{2,1,0:T(8,128)(2,1)S(1)} %all_to_all.10, f32[8]{0:T(128)S(1)} %exponential_reduce_fusion), kind=kLoop, calls=%fused_computation.4 | loop fusion | flops 753664 | bytes 655392 | tf_op jit(solution)/shard_map/reduce_sum | solution.py:228
  (23 shorter events, 0.4 us)
Async XLA Ops:
  1.5 16.6 %collective-permute-start.2 = (bf16[8,4224]{1,0:T(8,128)(2,1)S(1)}, bf16[8,4224]{1,0:T(8,128)(2,1)S(1)}, u32[]{:S(2)}, u32[]{:S(2)}) collective-permute-start(bf16[8,4224]{1,0:T(8,128)(2,1)S(1)} %concatenate.39), channel_id=1, source_target_pairs={{0,8},{1,24},{2,40},{3,56},{4,72},{5,88},{6,104},{7,120},{8,0},{9,... | collective-permute-start | bytes 202760 | tf_op jit(solution)/shard_map/ppermute | solution.py:183
  1.5 16.6 %collective-permute-start = (bf16[8,4224]{1,0:T(8,128)(2,1)S(1)}, bf16[8,4224]{1,0:T(8,128)(2,1)S(1)}, u32[]{:S(2)}, u32[]{:S(2)}) collective-permute-start(bf16[8,4224]{1,0:T(8,128)(2,1)S(1)} %concatenate.39), channel_id=1, source_target_pairs={{0,0},{1,16},{2,32},{3,48},{4,64},{5,80},{6,96},{7,112},{8,8},{9,2... | collective-permute-start | bytes 202760 | tf_op jit(solution)/shard_map/ppermute | solution.py:183
  3.8 38.9 %copy-start.1 = (bf16[64,192]{1,0:T(8,128)(2,1)S(1)}, bf16[64,192]{1,0:T(8,128)(2,1)}, u32[]{:S(2)}) copy-start(bf16[64,192]{1,0:T(8,128)(2,1)} %constant.38.refs_4_) | copy-start | bytes 73732
  3.8 38.9 %all-to-all-start = ((bf16[8,8,4096]{2,1,0:T(8,128)(2,1)}), bf16[8,8,4096]{2,1,0:T(8,128)(2,1)S(1)}, u32[]{:S(2)}, u32[]{:S(2)}) async-start(bf16[8,8,4096]{2,1,0:T(8,128)(2,1)} %broadcast_in_dim.21), calls=%async_computation | async-start | bytes 1048576 | tf_op jit(solution)/shard_map/all_to_all | solution.py:199
  18.2 18.2 %collective-permute-start.3 = (bf16[2,8,4224]{2,1,0:T(8,128)(2,1)S(1)}, bf16[2,8,4224]{2,1,0:T(8,128)(2,1)S(1)}, u32[]{:S(2)}, u32[]{:S(2)}) collective-permute-start(bf16[2,8,4224]{2,1,0:T(8,128)(2,1)S(1)} %pad_maximum_fusion.1), channel_id=1, source_target_pairs={{0,48},{1,49},{2,50},{3,51},{4,52},{5,53},{6,54},{7,55},{8,88},{9,... | collective-permute-start | bytes 405512 | tf_op jit(solution)/shard_map/ppermute | solution.py:183
  22.7 13.6 %collective-permute-start.1 = (bf16[8,4224]{1,0:T(8,128)(2,1)S(1)}, bf16[8,4224]{1,0:T(8,128)(2,1)S(1)}, u32[]{:S(2)}, u32[]{:S(2)}) collective-permute-start(bf16[8,4224]{1,0:T(8,128)(2,1)S(1)} %collective-permute-done), channel_id=1, source_target_pairs={{0,64},{1,65},{2,66},{3,67},{4,68},{5,69},{6,70},{7,71},{8,72},{9,... | collective-permute-start | bytes 202760 | tf_op jit(solution)/shard_map/ppermute | solution.py:183
  29.7 8.6 %collective-permute-start.6 = (bf16[2,8,4224]{2,1,0:T(8,128)(2,1)S(1)}, bf16[2,8,4224]{2,1,0:T(8,128)(2,1)S(1)}, u32[]{:S(2)}, u32[]{:S(2)}) collective-permute-start(bf16[2,8,4224]{2,1,0:T(8,128)(2,1)S(1)} %pad_maximum_fusion.1), channel_id=1, source_target_pairs={{0,16},{1,17},{2,18},{3,19},{4,20},{5,21},{6,22},{7,23},{8,120},{9... | collective-permute-start | bytes 405512 | tf_op jit(solution)/shard_map/ppermute | solution.py:183
  29.7 8.6 %collective-permute-start.5 = (bf16[2,8,4224]{2,1,0:T(8,128)(2,1)S(1)}, bf16[2,8,4224]{2,1,0:T(8,128)(2,1)S(1)}, u32[]{:S(2)}, u32[]{:S(2)}) collective-permute-start(bf16[2,8,4224]{2,1,0:T(8,128)(2,1)S(1)} %pad_maximum_fusion.1), channel_id=1, source_target_pairs={{0,32},{1,33},{2,34},{3,35},{4,36},{5,37},{6,38},{7,39},{8,104},{9... | collective-permute-start | bytes 405512 | tf_op jit(solution)/shard_map/ppermute | solution.py:183
  36.4 6.3 %collective-permute-start.8 = (bf16[4,8,4224]{2,1,0:T(8,128)(2,1)S(1)}, bf16[4,8,4224]{2,1,0:T(8,128)(2,1)}, u32[]{:S(2)}, u32[]{:S(2)}) collective-permute-start(bf16[4,8,4224]{2,1,0:T(8,128)(2,1)S(1)} %pad_maximum_fusion.refs_0_), channel_id=1, source_target_pairs={{0,8},{1,9},{2,10},{3,11},{4,12},{5,13},{6,14},{7,15},{8,0},{9,1},... | collective-permute-start | bytes 811016 | tf_op jit(solution)/shard_map/ppermute | solution.py:183
  38.4 4.3 %collective-permute-start.9 = (bf16[4,8,4224]{2,1,0:T(8,128)(2,1)S(1)}, bf16[4,8,4224]{2,1,0:T(8,128)(2,1)}, u32[]{:S(2)}, u32[]{:S(2)}) collective-permute-start(bf16[4,8,4224]{2,1,0:T(8,128)(2,1)S(1)} %constant_dynamic-update-slice_fusion.refs_1_), channel_id=1, source_target_pairs={{0,8},{1,9},{2,10},{3,11},{4,12},{5,13},{6,14},{7,15},{8,0},{9,1},... | collective-permute-start | bytes 811016 | tf_op jit(solution)/shard_map/ppermute | solution.py:183
  39.1 16.4 %collective-permute-start.4 = (bf16[4,8,4224]{2,1,0:T(8,128)(2,1)S(1)}, bf16[4,8,4224]{2,1,0:T(8,128)(2,1)S(1)}, u32[]{:S(2)}, u32[]{:S(2)}) collective-permute-start(bf16[4,8,4224]{2,1,0:T(8,128)(2,1)S(1)} %pad_maximum_fusion.refs_0_), channel_id=1, source_target_pairs={{0,128},{1,129},{2,130},{3,131},{4,132},{5,133},{6,134},{7,135},{8... | collective-permute-start | bytes 811016 | tf_op jit(solution)/shard_map/ppermute | solution.py:183
  40.6 14.8 %collective-permute-start.7 = (bf16[4,8,4224]{2,1,0:T(8,128)(2,1)S(1)}, bf16[4,8,4224]{2,1,0:T(8,128)(2,1)}, u32[]{:S(2)}, u32[]{:S(2)}) collective-permute-start(bf16[4,8,4224]{2,1,0:T(8,128)(2,1)S(1)} %constant_dynamic-update-slice_fusion.refs_1_), channel_id=1, source_target_pairs={{0,128},{1,129},{2,130},{3,131},{4,132},{5,133},{6,134},{7,135},{8... | collective-permute-start | bytes 811016 | tf_op jit(solution)/shard_map/ppermute | solution.py:183
  42.7 0.9 %copy-start = (bf16[256,256]{1,0:T(8,128)(2,1)S(1)}, bf16[256,256]{1,0:T(8,128)(2,1)}, u32[]{:S(2)}) copy-start(bf16[256,256]{1,0:T(8,128)(2,1)} %constant.46.refs_5_) | copy-start | bytes 393220
  55.5 1.5 %collective-permute-start.10 = (bf16[4,8,4224]{2,1,0:T(8,128)(2,1)S(1)}, bf16[4,8,4224]{2,1,0:T(8,128)(2,1)S(1)}, u32[]{:S(2)}, u32[]{:S(2)}) collective-permute-start(bf16[4,8,4224]{2,1,0:T(8,128)(2,1)S(1)} %collective-permute-done.4.refs_0_), channel_id=1, source_target_pairs={{0,8},{1,9},{2,10},{3,11},{4,12},{5,13},{6,14},{7,15},{8,0},{9,1},... | collective-permute-start | bytes 811016 | tf_op jit(solution)/shard_map/ppermute | solution.py:183
  55.5 1.9 %collective-permute-start.11 = (bf16[4,8,4224]{2,1,0:T(8,128)(2,1)}, bf16[4,8,4224]{2,1,0:T(8,128)(2,1)S(1)}, u32[]{:S(2)}, u32[]{:S(2)}) collective-permute-start(bf16[4,8,4224]{2,1,0:T(8,128)(2,1)} %collective-permute-done.7.refs_1_), channel_id=1, source_target_pairs={{0,8},{1,9},{2,10},{3,11},{4,12},{5,13},{6,14},{7,15},{8,0},{9,1},... | collective-permute-start | bytes 811016 | tf_op jit(solution)/shard_map/ppermute | solution.py:183

commit v2 on v1

--- a/solution.py
+++ b/solution.py
@@ -75,8 +75,8 @@
             hops = jnp.where(away > 4, 8 - away, away)
             single = jnp.logical_or(away == 0, away == 4)
             holder = jnp.where(single, member, jnp.where(away > 4, 0, 1))
-            paired = 8 - 2 * hops + jnp.bitwise_xor(holder, member)
-            index = jnp.where(single, jnp.right_shift(away, 2), paired)
+            paired = jnp.where(hops == 1, 6, 6 - 2 * hops) + jnp.bitwise_xor(holder, member)
+            index = jnp.where(single, 4 + jnp.right_shift(away, 2), paired)
             rows = slice(8 * block, 8 * block + 8)
             for other in range(2):
                 for half in range(2):
@@ -191,35 +191,38 @@
     return (h, z, 1 - c, l)
 
 
+def ring(k):
+    return lambda h, z, c, l: (h, (z + (k if c == 0 else 8 - k)) % 8, c, l)
+
+
 def exchange(mine, occupation):
     slice_out = jnp.concatenate([mine, jnp.broadcast_to(occupation, (8, 128))], axis=1)
     kept = moved(slice_out, lambda h, z, c, l: (h, l, c, z))
-    crossed = moved(slice_out, lambda h, z, c, l: (h, l, 1 - c, z))
     copies = jnp.broadcast_to(mine, (8, *mine.shape))
     row = lax.all_to_all(copies, "dist", split_axis=0, concat_axis=0, tiled=True)
     row = row.reshape(GRID, GRID * GRID)
+    seat = lax.axis_index("grp").astype(jnp.int32).reshape(1)
+    left, right = (jnp.where(seat[0] >= 0, t, 0) for t in tables())
+    left, right, green, kept = lax.optimization_barrier((left, right, green_table(), kept))
+    crossed = moved(kept, cores)
     pair = jnp.stack([kept, crossed])
-    fourth = moved(kept, lambda h, z, c, l: (h, (z + 4) % 8, c, l))
     shifted = {}
     for k in (3, 2, 1):
-        rule = lambda h, z, c, l, k=k: (h, (z + (k if c == 0 else 8 - k)) % 8, c, l)
-        shifted[k] = moved(pair, rule)
+        shifted[k] = moved(pair, ring(k))
+    fourth = moved(shifted[3][0], ring(1))
     halves = [
-        jnp.concatenate([kept[None], fourth[None], shifted[3]]),
-        jnp.concatenate([shifted[2], shifted[1]]),
+        jnp.concatenate([shifted[3], shifted[2]]),
+        jnp.concatenate([kept[None], fourth[None], shifted[1]]),
     ]
     far, core = [], []
     for half in halves:
         far.append(moved(half, lambda h, z, c, l: (1 - h, z, c, l)))
         core.append(moved(half, cores))
-    far_core = [moved(far[0], cores)]
-    seat = lax.axis_index("grp").astype(jnp.int32).reshape(1)
-    left, right = tables()
-    green = green_table()
     partial = solve(seat, row, halves, core, left, right, green)
-    last, partial = lax.optimization_barrier((far[1], partial))
-    far[1] = last
-    far_core.append(moved(last, cores))
+    far, partial = lax.optimization_barrier((far, partial))
+    far_core = []
+    for half in far:
+        far_core.append(moved(half, cores))
     partial = solve(seat, row, far, far_core, left, right, green, partial)
     sent = partial.astype(jnp.float16).reshape(8, 8, GRID * GRID + 128)
     arrived = lax.all_to_all(sent, "dist", split_axis=0, concat_axis=0, tiled=True)

time: 81.5 us -> 79.9 us (0.980)
  the two profiles are of different devices: /device:TPU:4 before, /device:TPU:8 now
where the time goes in v2:
time: 79.9 us; the launch traced here: 78.7 us
  starting transfers between devices  30.2 us (38%)
  waiting for transfers between devices  16.1 us (20%)
  blocking collectives  14.9 us (19%)
  Pallas kernels  12.2 us (15%)
  other arithmetic  2.8 us (4%)
  local copies, waits for them, and re-layouts  1.72 us (2%)
  between operations  0.82 us (1%)
    ppermute x12, starting transfers between devices, moved(): return lax.ppermute(x, AXES, pairs)  21.8 us
    ppermute x12, waiting for transfers between devices, moved(): return lax.ppermute(x, AXES, pairs)  16.1 us
    all_to_all x1, blocking collectives, exchange(): lax.all_to_all(sent, 'dist', split_axis=0, concat_axis=0, tiled=True)  14.9 us
    pallas_call x2, Pallas kernels, solve(): pl.pallas_call(functools.partial(solve_kernel, not more), out_shape=jax.S...  12.2 us
    all_to_all x1, starting transfers between devices, exchange(): lax.all_to_all(copies, 'dist', split_axis=0, concat_axis=0, tiled=True)  8.38 us
  transfers between devices with their start and end apart: 13, of which 8 were waited for; matrix products, arithmetic and copies ran while one was open for 3% of the time, Pallas kernels for 8%

profile of v2, /device:TPU:8, one launch (start us, length us, event | category | flops | bytes accessed | tf_op | source)
XLA Modules:
  0.0 78.7 jit_solution(982676859630442139)
XLA Ops:
  0.7 0.8 %concatenate.49 = bf16[8,4224]{1,0:T(8,128)(2,1)S(1)} pad(bf16[8,4096]{1,0:T(8,128)(2,1)} %bitcast.17, bf16[]{:T(256)} %bitcast.12), padding=0_0x0_128 | pad | bytes 133122 | tf_op jit(solution)/shard_map/concatenate | solution.py:199
  1.5 5.1 %collective-permute-start = (bf16[8,4224]{1,0:T(8,128)(2,1)S(1)}, bf16[8,4224]{1,0:T(8,128)(2,1)S(1)}, u32[]{:S(2)}, u32[]{:S(2)}) collective-permute-start(bf16[8,4224]{1,0:T(8,128)(2,1)S(1)} %concatenate.49), channel_id=1, source_target_pairs={{0,0},{1,16},{2,32},{3,48},{4,64},{5,80},{6,96},{7,112},{8,8},{9,2... | collective-permute-start | bytes 202760 | tf_op jit(solution)/shard_map/ppermute | solution.py:183
  6.8 0.9 %broadcast_select_fusion.refs_5_ = bf16[256,256]{1,0:T(8,128)(2,1)S(1)} fusion(bf16[256,256]{1,0:T(8,128)(2,1)} %constant.49, pred[]{:T(512)S(6)} %ge.4), kind=kLoop, calls=%fused_computation.8 | loop fusion | flops 65536 | bytes 262145 | tf_op jit(solution)/shard_map/jit(_where)/select_n | solution.py:205
  7.7 0.6 fusion.1.refs_6_
  8.3 1.2 %collective-permute-done = bf16[8,4224]{1,0:T(8,128)(2,1)S(1)} collective-permute-done((bf16[8,4224]{1,0:T(8,128)(2,1)S(1)}, bf16[8,4224]{1,0:T(8,128)(2,1)S(1)}, u32[]{:S(2)}, u32[]{:S(2)}) %collective-permute-start) | collective-permute-done | bytes 67616 | tf_op jit(solution)/shard_map/ppermute | solution.py:183
  9.5 1.3 %collective-permute-done.1 = bf16[8,4224]{1,0:T(8,128)(2,1)S(1)} collective-permute-done((bf16[8,4224]{1,0:T(8,128)(2,1)S(1)}, bf16[8,4224]{1,0:T(8,128)(2,1)S(1)}, u32[]{:S(2)}, u32[]{:S(2)}) %collective-permute-start.1) | collective-permute-done | bytes 67616 | tf_op jit(solution)/shard_map/ppermute | solution.py:183
  10.8 6.8 %collective-permute-start.2 = (bf16[2,8,4224]{2,1,0:T(8,128)(2,1)S(1)}, bf16[2,8,4224]{2,1,0:T(8,128)(2,1)S(1)}, u32[]{:S(2)}, u32[]{:S(2)}) collective-permute-start(bf16[2,8,4224]{2,1,0:T(8,128)(2,1)S(1)} %pad_maximum_fusion.1), channel_id=1, source_target_pairs={{0,48},{1,49},{2,50},{3,51},{4,52},{5,53},{6,54},{7,55},{8,88},{9,... | collective-permute-start | bytes 405512 | tf_op jit(solution)/shard_map/ppermute | solution.py:183
  17.6 0.8 %broadcast_in_dim.27 = bf16[8,8,4096]{2,1,0:T(8,128)(2,1)} broadcast(bf16[8,4096]{1,0:T(8,128)(2,1)S(1)} %bitcast.18), dimensions={1,2} | broadcast | bytes 589824 | tf_op jit(solution)/shard_map/broadcast_in_dim | solution.py:201
  18.4 8.4 %all-to-all-start = ((bf16[8,8,4096]{2,1,0:T(8,128)(2,1)}), bf16[8,8,4096]{2,1,0:T(8,128)(2,1)S(1)}, u32[]{:S(2)}, u32[]{:S(2)}) async-start(bf16[8,8,4096]{2,1,0:T(8,128)(2,1)} %broadcast_in_dim.27), calls=%async_computation | async-start | bytes 1048576 | tf_op jit(solution)/shard_map/all_to_all | solution.py:202
  26.8 2.0 %collective-permute-start.6 = (bf16[2,8,4224]{2,1,0:T(8,128)(2,1)S(1)}, bf16[2,8,4224]{2,1,0:T(8,128)(2,1)S(1)}, u32[]{:S(2)}, u32[]{:S(2)}) collective-permute-start(bf16[2,8,4224]{2,1,0:T(8,128)(2,1)S(1)} %pad_maximum_fusion.1), channel_id=1, source_target_pairs={{0,16},{1,17},{2,18},{3,19},{4,20},{5,21},{6,22},{7,23},{8,120},{9... | collective-permute-start | bytes 405512 | tf_op jit(solution)/shard_map/ppermute | solution.py:183
  28.8 1.9 %collective-permute-start.3 = (bf16[2,8,4224]{2,1,0:T(8,128)(2,1)S(1)}, bf16[2,8,4224]{2,1,0:T(8,128)(2,1)S(1)}, u32[]{:S(2)}, u32[]{:S(2)}) collective-permute-start(bf16[2,8,4224]{2,1,0:T(8,128)(2,1)S(1)} %pad_maximum_fusion.1), channel_id=1, source_target_pairs={{0,32},{1,33},{2,34},{3,35},{4,36},{5,37},{6,38},{7,39},{8,104},{9... | collective-permute-start | bytes 405512 | tf_op jit(solution)/shard_map/ppermute | solution.py:183
  30.7 1.8 %collective-permute-start.5 = (bf16[8,4224]{1,0:T(8,128)(2,1)S(1)}, bf16[8,4224]{1,0:T(8,128)(2,1)S(1)}, u32[]{:S(2)}, u32[]{:S(2)}) collective-permute-start(bf16[8,4224]{1,0:T(8,128)(2,1)S(1)} %slice_bitcast_fusion), channel_id=1, source_target_pairs={{0,16},{1,17},{2,18},{3,19},{4,20},{5,21},{6,22},{7,23},{8,120},{9... | collective-permute-start | bytes 202760 | tf_op jit(solution)/shard_map/ppermute | solution.py:183
  32.5 4.6 %collective-permute-done.3 = bf16[2,8,4224]{2,1,0:T(8,128)(2,1)S(1)} collective-permute-done((bf16[2,8,4224]{2,1,0:T(8,128)(2,1)S(1)}, bf16[2,8,4224]{2,1,0:T(8,128)(2,1)S(1)}, u32[]{:S(2)}, u32[]{:S(2)}) %collective-permute-start.3) | collective-permute-done | bytes 135200 | tf_op jit(solution)/shard_map/ppermute | solution.py:183
  37.2 0.7 collective-permute-done.5
  38.1 3.0 %collective-permute-start.4 = (bf16[4,8,4224]{2,1,0:T(8,128)(2,1)S(1)}, bf16[4,8,4224]{2,1,0:T(8,128)(2,1)}, u32[]{:S(2)}, u32[]{:S(2)}) collective-permute-start(bf16[4,8,4224]{2,1,0:T(8,128)(2,1)S(1)} %constant_dynamic-update-slice_fusion.refs_0_), channel_id=1, source_target_pairs={{0,128},{1,129},{2,130},{3,131},{4,132},{5,133},{6,134},{7,135},{8... | collective-permute-start | bytes 811016 | tf_op jit(solution)/shard_map/ppermute | solution.py:183
  41.1 0.6 collective-permute-start.7
  41.7 5.9 %solve.2.refs_7_ = f32[64,4096]{1,0:T(8,128)S(1)} custom-call(s32[1]{0:T(128)} %bitcast.seat_ref, bf16[64,4096]{1,0:T(8,128)(2,1)S(1)} %bitcast.13, bf16[4,8,4224]{2,1,0:T(8,128)(2,1)S(1)} %constant_dynamic-update-slice_fusion.refs_0_, bf16[4,8,4224]{2,1,0:T(8,128)(2,1)S(1)} %pad_maximum_fusion.refs_1_, bf16[4,8,4224]{2,1,0:T(8,128)(2,1)} %collective-permute-done.8.refs_2_, ...), custom_call_target="tpu_custom_call" | custom-call | flops 10000000000 | bytes 10000000 | tf_op jit(solution)/shard_map/solve/pallas_call | solution.py:153
  47.6 1.5 %collective-permute-done.4.refs_0_ = bf16[4,8,4224]{2,1,0:T(8,128)(2,1)} collective-permute-done((bf16[4,8,4224]{2,1,0:T(8,128)(2,1)S(1)}, bf16[4,8,4224]{2,1,0:T(8,128)(2,1)}, u32[]{:S(2)}, u32[]{:S(2)}) %collective-permute-start.4) | collective-permute-done | bytes 270368 | tf_op jit(solution)/shard_map/ppermute | solution.py:183
  49.1 5.2 %collective-permute-done.7.refs_1_ = bf16[4,8,4224]{2,1,0:T(8,128)(2,1)} collective-permute-done((bf16[4,8,4224]{2,1,0:T(8,128)(2,1)S(1)}, bf16[4,8,4224]{2,1,0:T(8,128)(2,1)}, u32[]{:S(2)}, u32[]{:S(2)}) %collective-permute-start.7) | collective-permute-done | bytes 270368 | tf_op jit(solution)/shard_map/ppermute | solution.py:183
  54.3 0.5 collective-permute-start.11
  54.9 1.2 %collective-permute-done.10.refs_2_ = bf16[4,8,4224]{2,1,0:T(8,128)(2,1)S(1)} collective-permute-done((bf16[4,8,4224]{2,1,0:T(8,128)(2,1)}, bf16[4,8,4224]{2,1,0:T(8,128)(2,1)S(1)}, u32[]{:S(2)}, u32[]{:S(2)}) %collective-permute-start.10) | collective-permute-done | bytes 270368 | tf_op jit(solution)/shard_map/ppermute | solution.py:183
  56.5 6.2 %solve.3 = f32[64,4224]{1,0:T(8,128)S(1)} custom-call(s32[1]{0:T(128)} %bitcast.seat_ref, bf16[64,4096]{1,0:T(8,128)(2,1)S(1)} %bitcast.14, bf16[4,8,4224]{2,1,0:T(8,128)(2,1)} %collective-permute-done.4.refs_0_, bf16[4,8,4224]{2,1,0:T(8,128)(2,1)} %collective-permute-done.7.refs_1_, bf16[4,8,4224]{2,1,0:T(8,128)(2,1)S(1)} %collective-permute-done.10.refs_2_, ...), custom_call_target="tpu_custom_call" | custom-call | flops 10000000000 | bytes 10000000 | tf_op jit(solution)/shard_map/solve/pallas_call | solution.py:153
  62.8 14.9 %all_to_all.10 = f16[8,8,4224]{2,1,0:T(8,128)(2,1)S(1)} all-to-all(f16[8,8,4224]{2,1,0:T(8,128)(2,1)S(1)} %convert_bitcast_fusion), channel_id=1, replica_groups=mesh['grp'=32,'dist'=8] {'dist'}, dimensions={0} | all-to-all | bytes 1081344 | tf_op jit(solution)/shard_map/all_to_all | solution.py:228
  77.8 0.8 %multiply_reduce_fusion = f32[8,4096]{1,0:T(8,128)} fusion(f16[8,8,4224]{2,1,0:T(8,128)(2,1)S(1)} %all_to_all.10, f32[8]{0:T(128)S(1)} %exponential_reduce_fusion), kind=kLoop, calls=%fused_computation.4 | loop fusion | flops 753664 | bytes 655392 | tf_op jit(solution)/shard_map/reduce_sum | solution.py:231
  (26 shorter events, 1.1 us)
Async XLA Ops:
  0.0 8.3 %copy-start.1 = (bf16[64,192]{1,0:T(8,128)(2,1)S(1)}, bf16[64,192]{1,0:T(8,128)(2,1)}, u32[]{:S(2)}) copy-start(bf16[64,192]{1,0:T(8,128)(2,1)} %constant.41) | copy-start | bytes 73732
  0.0 17.6 %copy-start = (bf16[1,8,4096]{2,1,0:T(8,128)(2,1)S(1)}, bf16[1,8,4096]{2,1,0:T(8,128)(2,1)}, u32[]{:S(2)}) copy-start(bf16[1,8,4096]{2,1,0:T(8,128)(2,1)} %param.4) | copy-start | bytes 196612
  1.5 8.0 %collective-permute-start = (bf16[8,4224]{1,0:T(8,128)(2,1)S(1)}, bf16[8,4224]{1,0:T(8,128)(2,1)S(1)}, u32[]{:S(2)}, u32[]{:S(2)}) collective-permute-start(bf16[8,4224]{1,0:T(8,128)(2,1)S(1)} %concatenate.49), channel_id=1, source_target_pairs={{0,0},{1,16},{2,32},{3,48},{4,64},{5,80},{6,96},{7,112},{8,8},{9,2... | collective-permute-start | bytes 202760 | tf_op jit(solution)/shard_map/ppermute | solution.py:183
  9.5 1.3 %collective-permute-start.1 = (bf16[8,4224]{1,0:T(8,128)(2,1)S(1)}, bf16[8,4224]{1,0:T(8,128)(2,1)S(1)}, u32[]{:S(2)}, u32[]{:S(2)}) collective-permute-start(bf16[8,4224]{1,0:T(8,128)(2,1)S(1)} %collective-permute-done), channel_id=1, source_target_pairs={{0,8},{1,9},{2,10},{3,11},{4,12},{5,13},{6,14},{7,15},{8,0},{9,1},... | collective-permute-start | bytes 202760 | tf_op jit(solution)/shard_map/ppermute | solution.py:183
  10.8 19.9 %collective-permute-start.2 = (bf16[2,8,4224]{2,1,0:T(8,128)(2,1)S(1)}, bf16[2,8,4224]{2,1,0:T(8,128)(2,1)S(1)}, u32[]{:S(2)}, u32[]{:S(2)}) collective-permute-start(bf16[2,8,4224]{2,1,0:T(8,128)(2,1)S(1)} %pad_maximum_fusion.1), channel_id=1, source_target_pairs={{0,48},{1,49},{2,50},{3,51},{4,52},{5,53},{6,54},{7,55},{8,88},{9,... | collective-permute-start | bytes 405512 | tf_op jit(solution)/shard_map/ppermute | solution.py:183
  18.4 23.2 %all-to-all-start = ((bf16[8,8,4096]{2,1,0:T(8,128)(2,1)}), bf16[8,8,4096]{2,1,0:T(8,128)(2,1)S(1)}, u32[]{:S(2)}, u32[]{:S(2)}) async-start(bf16[8,8,4096]{2,1,0:T(8,128)(2,1)} %broadcast_in_dim.27), calls=%async_computation | async-start | bytes 1048576 | tf_op jit(solution)/shard_map/all_to_all | solution.py:202
  26.8 10.4 %collective-permute-start.6 = (bf16[2,8,4224]{2,1,0:T(8,128)(2,1)S(1)}, bf16[2,8,4224]{2,1,0:T(8,128)(2,1)S(1)}, u32[]{:S(2)}, u32[]{:S(2)}) collective-permute-start(bf16[2,8,4224]{2,1,0:T(8,128)(2,1)S(1)} %pad_maximum_fusion.1), channel_id=1, source_target_pairs={{0,16},{1,17},{2,18},{3,19},{4,20},{5,21},{6,22},{7,23},{8,120},{9... | collective-permute-start | bytes 405512 | tf_op jit(solution)/shard_map/ppermute | solution.py:183
  28.8 8.3 %collective-permute-start.3 = (bf16[2,8,4224]{2,1,0:T(8,128)(2,1)S(1)}, bf16[2,8,4224]{2,1,0:T(8,128)(2,1)S(1)}, u32[]{:S(2)}, u32[]{:S(2)}) collective-permute-start(bf16[2,8,4224]{2,1,0:T(8,128)(2,1)S(1)} %pad_maximum_fusion.1), channel_id=1, source_target_pairs={{0,32},{1,33},{2,34},{3,35},{4,36},{5,37},{6,38},{7,39},{8,104},{9... | collective-permute-start | bytes 405512 | tf_op jit(solution)/shard_map/ppermute | solution.py:183
  30.7 7.2 %collective-permute-start.5 = (bf16[8,4224]{1,0:T(8,128)(2,1)S(1)}, bf16[8,4224]{1,0:T(8,128)(2,1)S(1)}, u32[]{:S(2)}, u32[]{:S(2)}) collective-permute-start(bf16[8,4224]{1,0:T(8,128)(2,1)S(1)} %slice_bitcast_fusion), channel_id=1, source_target_pairs={{0,16},{1,17},{2,18},{3,19},{4,20},{5,21},{6,22},{7,23},{8,120},{9... | collective-permute-start | bytes 202760 | tf_op jit(solution)/shard_map/ppermute | solution.py:183
  37.1 4.6 %collective-permute-start.8 = (bf16[4,8,4224]{2,1,0:T(8,128)(2,1)S(1)}, bf16[4,8,4224]{2,1,0:T(8,128)(2,1)}, u32[]{:S(2)}, u32[]{:S(2)}) collective-permute-start(bf16[4,8,4224]{2,1,0:T(8,128)(2,1)S(1)} %constant_dynamic-update-slice_fusion.refs_0_), channel_id=1, source_target_pairs={{0,8},{1,9},{2,10},{3,11},{4,12},{5,13},{6,14},{7,15},{8,0},{9,1},... | collective-permute-start | bytes 811016 | tf_op jit(solution)/shard_map/ppermute | solution.py:183
  38.0 3.7 %collective-permute-start.9 = (bf16[4,8,4224]{2,1,0:T(8,128)(2,1)S(1)}, bf16[4,8,4224]{2,1,0:T(8,128)(2,1)}, u32[]{:S(2)}, u32[]{:S(2)}) collective-permute-start(bf16[4,8,4224]{2,1,0:T(8,128)(2,1)S(1)} %pad_maximum_fusion.refs_1_), channel_id=1, source_target_pairs={{0,8},{1,9},{2,10},{3,11},{4,12},{5,13},{6,14},{7,15},{8,0},{9,1},... | collective-permute-start | bytes 811016 | tf_op jit(solution)/shard_map/ppermute | solution.py:183
  38.1 11.1 %collective-permute-start.4 = (bf16[4,8,4224]{2,1,0:T(8,128)(2,1)S(1)}, bf16[4,8,4224]{2,1,0:T(8,128)(2,1)}, u32[]{:S(2)}, u32[]{:S(2)}) collective-permute-start(bf16[4,8,4224]{2,1,0:T(8,128)(2,1)S(1)} %constant_dynamic-update-slice_fusion.refs_0_), channel_id=1, source_target_pairs={{0,128},{1,129},{2,130},{3,131},{4,132},{5,133},{6,134},{7,135},{8... | collective-permute-start | bytes 811016 | tf_op jit(solution)/shard_map/ppermute | solution.py:183
  41.1 13.3 %collective-permute-start.7 = (bf16[4,8,4224]{2,1,0:T(8,128)(2,1)S(1)}, bf16[4,8,4224]{2,1,0:T(8,128)(2,1)}, u32[]{:S(2)}, u32[]{:S(2)}) collective-permute-start(bf16[4,8,4224]{2,1,0:T(8,128)(2,1)S(1)} %pad_maximum_fusion.refs_1_), channel_id=1, source_target_pairs={{0,128},{1,129},{2,130},{3,131},{4,132},{5,133},{6,134},{7,135},{8... | collective-permute-start | bytes 811016 | tf_op jit(solution)/shard_map/ppermute | solution.py:183
  54.3 1.8 %collective-permute-start.10 = (bf16[4,8,4224]{2,1,0:T(8,128)(2,1)}, bf16[4,8,4224]{2,1,0:T(8,128)(2,1)S(1)}, u32[]{:S(2)}, u32[]{:S(2)}) collective-permute-start(bf16[4,8,4224]{2,1,0:T(8,128)(2,1)} %collective-permute-done.4.refs_0_), channel_id=1, source_target_pairs={{0,8},{1,9},{2,10},{3,11},{4,12},{5,13},{6,14},{7,15},{8,0},{9,1},... | collective-permute-start | bytes 811016 | tf_op jit(solution)/shard_map/ppermute | solution.py:183
  54.3 2.1 %collective-permute-start.11 = (bf16[4,8,4224]{2,1,0:T(8,128)(2,1)}, bf16[4,8,4224]{2,1,0:T(8,128)(2,1)S(1)}, u32[]{:S(2)}, u32[]{:S(2)}) collective-permute-start(bf16[4,8,4224]{2,1,0:T(8,128)(2,1)} %collective-permute-done.7.refs_1_), channel_id=1, source_target_pairs={{0,8},{1,9},{2,10},{3,11},{4,12},{5,13},{6,14},{7,15},{8,0},{9,1},... | collective-permute-start | bytes 811016 | tf_op jit(solution)/shard_map/ppermute | solution.py:183

commit v3 on v2

--- a/solution.py
+++ b/solution.py
@@ -36,12 +36,12 @@
     return left, right
 
 
-def green_table():
+def green_table(live):
     p = jnp.arange(GRID, dtype=jnp.int32)
     f = jnp.minimum(p, GRID - p)
     sq = (f * f).astype(jnp.float32)
     tot = sq[:, None, None] + sq[None, :, None] + jnp.concatenate([sq, sq])[None, None, :]
-    c = box_length**2 / (math.pi * GRID**3)
+    c = jnp.where(live, box_length**2 / (math.pi * GRID**3), 0.0)
     return jnp.where(tot > 0.5, c / jnp.maximum(tot, 1.0), 0.0)
 
 
@@ -75,17 +75,18 @@
             hops = jnp.where(away > 4, 8 - away, away)
             single = jnp.logical_or(away == 0, away == 4)
             holder = jnp.where(single, member, jnp.where(away > 4, 0, 1))
-            paired = jnp.where(hops == 1, 6, 6 - 2 * hops) + jnp.bitwise_xor(holder, member)
-            index = jnp.where(single, 4 + jnp.right_shift(away, 2), paired)
+            early = jnp.logical_or(away == 0, hops == 1)
+            paired = jnp.where(hops == 2, 3, 1) + jnp.bitwise_xor(holder, member)
+            index = jnp.where(single, 0, paired)
             rows = slice(8 * block, 8 * block + 8)
             for other in range(2):
                 for half in range(2):
                     here = jnp.bitwise_xor(holder, core) == other
-                    here = jnp.logical_and(here, jnp.right_shift(index, 2) == half)
+                    here = jnp.logical_and(here, early == (half == 0))
 
                     @pl.when(here)
                     def _():
-                        piece = sources[other][half][jnp.bitwise_and(index, 3)]
+                        piece = sources[other][half][index]
                         col_ref[member, rows, :] = piece.astype(jnp.float32)
 
     left = left_ref[...]
@@ -201,28 +202,31 @@
     copies = jnp.broadcast_to(mine, (8, *mine.shape))
     row = lax.all_to_all(copies, "dist", split_axis=0, concat_axis=0, tiled=True)
     row = row.reshape(GRID, GRID * GRID)
+    crossed = moved(kept, cores)
     seat = lax.axis_index("grp").astype(jnp.int32).reshape(1)
-    left, right = (jnp.where(seat[0] >= 0, t, 0) for t in tables())
-    left, right, green, kept = lax.optimization_barrier((left, right, green_table(), kept))
-    crossed = moved(kept, cores)
-    pair = jnp.stack([kept, crossed])
+    pair, seat = lax.optimization_barrier((jnp.stack([kept, crossed]), seat))
+    live = seat[0] >= 0
+    left, right = tables()
+    left = jnp.where(live, left, 0)
+    right = jnp.where(live, right, 0)
+    green = green_table(live)
     shifted = {}
-    for k in (3, 2, 1):
+    for k in (1, 3, 2):
         shifted[k] = moved(pair, ring(k))
-    fourth = moved(shifted[3][0], ring(1))
+    third, left, right, green = lax.optimization_barrier((shifted[3], left, right, green))
+    fourth = moved(third[0], ring(1))
     halves = [
-        jnp.concatenate([shifted[3], shifted[2]]),
-        jnp.concatenate([kept[None], fourth[None], shifted[1]]),
+        jnp.concatenate([kept[None], shifted[1]]),
+        jnp.concatenate([fourth[None], third, shifted[2]]),
     ]
     far, core = [], []
     for half in halves:
         far.append(moved(half, lambda h, z, c, l: (1 - h, z, c, l)))
         core.append(moved(half, cores))
+    far_core = [moved(far[0], cores)]
     partial = solve(seat, row, halves, core, left, right, green)
-    far, partial = lax.optimization_barrier((far, partial))
-    far_core = []
-    for half in far:
-        far_core.append(moved(half, cores))
+    far[1], partial = lax.optimization_barrier((far[1], partial))
+    far_core.append(moved(far[1], cores))
     partial = solve(seat, row, far, far_core, left, right, green, partial)
     sent = partial.astype(jnp.float16).reshape(8, 8, GRID * GRID + 128)
     arrived = lax.all_to_all(sent, "dist", split_axis=0, concat_axis=0, tiled=True)

time: 79.9 us -> 85.6 us (1.071)
  waiting for transfers between devices: 16.1 us -> 24.3 us
  starting transfers between devices: 30.2 us -> 26.9 us
  other arithmetic: 2.8 us -> 3.76 us
    ppermute x12, waiting for transfers between devices: 16.1 us -> 24.3 us  [moved(): return lax.ppermute(x, AXES, pairs)]
    all_to_all x1, starting transfers between devices: 8.38 us -> 4.4 us  [exchange(): lax.all_to_all(copies, 'dist', split_axis=0, concat_axis=0, tiled=True)]
    concatenate x1 -> x2, other arithmetic: 0.04 us -> 1.01 us  [the longest x1 0.99 us: exchange(): jnp.concatenate([fourth[None], third, shifted[2]])]
  transfers between devices with their start and end apart: 13 -> 13, of which waited for: 8 -> 6; matrix products, arithmetic and copies ran while one was open for 3% -> 4% of each run, Pallas kernels for 8% -> 7%
where the time goes in v3:
time: 85.6 us; the launch traced here: 84.6 us
  starting transfers between devices  26.9 us (31%)
  waiting for transfers between devices  24.3 us (28%)
  blocking collectives  14.8 us (17%)
  Pallas kernels  12.3 us (14%)
  other arithmetic  3.76 us (4%)
  local copies, waits for them, and re-layouts  1.69 us (2%)
    ppermute x12, waiting for transfers between devices, moved(): return lax.ppermute(x, AXES, pairs)  24.3 us
    ppermute x12, starting transfers between devices, moved(): return lax.ppermute(x, AXES, pairs)  22.5 us
    all_to_all x1, blocking collectives, exchange(): lax.all_to_all(sent, 'dist', split_axis=0, concat_axis=0, tiled=True)  14.8 us
    pallas_call x2, Pallas kernels, solve(): pl.pallas_call(functools.partial(solve_kernel, not more), out_shape=jax.S...  12.3 us
    all_to_all x1, starting transfers between devices, exchange(): lax.all_to_all(copies, 'dist', split_axis=0, concat_axis=0, tiled=True)  4.4 us
  transfers between devices with their start and end apart: 13, of which 6 were waited for; matrix products, arithmetic and copies ran while one was open for 4% of the time, Pallas kernels for 7%

profile of v3, /device:TPU:8, one launch (start us, length us, event | category | flops | bytes accessed | tf_op | source)
XLA Modules:
  0.0 84.6 jit_solution(1410991688117910312)
XLA Ops:
  0.7 0.8 %concatenate.39 = bf16[8,4224]{1,0:T(8,128)(2,1)S(1)} pad(bf16[8,4096]{1,0:T(8,128)(2,1)} %bitcast.18, bf16[]{:T(256)} %bitcast.13), padding=0_0x0_128 | pad | bytes 133122 | tf_op jit(solution)/shard_map/concatenate | solution.py:200
  1.5 5.1 %collective-permute-start = (bf16[8,4224]{1,0:T(8,128)(2,1)S(1)}, bf16[8,4224]{1,0:T(8,128)(2,1)S(1)}, u32[]{:S(2)}, u32[]{:S(2)}) collective-permute-start(bf16[8,4224]{1,0:T(8,128)(2,1)S(1)} %concatenate.39), channel_id=1, source_target_pairs={{0,0},{1,16},{2,32},{3,48},{4,64},{5,80},{6,96},{7,112},{8,8},{9,2... | collective-permute-start | bytes 202760 | tf_op jit(solution)/shard_map/ppermute | solution.py:184
  6.7 2.8 %collective-permute-done = bf16[8,4224]{1,0:T(8,128)(2,1)S(1)} collective-permute-done((bf16[8,4224]{1,0:T(8,128)(2,1)S(1)}, bf16[8,4224]{1,0:T(8,128)(2,1)S(1)}, u32[]{:S(2)}, u32[]{:S(2)}) %collective-permute-start) | collective-permute-done | bytes 67616 | tf_op jit(solution)/shard_map/ppermute | solution.py:184
  9.6 1.2 %collective-permute-done.1 = bf16[8,4224]{1,0:T(8,128)(2,1)S(1)} collective-permute-done((bf16[8,4224]{1,0:T(8,128)(2,1)S(1)}, bf16[8,4224]{1,0:T(8,128)(2,1)S(1)}, u32[]{:S(2)}, u32[]{:S(2)}) %collective-permute-start.1) | collective-permute-done | bytes 67616 | tf_op jit(solution)/shard_map/ppermute | solution.py:184
  10.9 11.7 %collective-permute-start.4 = (bf16[2,8,4224]{2,1,0:T(8,128)(2,1)S(1)}, bf16[2,8,4224]{2,1,0:T(8,128)(2,1)S(1)}, u32[]{:S(2)}, u32[]{:S(2)}) collective-permute-start(bf16[2,8,4224]{2,1,0:T(8,128)(2,1)S(1)} %pad_maximum_fusion.2), channel_id=1, source_target_pairs={{0,48},{1,49},{2,50},{3,51},{4,52},{5,53},{6,54},{7,55},{8,88},{9,... | collective-permute-start | bytes 405512 | tf_op jit(solution)/shard_map/ppermute | solution.py:184
  22.6 0.9 %broadcast_select_fusion.refs_5_ = bf16[256,256]{1,0:T(8,128)(2,1)S(1)} fusion(bf16[256,256]{1,0:T(8,128)(2,1)} %constant.50, pred[]{:T(512)} %bitcast.6), kind=kLoop, calls=%fused_computation.9 | loop fusion | flops 65536 | bytes 262145 | tf_op jit(solution)/shard_map/jit(_where)/select_n | solution.py:211
  23.5 0.6 fusion.1.refs_6_
  24.2 8.2 %collective-permute-done.4 = bf16[2,8,4224]{2,1,0:T(8,128)(2,1)S(1)} collective-permute-done((bf16[2,8,4224]{2,1,0:T(8,128)(2,1)S(1)}, bf16[2,8,4224]{2,1,0:T(8,128)(2,1)S(1)}, u32[]{:S(2)}, u32[]{:S(2)}) %collective-permute-start.4) | collective-permute-done | bytes 135200 | tf_op jit(solution)/shard_map/ppermute | solution.py:184
  32.4 0.8 broadcast_in_dim.27
  33.2 4.4 %all-to-all-start = ((bf16[8,8,4096]{2,1,0:T(8,128)(2,1)}), bf16[8,8,4096]{2,1,0:T(8,128)(2,1)S(1)}, u32[]{:S(2)}, u32[]{:S(2)}) async-start(bf16[8,8,4096]{2,1,0:T(8,128)(2,1)} %broadcast_in_dim.27), calls=%async_computation | async-start | bytes 1048576 | tf_op jit(solution)/shard_map/all_to_all | solution.py:203
  37.6 1.2 %collective-permute-start.2 = (bf16[2,8,4224]{2,1,0:T(8,128)(2,1)S(1)}, bf16[2,8,4224]{2,1,0:T(8,128)(2,1)S(1)}, u32[]{:S(2)}, u32[]{:S(2)}) collective-permute-start(bf16[2,8,4224]{2,1,0:T(8,128)(2,1)S(1)} %pad_maximum_fusion.2), channel_id=1, source_target_pairs={{0,16},{1,17},{2,18},{3,19},{4,20},{5,21},{6,22},{7,23},{8,120},{9... | collective-permute-start | bytes 405512 | tf_op jit(solution)/shard_map/ppermute | solution.py:184
  38.9 1.0 %pad_maximum_fusion.refs_1_ = bf16[5,8,4224]{2,1,0:T(8,128)(2,1)S(1)} fusion(bf16[2,8,4224]{2,1,0:T(8,128)(2,1)} %collective-permute-done.6, bf16[2,8,4224]{2,1,0:T(8,128)(2,1)S(1)} %collective-permute-done.4, bf16[1,8,4224]{2,1,0:T(8,128)(2,1)} %bitcast.8), kind=kLoop, calls=%fused_computation.6 | loop fusion | flops 337920 | bytes 675840 | tf_op jit(solution)/shard_map/concatenate | solution.py:220
  39.9 0.2 collective-permute-start.9
  40.1 3.8 %collective-permute-done.2 = bf16[2,8,4224]{2,1,0:T(8,128)(2,1)S(1)} collective-permute-done((bf16[2,8,4224]{2,1,0:T(8,128)(2,1)S(1)}, bf16[2,8,4224]{2,1,0:T(8,128)(2,1)S(1)}, u32[]{:S(2)}, u32[]{:S(2)}) %collective-permute-start.2) | collective-permute-done | bytes 135200 | tf_op jit(solution)/shard_map/ppermute | solution.py:184
  44.0 2.7 %collective-permute-start.3 = (bf16[3,8,4224]{2,1,0:T(8,128)(2,1)S(1)}, bf16[3,8,4224]{2,1,0:T(8,128)(2,1)S(1)}, u32[]{:S(2)}, u32[]{:S(2)}) collective-permute-start(bf16[3,8,4224]{2,1,0:T(8,128)(2,1)S(1)} %pad_maximum_fusion.1.refs_0_), channel_id=1, source_target_pairs={{0,128},{1,129},{2,130},{3,131},{4,132},{5,133},{6,134},{7,135},{8... | collective-permute-start | bytes 608264 | tf_op jit(solution)/shard_map/ppermute | solution.py:184
  46.7 0.9 %collective-permute-start.7 = (bf16[5,8,4224]{2,1,0:T(8,128)(2,1)S(1)}, bf16[5,8,4224]{2,1,0:T(8,128)(2,1)}, u32[]{:S(2)}, u32[]{:S(2)}) collective-permute-start(bf16[5,8,4224]{2,1,0:T(8,128)(2,1)S(1)} %pad_maximum_fusion.refs_1_), channel_id=1, source_target_pairs={{0,128},{1,129},{2,130},{3,131},{4,132},{5,133},{6,134},{7,135},{8... | collective-permute-start | bytes 1013768 | tf_op jit(solution)/shard_map/ppermute | solution.py:184
  47.6 6.0 %solve.2.refs_7_ = f32[64,4096]{1,0:T(8,128)S(1)} custom-call(s32[1]{0:T(128)} %bitcast.4.seat_ref, bf16[64,4096]{1,0:T(8,128)(2,1)S(1)} %bitcast.14, bf16[3,8,4224]{2,1,0:T(8,128)(2,1)S(1)} %pad_maximum_fusion.1.refs_0_, bf16[5,8,4224]{2,1,0:T(8,128)(2,1)S(1)} %pad_maximum_fusion.refs_1_, bf16[3,8,4224]{2,1,0:T(8,128)(2,1)} %collective-permute-done.8.refs_2_, ...), custom_call_target="tpu_custom_call" | custom-call | flops 10000000000 | bytes 10000000 | tf_op jit(solution)/shard_map/solve/pallas_call | solution.py:154
  53.6 6.6 %collective-permute-done.7.refs_1_ = bf16[5,8,4224]{2,1,0:T(8,128)(2,1)} collective-permute-done((bf16[5,8,4224]{2,1,0:T(8,128)(2,1)S(1)}, bf16[5,8,4224]{2,1,0:T(8,128)(2,1)}, u32[]{:S(2)}, u32[]{:S(2)}) %collective-permute-start.7) | collective-permute-done | bytes 337952 | tf_op jit(solution)/shard_map/ppermute | solution.py:184
  60.3 0.5 collective-permute-start.10
  60.8 1.6 %collective-permute-done.10.refs_2_ = bf16[3,8,4224]{2,1,0:T(8,128)(2,1)S(1)} collective-permute-done((bf16[3,8,4224]{2,1,0:T(8,128)(2,1)S(1)}, bf16[3,8,4224]{2,1,0:T(8,128)(2,1)S(1)}, u32[]{:S(2)}, u32[]{:S(2)}) %collective-permute-start.10) | collective-permute-done | bytes 202784 | tf_op jit(solution)/shard_map/ppermute | solution.py:184
  62.4 6.3 %solve.3 = f32[64,4224]{1,0:T(8,128)S(1)} custom-call(s32[1]{0:T(128)} %bitcast.4.seat_ref, bf16[64,4096]{1,0:T(8,128)(2,1)S(1)} %bitcast.15, bf16[3,8,4224]{2,1,0:T(8,128)(2,1)S(1)} %collective-permute-done.3.refs_0_, bf16[5,8,4224]{2,1,0:T(8,128)(2,1)} %collective-permute-done.7.refs_1_, bf16[3,8,4224]{2,1,0:T(8,128)(2,1)S(1)} %collective-permute-done.10.refs_2_, ...), custom_call_target="tpu_custom_call" | custom-call | flops 10000000000 | bytes 10000000 | tf_op jit(solution)/shard_map/solve/pallas_call | solution.py:154
  68.8 14.8 %all_to_all.10 = f16[8,8,4224]{2,1,0:T(8,128)(2,1)S(1)} all-to-all(f16[8,8,4224]{2,1,0:T(8,128)(2,1)S(1)} %convert_bitcast_fusion), channel_id=1, replica_groups=mesh['grp'=32,'dist'=8] {'dist'}, dimensions={0} | all-to-all | bytes 1081344 | tf_op jit(solution)/shard_map/all_to_all | solution.py:232
  83.6 0.2 exponential_reduce_fusion
  83.8 0.8 multiply_reduce_fusion
  (25 shorter events, 0.5 us)
Async XLA Ops:
  0.0 24.2 %copy-start.1 = (bf16[64,192]{1,0:T(8,128)(2,1)S(1)}, bf16[64,192]{1,0:T(8,128)(2,1)}, u32[]{:S(2)}) copy-start(bf16[64,192]{1,0:T(8,128)(2,1)} %constant.42) | copy-start | bytes 73732
  0.0 32.4 %copy-start = (bf16[1,8,4096]{2,1,0:T(8,128)(2,1)S(1)}, bf16[1,8,4096]{2,1,0:T(8,128)(2,1)}, u32[]{:S(2)}) copy-start(bf16[1,8,4096]{2,1,0:T(8,128)(2,1)} %param.4) | copy-start | bytes 196612
  1.5 8.0 %collective-permute-start = (bf16[8,4224]{1,0:T(8,128)(2,1)S(1)}, bf16[8,4224]{1,0:T(8,128)(2,1)S(1)}, u32[]{:S(2)}, u32[]{:S(2)}) collective-permute-start(bf16[8,4224]{1,0:T(8,128)(2,1)S(1)} %concatenate.39), channel_id=1, source_target_pairs={{0,0},{1,16},{2,32},{3,48},{4,64},{5,80},{6,96},{7,112},{8,8},{9,2... | collective-permute-start | bytes 202760 | tf_op jit(solution)/shard_map/ppermute | solution.py:184
  9.5 1.3 %collective-permute-start.1 = (bf16[8,4224]{1,0:T(8,128)(2,1)S(1)}, bf16[8,4224]{1,0:T(8,128)(2,1)S(1)}, u32[]{:S(2)}, u32[]{:S(2)}) collective-permute-start(bf16[8,4224]{1,0:T(8,128)(2,1)S(1)} %collective-permute-done), channel_id=1, source_target_pairs={{0,8},{1,9},{2,10},{3,11},{4,12},{5,13},{6,14},{7,15},{8,0},{9,1},... | collective-permute-start | bytes 202760 | tf_op jit(solution)/shard_map/ppermute | solution.py:184
  10.8 28.1 %collective-permute-start.6 = (bf16[2,8,4224]{2,1,0:T(8,128)(2,1)S(1)}, bf16[2,8,4224]{2,1,0:T(8,128)(2,1)}, u32[]{:S(2)}, u32[]{:S(2)}) collective-permute-start(bf16[2,8,4224]{2,1,0:T(8,128)(2,1)S(1)} %pad_maximum_fusion.2), channel_id=1, source_target_pairs={{0,32},{1,33},{2,34},{3,35},{4,36},{5,37},{6,38},{7,39},{8,104},{9... | collective-permute-start | bytes 405512 | tf_op jit(solution)/shard_map/ppermute | solution.py:184
  10.9 21.5 %collective-permute-start.4 = (bf16[2,8,4224]{2,1,0:T(8,128)(2,1)S(1)}, bf16[2,8,4224]{2,1,0:T(8,128)(2,1)S(1)}, u32[]{:S(2)}, u32[]{:S(2)}) collective-permute-start(bf16[2,8,4224]{2,1,0:T(8,128)(2,1)S(1)} %pad_maximum_fusion.2), channel_id=1, source_target_pairs={{0,48},{1,49},{2,50},{3,51},{4,52},{5,53},{6,54},{7,55},{8,88},{9,... | collective-permute-start | bytes 405512 | tf_op jit(solution)/shard_map/ppermute | solution.py:184
  32.4 6.5 %collective-permute-start.5 = (bf16[8,4224]{1,0:T(8,128)(2,1)S(1)}, bf16[8,4224]{1,0:T(8,128)(2,1)}, u32[]{:S(2)}, u32[]{:S(2)}) collective-permute-start(bf16[8,4224]{1,0:T(8,128)(2,1)S(1)} %slice_bitcast_fusion), channel_id=1, source_target_pairs={{0,16},{1,17},{2,18},{3,19},{4,20},{5,21},{6,22},{7,23},{8,120},{9... | collective-permute-start | bytes 202760 | tf_op jit(solution)/shard_map/ppermute | solution.py:184
  33.2 14.4 %all-to-all-start = ((bf16[8,8,4096]{2,1,0:T(8,128)(2,1)}), bf16[8,8,4096]{2,1,0:T(8,128)(2,1)S(1)}, u32[]{:S(2)}, u32[]{:S(2)}) async-start(bf16[8,8,4096]{2,1,0:T(8,128)(2,1)} %broadcast_in_dim.27), calls=%async_computation | async-start | bytes 1048576 | tf_op jit(solution)/shard_map/all_to_all | solution.py:203
  37.6 6.2 %collective-permute-start.2 = (bf16[2,8,4224]{2,1,0:T(8,128)(2,1)S(1)}, bf16[2,8,4224]{2,1,0:T(8,128)(2,1)S(1)}, u32[]{:S(2)}, u32[]{:S(2)}) collective-permute-start(bf16[2,8,4224]{2,1,0:T(8,128)(2,1)S(1)} %pad_maximum_fusion.2), channel_id=1, source_target_pairs={{0,16},{1,17},{2,18},{3,19},{4,20},{5,21},{6,22},{7,23},{8,120},{9... | collective-permute-start | bytes 405512 | tf_op jit(solution)/shard_map/ppermute | solution.py:184
  39.9 7.7 %collective-permute-start.9 = (bf16[5,8,4224]{2,1,0:T(8,128)(2,1)S(1)}, bf16[5,8,4224]{2,1,0:T(8,128)(2,1)}, u32[]{:S(2)}, u32[]{:S(2)}) collective-permute-start(bf16[5,8,4224]{2,1,0:T(8,128)(2,1)S(1)} %pad_maximum_fusion.refs_1_), channel_id=1, source_target_pairs={{0,8},{1,9},{2,10},{3,11},{4,12},{5,13},{6,14},{7,15},{8,0},{9,1},... | collective-permute-start | bytes 1013768 | tf_op jit(solution)/shard_map/ppermute | solution.py:184
  43.9 3.7 %collective-permute-start.8 = (bf16[3,8,4224]{2,1,0:T(8,128)(2,1)S(1)}, bf16[3,8,4224]{2,1,0:T(8,128)(2,1)}, u32[]{:S(2)}, u32[]{:S(2)}) collective-permute-start(bf16[3,8,4224]{2,1,0:T(8,128)(2,1)S(1)} %pad_maximum_fusion.1.refs_0_), channel_id=1, source_target_pairs={{0,8},{1,9},{2,10},{3,11},{4,12},{5,13},{6,14},{7,15},{8,0},{9,1},... | collective-permute-start | bytes 608264 | tf_op jit(solution)/shard_map/ppermute | solution.py:184
  44.0 16.3 %collective-permute-start.3 = (bf16[3,8,4224]{2,1,0:T(8,128)(2,1)S(1)}, bf16[3,8,4224]{2,1,0:T(8,128)(2,1)S(1)}, u32[]{:S(2)}, u32[]{:S(2)}) collective-permute-start(bf16[3,8,4224]{2,1,0:T(8,128)(2,1)S(1)} %pad_maximum_fusion.1.refs_0_), channel_id=1, source_target_pairs={{0,128},{1,129},{2,130},{3,131},{4,132},{5,133},{6,134},{7,135},{8... | collective-permute-start | bytes 608264 | tf_op jit(solution)/shard_map/ppermute | solution.py:184
  46.7 13.6 %collective-permute-start.7 = (bf16[5,8,4224]{2,1,0:T(8,128)(2,1)S(1)}, bf16[5,8,4224]{2,1,0:T(8,128)(2,1)}, u32[]{:S(2)}, u32[]{:S(2)}) collective-permute-start(bf16[5,8,4224]{2,1,0:T(8,128)(2,1)S(1)} %pad_maximum_fusion.refs_1_), channel_id=1, source_target_pairs={{0,128},{1,129},{2,130},{3,131},{4,132},{5,133},{6,134},{7,135},{8... | collective-permute-start | bytes 1013768 | tf_op jit(solution)/shard_map/ppermute | solution.py:184
  60.3 2.1 %collective-permute-start.11 = (bf16[5,8,4224]{2,1,0:T(8,128)(2,1)}, bf16[5,8,4224]{2,1,0:T(8,128)(2,1)S(1)}, u32[]{:S(2)}, u32[]{:S(2)}) collective-permute-start(bf16[5,8,4224]{2,1,0:T(8,128)(2,1)} %collective-permute-done.7.refs_1_), channel_id=1, source_target_pairs={{0,8},{1,9},{2,10},{3,11},{4,12},{5,13},{6,14},{7,15},{8,0},{9,1},... | collective-permute-start | bytes 1013768 | tf_op jit(solution)/shard_map/ppermute | solution.py:184
  60.3 2.1 %collective-permute-start.10 = (bf16[3,8,4224]{2,1,0:T(8,128)(2,1)S(1)}, bf16[3,8,4224]{2,1,0:T(8,128)(2,1)S(1)}, u32[]{:S(2)}, u32[]{:S(2)}) collective-permute-start(bf16[3,8,4224]{2,1,0:T(8,128)(2,1)S(1)} %collective-permute-done.3.refs_0_), channel_id=1, source_target_pairs={{0,8},{1,9},{2,10},{3,11},{4,12},{5,13},{6,14},{7,15},{8,0},{9,1},... | collective-permute-start | bytes 608264 | tf_op jit(solution)/shard_map/ppermute | solution.py:184

commit v4 on v3

--- a/solution.py
+++ b/solution.py
@@ -61,33 +61,25 @@
 
 
 def solve_kernel(first, seat_ref, row_ref, *refs):
-    sources = ((refs[0], refs[1]), (refs[2], refs[3]))
-    left_ref, right_ref, green_ref = refs[4:7]
+    pair_ref, near_refs, fourth_ref, other_refs = refs[0], refs[1:4], refs[4], refs[5:8]
+    left_ref, right_ref, green_ref = refs[8:11]
     col_ref, f_ref = refs[-2:]
     out_ref = refs[-3]
     group = seat_ref[0]
     core = jnp.bitwise_and(group, 1)
     z = jnp.bitwise_and(jnp.right_shift(group, 1), 7)
 
-    for member in range(2):
-        for block in range(8):
-            away = jnp.bitwise_and(block - z + 8, 7)
-            hops = jnp.where(away > 4, 8 - away, away)
-            single = jnp.logical_or(away == 0, away == 4)
-            holder = jnp.where(single, member, jnp.where(away > 4, 0, 1))
-            early = jnp.logical_or(away == 0, hops == 1)
-            paired = jnp.where(hops == 2, 3, 1) + jnp.bitwise_xor(holder, member)
-            index = jnp.where(single, 0, paired)
-            rows = slice(8 * block, 8 * block + 8)
-            for other in range(2):
-                for half in range(2):
-                    here = jnp.bitwise_xor(holder, core) == other
-                    here = jnp.logical_and(here, early == (half == 0))
-
-                    @pl.when(here)
-                    def _():
-                        piece = sources[other][half][index]
-                        col_ref[member, rows, :] = piece.astype(jnp.float32)
+    def place(ref, holder, block):
+        rows = pl.ds(pl.multiple_of(8 * jnp.bitwise_and(block + 8, 7), 8), 8)
+        for i in range(2):
+            col_ref[jnp.bitwise_xor(i, holder), rows, :] = ref[i].astype(jnp.float32)
+
+    place(pair_ref, core, z)
+    place(fourth_ref, core, z + 4)
+    for k in (1, 2, 3):
+        step = jnp.where(core == 0, -k, k)
+        place(near_refs[k - 1], core, z + step)
+        place(other_refs[k - 1], 1 - core, z - step)
 
     left = left_ref[...]
     right = right_ref[...]
@@ -131,7 +123,7 @@
         v2 = jnp.where(low, pltpu.roll(p0, 64, 1), p1)
         term = v1 * (col_ref[0, :, lanes] * occ[0]) + v2 * (col_ref[1, :, lanes] * occ[1])
         if not first:
-            term = refs[7][:, lanes] + term
+            term = refs[11][:, lanes] + term
         out_ref[:, lanes] = term
 
     if not first:
@@ -154,14 +146,14 @@
     return pl.pallas_call(
         functools.partial(solve_kernel, not more),
         out_shape=jax.ShapeDtypeStruct((GRID, width), jnp.float32),
-        in_specs=[sm] + [vm] * (8 + len(more)),
+        in_specs=[sm] + [vm] * (12 + len(more)),
         out_specs=vm,
         scratch_shapes=[
             pltpu.VMEM((2, GRID, GRID * GRID + 128), jnp.float32),
             pltpu.VMEM((GRID * PITCH, 128), jnp.float32),
         ],
         cost_estimate=pl.CostEstimate(flops=10**10, bytes_accessed=10**7, transcendentals=0),
-        compiler_params=pltpu.CompilerParams(vmem_limit_bytes=40 * 2**20),
+        compiler_params=pltpu.CompilerParams(vmem_limit_bytes=32 * 2**20),
         name="solve",
     )(seat, row, *mine, *other, left, right, green, *more)
 
@@ -190,6 +182,10 @@
 
 def cores(h, z, c, l):
     return (h, z, 1 - c, l)
+
+
+def halves(h, z, c, l):
+    return (1 - h, z, c, l)
 
 
 def ring(k):
@@ -210,23 +206,21 @@
     left = jnp.where(live, left, 0)
     right = jnp.where(live, right, 0)
     green = green_table(live)
-    shifted = {}
-    for k in (1, 3, 2):
-        shifted[k] = moved(pair, ring(k))
-    third, left, right, green = lax.optimization_barrier((shifted[3], left, right, green))
-    fourth = moved(third[0], ring(1))
-    halves = [
-        jnp.concatenate([kept[None], shifted[1]]),
-        jnp.concatenate([fourth[None], third, shifted[2]]),
-    ]
-    far, core = [], []
-    for half in halves:
-        far.append(moved(half, lambda h, z, c, l: (1 - h, z, c, l)))
-        core.append(moved(half, cores))
-    far_core = [moved(far[0], cores)]
-    partial = solve(seat, row, halves, core, left, right, green)
-    far[1], partial = lax.optimization_barrier((far[1], partial))
-    far_core.append(moved(far[1], cores))
+    chain, far, core = [pair], [], [None]
+    for k in range(5):
+        if k == 2:
+            chain[k], left, right, green = lax.optimization_barrier((chain[k], left, right, green))
+        if k < 4:
+            chain.append(moved(chain[k], ring(1)))
+        if k in (1, 2, 3):
+            core.append(moved(chain[k], cores))
+        far.append(moved(chain[k], halves))
+    far_core = []
+    for k in (1, 2):
+        far_core.append(moved(far[k], cores))
+    partial = solve(seat, row, chain, core[1:], left, right, green)
+    far[3], partial = lax.optimization_barrier((far[3], partial))
+    far_core.append(moved(far[3], cores))
     partial = solve(seat, row, far, far_core, left, right, green, partial)
     sent = partial.astype(jnp.float16).reshape(8, 8, GRID * GRID + 128)
     arrived = lax.all_to_all(sent, "dist", split_axis=0, concat_axis=0, tiled=True)

time: 85.6 us -> 83 us (0.970)
  local copies, waits for them, and re-layouts: 1.69 us -> 7.26 us
  waiting for transfers between devices: 24.3 us -> 19.7 us
  other arithmetic: 3.76 us -> 1.85 us
  blocking collectives: 14.8 us -> 13.3 us
  starting transfers between devices: 26.9 us -> 28 us
  Pallas kernels: 12.3 us -> 11.4 us
    all_to_all x1, starting transfers between devices: 4.4 us -> 9.17 us  [exchange(): lax.all_to_all(copies, 'dist', split_axis=0, concat_axis=0, tiled=True)]
    unnamed x4 -> x16, local copies, waits for them, and re-layouts: 0.01 us -> 4.7 us
    ppermute x12 -> x17, waiting for transfers between devices: 24.3 us -> 19.7 us  [moved(): return lax.ppermute(x, AXES, pairs)]
    ppermute x12 -> x17, starting transfers between devices: 22.5 us -> 18.8 us  [moved(): return lax.ppermute(x, AXES, pairs)]
    all_to_all x1, blocking collectives: 14.8 us -> 13.3 us  [exchange(): lax.all_to_all(sent, 'dist', split_axis=0, concat_axis=0, tiled=True)]
    concatenate x2 -> x0, other arithmetic: 1.01 us -> none  [the longest x1 0.99 us: exchange(): jnp.concatenate([fourth[None], third, shifted[2]])]
    select_n x1, other arithmetic: 0.92 us -> 0.02 us  [exchange(): right = jnp.where(live, right, 0)]
    pallas_call x2, Pallas kernels: 12.3 us -> 11.4 us  [solve(): pl.pallas_call(functools.partial(solve_kernel, not more), out_shape=jax.S...]
  transfers between devices with their start and end apart: 13 -> 18, of which waited for: 6 -> 6; matrix products, arithmetic and copies ran while one was open for 4% -> 3% of each run, Pallas kernels for 7% -> 7%
where the time goes in v4:
time: 83 us; the launch traced here: 82.4 us
  starting transfers between devices  28 us (34%)
  waiting for transfers between devices  19.7 us (24%)
  blocking collectives  13.3 us (16%)
  Pallas kernels  11.4 us (14%)
  local copies, waits for them, and re-layouts  7.26 us (9%)
  other arithmetic  1.85 us (2%)
    ppermute x17, waiting for transfers between devices, moved(): return lax.ppermute(x, AXES, pairs)  19.7 us
    ppermute x17, starting transfers between devices, moved(): return lax.ppermute(x, AXES, pairs)  18.8 us
    all_to_all x1, blocking collectives, exchange(): lax.all_to_all(sent, 'dist', split_axis=0, concat_axis=0, tiled=True)  13.3 us
    pallas_call x2, Pallas kernels, solve(): pl.pallas_call(functools.partial(solve_kernel, not more), out_shape=jax.S...  11.4 us
    all_to_all x1, starting transfers between devices, exchange(): lax.all_to_all(copies, 'dist', split_axis=0, concat_axis=0, tiled=True)  9.17 us
    unnamed x16, local copies, waits for them, and re-layouts  4.7 us
    broadcast_in_dim x1, local copies, waits for them, and re-layouts, exchange(): copies = jnp.broadcast_to(mine, (8, *mine.shape))  1.68 us
  transfers between devices with their start and end apart: 18, of which 6 were waited for; matrix products, arithmetic and copies ran while one was open for 3% of the time, Pallas kernels for 7%

profile of v4, /device:TPU:8, one launch (start us, length us, event | category | flops | bytes accessed | tf_op | source)
XLA Modules:
  0.0 82.4 jit_solution(11071733685255082337)
XLA Ops:
  0.7 0.9 %concatenate.33 = bf16[8,4224]{1,0:T(8,128)(2,1)S(1)} pad(bf16[8,4096]{1,0:T(8,128)(2,1)} %bitcast.13, bf16[]{:T(256)} %bitcast.10), padding=0_0x0_128 | pad | bytes 133122 | tf_op jit(solution)/shard_map/concatenate | solution.py:196
  1.6 5.2 %collective-permute-start = (bf16[8,4224]{1,0:T(8,128)(2,1)S(1)}, bf16[8,4224]{1,0:T(8,128)(2,1)S(1)}, u32[]{:S(2)}, u32[]{:S(2)}) collective-permute-start(bf16[8,4224]{1,0:T(8,128)(2,1)S(1)} %concatenate.33), channel_id=1, source_target_pairs={{0,0},{1,16},{2,32},{3,48},{4,64},{5,80},{6,96},{7,112},{8,8},{9,2... | collective-permute-start | bytes 202760 | tf_op jit(solution)/shard_map/ppermute | solution.py:176
  6.8 1.7 %broadcast_in_dim.23 = bf16[8,8,4096]{2,1,0:T(8,128)(2,1)} broadcast(bf16[8,4096]{1,0:T(8,128)(2,1)} %bitcast.14), dimensions={1,2} | broadcast | bytes 589824 | tf_op jit(solution)/shard_map/broadcast_in_dim | solution.py:198
  8.4 9.2 %all-to-all-start = ((bf16[8,8,4096]{2,1,0:T(8,128)(2,1)}), bf16[8,8,4096]{2,1,0:T(8,128)(2,1)S(1)}, u32[]{:S(2)}, u32[]{:S(2)}) async-start(bf16[8,8,4096]{2,1,0:T(8,128)(2,1)} %broadcast_in_dim.23), calls=%async_computation | async-start | bytes 1048576 | tf_op jit(solution)/shard_map/all_to_all | solution.py:199
  17.9 1.2 %collective-permute-done.1 = bf16[8,4224]{1,0:T(8,128)(2,1)S(1)} collective-permute-done((bf16[8,4224]{1,0:T(8,128)(2,1)S(1)}, bf16[8,4224]{1,0:T(8,128)(2,1)S(1)}, u32[]{:S(2)}, u32[]{:S(2)}) %collective-permute-start.1) | collective-permute-done | bytes 67616 | tf_op jit(solution)/shard_map/ppermute | solution.py:176
  19.1 1.6 %collective-permute-start.3 = (bf16[2,8,4224]{2,1,0:T(8,128)(2,1)S(1)}, bf16[2,8,4224]{2,1,0:T(8,128)(2,1)S(1)}, u32[]{:S(2)}, u32[]{:S(2)}) collective-permute-start(bf16[2,8,4224]{2,1,0:T(8,128)(2,1)S(1)} %pad_maximum_fusion.refs_0_), channel_id=1, source_target_pairs={{0,16},{1,17},{2,18},{3,19},{4,20},{5,21},{6,22},{7,23},{8,120},{9... | collective-permute-start | bytes 405512 | tf_op jit(solution)/shard_map/ppermute | solution.py:176
  21.3 4.4 %collective-permute-done.3.refs_1_ = bf16[2,8,4224]{2,1,0:T(8,128)(2,1)S(1)} collective-permute-done((bf16[2,8,4224]{2,1,0:T(8,128)(2,1)S(1)}, bf16[2,8,4224]{2,1,0:T(8,128)(2,1)S(1)}, u32[]{:S(2)}, u32[]{:S(2)}) %collective-permute-start.3) | collective-permute-done | bytes 135200 | tf_op jit(solution)/shard_map/ppermute | solution.py:176
  25.7 6.2 %collective-permute-done.5.refs_2_ = bf16[2,8,4224]{2,1,0:T(8,128)(2,1)S(1)} collective-permute-done((bf16[2,8,4224]{2,1,0:T(8,128)(2,1)S(1)}, bf16[2,8,4224]{2,1,0:T(8,128)(2,1)S(1)}, u32[]{:S(2)}, u32[]{:S(2)}) %collective-permute-start.5) | collective-permute-done | bytes 135200 | tf_op jit(solution)/shard_map/ppermute | solution.py:176
  31.9 0.8 collective-permute-start.10
  32.7 2.8 %collective-permute-start.4 = (bf16[2,8,4224]{2,1,0:T(8,128)(2,1)S(1)}, bf16[2,8,4224]{2,1,0:T(8,128)(2,1)S(1)}, u32[]{:S(2)}, u32[]{:S(2)}) collective-permute-start(bf16[2,8,4224]{2,1,0:T(8,128)(2,1)S(1)} %collective-permute-done.3.refs_1_), channel_id=1, source_target_pairs={{0,128},{1,129},{2,130},{3,131},{4,132},{5,133},{6,134},{7,135},{8... | collective-permute-start | bytes 405512 | tf_op jit(solution)/shard_map/ppermute | solution.py:176
  35.5 0.7 collective-permute-start.6
  36.2 2.0 %collective-permute-done.7.refs_3_ = bf16[2,8,4224]{2,1,0:T(8,128)(2,1)} collective-permute-done((bf16[2,8,4224]{2,1,0:T(8,128)(2,1)S(1)}, bf16[2,8,4224]{2,1,0:T(8,128)(2,1)}, u32[]{:S(2)}, u32[]{:S(2)}) %collective-permute-start.7) | collective-permute-done | bytes 135200 | tf_op jit(solution)/shard_map/ppermute | solution.py:176
  38.9 0.8 collective-permute-done.4.refs_1_
  39.7 3.8 %collective-permute-start.2 = (bf16[2,8,4224]{2,1,0:T(8,128)(2,1)S(1)}, bf16[2,8,4224]{2,1,0:T(8,128)(2,1)}, u32[]{:S(2)}, u32[]{:S(2)}) collective-permute-start(bf16[2,8,4224]{2,1,0:T(8,128)(2,1)S(1)} %pad_maximum_fusion.refs_0_), channel_id=1, source_target_pairs={{0,128},{1,129},{2,130},{3,131},{4,132},{5,133},{6,134},{7,135},{8... | collective-permute-start | bytes 405512 | tf_op jit(solution)/shard_map/ppermute | solution.py:176
  44.1 1.3 %collective-permute-start.8 = (bf16[2,8,4224]{2,1,0:T(8,128)(2,1)}, bf16[2,8,4224]{2,1,0:T(8,128)(2,1)}, u32[]{:S(2)}, u32[]{:S(2)}) collective-permute-start(bf16[2,8,4224]{2,1,0:T(8,128)(2,1)} %collective-permute-done.7.refs_3_), channel_id=1, source_target_pairs={{0,128},{1,129},{2,130},{3,131},{4,132},{5,133},{6,134},{7,135},{8... | collective-permute-start | bytes 405512 | tf_op jit(solution)/shard_map/ppermute | solution.py:176
  46.1 0.9 %copy-done.1 = bf16[2,8,4224]{2,1,0:T(8,128)(2,1)S(1)} copy-done((bf16[2,8,4224]{2,1,0:T(8,128)(2,1)S(1)}, bf16[2,8,4224]{2,1,0:T(8,128)(2,1)}, u32[]{:S(2)}) %copy-start.1) | copy-done | bytes 135192
  47.0 0.9 %copy-done.3 = bf16[2,8,4224]{2,1,0:T(8,128)(2,1)S(1)} copy-done((bf16[2,8,4224]{2,1,0:T(8,128)(2,1)S(1)}, bf16[2,8,4224]{2,1,0:T(8,128)(2,1)}, u32[]{:S(2)}) %copy-start.3) | copy-done | bytes 135192
  47.9 0.9 %copy-done.5 = bf16[2,8,4224]{2,1,0:T(8,128)(2,1)S(1)} copy-done((bf16[2,8,4224]{2,1,0:T(8,128)(2,1)S(1)}, bf16[2,8,4224]{2,1,0:T(8,128)(2,1)}, u32[]{:S(2)}) %copy-start.5) | copy-done | bytes 135192
  48.8 5.4 %solve.2.refs_11_ = f32[64,4096]{1,0:T(8,128)S(1)} custom-call(s32[1]{0:T(128)} %bitcast.4.seat_ref, bf16[64,4096]{1,0:T(8,128)(2,1)S(1)} %bitcast.11, bf16[2,8,4224]{2,1,0:T(8,128)(2,1)S(1)} %pad_maximum_fusion.refs_0_, bf16[2,8,4224]{2,1,0:T(8,128)(2,1)S(1)} %collective-permute-done.3.refs_1_, bf16[2,8,4224]{2,1,0:T(8,128)(2,1)S(1)} %collective-permute-done.5.refs_2_, ...), custom_call_target="tpu_custom_call" | custom-call | flops 10000000000 | bytes 10000000 | tf_op jit(solution)/shard_map/solve/pallas_call | solution.py:146
  54.2 2.6 %collective-permute-start.13 = (bf16[2,8,4224]{2,1,0:T(8,128)(2,1)}, bf16[2,8,4224]{2,1,0:T(8,128)(2,1)S(1)}, u32[]{:S(2)}, u32[]{:S(2)}) collective-permute-start(bf16[2,8,4224]{2,1,0:T(8,128)(2,1)} %collective-permute-done.9.refs_4_), channel_id=1, source_target_pairs={{0,128},{1,129},{2,130},{3,131},{4,132},{5,133},{6,134},{7,135},{8... | collective-permute-start | bytes 405512 | tf_op jit(solution)/shard_map/ppermute | solution.py:176
  56.8 5.2 %collective-permute-done.13.refs_4_ = bf16[2,8,4224]{2,1,0:T(8,128)(2,1)S(1)} collective-permute-done((bf16[2,8,4224]{2,1,0:T(8,128)(2,1)}, bf16[2,8,4224]{2,1,0:T(8,128)(2,1)S(1)}, u32[]{:S(2)}, u32[]{:S(2)}) %collective-permute-start.13) | collective-permute-done | bytes 135200 | tf_op jit(solution)/shard_map/ppermute | solution.py:176
  62.0 6.0 %solve.3 = f32[64,4224]{1,0:T(8,128)S(1)} custom-call(s32[1]{0:T(128)} %bitcast.4.seat_ref, bf16[64,4096]{1,0:T(8,128)(2,1)S(1)} %bitcast.12, bf16[2,8,4224]{2,1,0:T(8,128)(2,1)} %collective-permute-done.2.refs_0_, bf16[2,8,4224]{2,1,0:T(8,128)(2,1)S(1)} %collective-permute-done.4.refs_1_, bf16[2,8,4224]{2,1,0:T(8,128)(2,1)S(1)} %collective-permute-done.6.refs_2_, ...), custom_call_target="tpu_custom_call" | custom-call | flops 10000000000 | bytes 10000000 | tf_op jit(solution)/shard_map/solve/pallas_call | solution.py:146
  68.1 13.3 %all_to_all.10 = f16[8,8,4224]{2,1,0:T(8,128)(2,1)S(1)} all-to-all(f16[8,8,4224]{2,1,0:T(8,128)(2,1)S(1)} %convert_bitcast_fusion), channel_id=1, replica_groups=mesh['grp'=32,'dist'=8] {'dist'}, dimensions={0} | all-to-all | bytes 1081344 | tf_op jit(solution)/shard_map/all_to_all | solution.py:226
  81.6 0.8 %multiply_reduce_fusion = f32[8,4096]{1,0:T(8,128)} fusion(f16[8,8,4224]{2,1,0:T(8,128)(2,1)S(1)} %all_to_all.10, f32[8]{0:T(128)S(1)} %exponential_reduce_fusion), kind=kLoop, calls=%fused_computation.4 | loop fusion | flops 753664 | bytes 655392 | tf_op jit(solution)/shard_map/reduce_sum | solution.py:229
  (44 shorter events, 3.2 us)
Async XLA Ops:
  0.7 20.6 %copy-start.6 = (bf16[256,256]{1,0:T(8,128)(2,1)S(1)}, bf16[256,256]{1,0:T(8,128)(2,1)}, u32[]{:S(2)}) copy-start(bf16[256,256]{1,0:T(8,128)(2,1)} %constant.50) | copy-start | bytes 393220
  1.6 24.1 %copy-start.7 = (bf16[64,192]{1,0:T(8,128)(2,1)S(1)}, bf16[64,192]{1,0:T(8,128)(2,1)}, u32[]{:S(2)}) copy-start(bf16[64,192]{1,0:T(8,128)(2,1)} %constant.42) | copy-start | bytes 73732
  1.6 16.1 %collective-permute-start = (bf16[8,4224]{1,0:T(8,128)(2,1)S(1)}, bf16[8,4224]{1,0:T(8,128)(2,1)S(1)}, u32[]{:S(2)}, u32[]{:S(2)}) collective-permute-start(bf16[8,4224]{1,0:T(8,128)(2,1)S(1)} %concatenate.33), channel_id=1, source_target_pairs={{0,0},{1,16},{2,32},{3,48},{4,64},{5,80},{6,96},{7,112},{8,8},{9,2... | collective-permute-start | bytes 202760 | tf_op jit(solution)/shard_map/ppermute | solution.py:176
  8.4 37.6 %all-to-all-start = ((bf16[8,8,4096]{2,1,0:T(8,128)(2,1)}), bf16[8,8,4096]{2,1,0:T(8,128)(2,1)S(1)}, u32[]{:S(2)}, u32[]{:S(2)}) async-start(bf16[8,8,4096]{2,1,0:T(8,128)(2,1)} %broadcast_in_dim.23), calls=%async_computation | async-start | bytes 1048576 | tf_op jit(solution)/shard_map/all_to_all | solution.py:199
  17.7 1.3 %collective-permute-start.1 = (bf16[8,4224]{1,0:T(8,128)(2,1)S(1)}, bf16[8,4224]{1,0:T(8,128)(2,1)S(1)}, u32[]{:S(2)}, u32[]{:S(2)}) collective-permute-start(bf16[8,4224]{1,0:T(8,128)(2,1)S(1)} %collective-permute-done), channel_id=1, source_target_pairs={{0,8},{1,9},{2,10},{3,11},{4,12},{5,13},{6,14},{7,15},{8,0},{9,1},... | collective-permute-start | bytes 202760 | tf_op jit(solution)/shard_map/ppermute | solution.py:176
  19.1 6.6 %collective-permute-start.3 = (bf16[2,8,4224]{2,1,0:T(8,128)(2,1)S(1)}, bf16[2,8,4224]{2,1,0:T(8,128)(2,1)S(1)}, u32[]{:S(2)}, u32[]{:S(2)}) collective-permute-start(bf16[2,8,4224]{2,1,0:T(8,128)(2,1)S(1)} %pad_maximum_fusion.refs_0_), channel_id=1, source_target_pairs={{0,16},{1,17},{2,18},{3,19},{4,20},{5,21},{6,22},{7,23},{8,120},{9... | collective-permute-start | bytes 405512 | tf_op jit(solution)/shard_map/ppermute | solution.py:176
  25.6 6.2 %collective-permute-start.5 = (bf16[2,8,4224]{2,1,0:T(8,128)(2,1)S(1)}, bf16[2,8,4224]{2,1,0:T(8,128)(2,1)S(1)}, u32[]{:S(2)}, u32[]{:S(2)}) collective-permute-start(bf16[2,8,4224]{2,1,0:T(8,128)(2,1)S(1)} %collective-permute-done.3.refs_1_), channel_id=1, source_target_pairs={{0,16},{1,17},{2,18},{3,19},{4,20},{5,21},{6,22},{7,23},{8,120},{9... | collective-permute-start | bytes 405512 | tf_op jit(solution)/shard_map/ppermute | solution.py:176
  31.9 6.3 %collective-permute-start.7 = (bf16[2,8,4224]{2,1,0:T(8,128)(2,1)S(1)}, bf16[2,8,4224]{2,1,0:T(8,128)(2,1)}, u32[]{:S(2)}, u32[]{:S(2)}) collective-permute-start(bf16[2,8,4224]{2,1,0:T(8,128)(2,1)S(1)} %collective-permute-done.5.refs_2_), channel_id=1, source_target_pairs={{0,16},{1,17},{2,18},{3,19},{4,20},{5,21},{6,22},{7,23},{8,120},{9... | collective-permute-start | bytes 405512 | tf_op jit(solution)/shard_map/ppermute | solution.py:176
  31.9 6.3 %collective-permute-start.10 = (bf16[2,8,4224]{2,1,0:T(8,128)(2,1)S(1)}, bf16[2,8,4224]{2,1,0:T(8,128)(2,1)S(1)}, u32[]{:S(2)}, u32[]{:S(2)}) collective-permute-start(bf16[2,8,4224]{2,1,0:T(8,128)(2,1)S(1)} %collective-permute-done.3.refs_1_), channel_id=1, source_target_pairs={{0,8},{1,9},{2,10},{3,11},{4,12},{5,13},{6,14},{7,15},{8,0},{9,1},... | collective-permute-start | bytes 405512 | tf_op jit(solution)/shard_map/ppermute | solution.py:176
  32.7 7.0 %collective-permute-start.4 = (bf16[2,8,4224]{2,1,0:T(8,128)(2,1)S(1)}, bf16[2,8,4224]{2,1,0:T(8,128)(2,1)S(1)}, u32[]{:S(2)}, u32[]{:S(2)}) collective-permute-start(bf16[2,8,4224]{2,1,0:T(8,128)(2,1)S(1)} %collective-permute-done.3.refs_1_), channel_id=1, source_target_pairs={{0,128},{1,129},{2,130},{3,131},{4,132},{5,133},{6,134},{7,135},{8... | collective-permute-start | bytes 405512 | tf_op jit(solution)/shard_map/ppermute | solution.py:176
  35.5 8.0 %collective-permute-start.11 = (bf16[2,8,4224]{2,1,0:T(8,128)(2,1)S(1)}, bf16[2,8,4224]{2,1,0:T(8,128)(2,1)S(1)}, u32[]{:S(2)}, u32[]{:S(2)}) collective-permute-start(bf16[2,8,4224]{2,1,0:T(8,128)(2,1)S(1)} %collective-permute-done.5.refs_2_), channel_id=1, source_target_pairs={{0,8},{1,9},{2,10},{3,11},{4,12},{5,13},{6,14},{7,15},{8,0},{9,1},... | collective-permute-start | bytes 405512 | tf_op jit(solution)/shard_map/ppermute | solution.py:176
  35.5 8.6 %collective-permute-start.6 = (bf16[2,8,4224]{2,1,0:T(8,128)(2,1)S(1)}, bf16[2,8,4224]{2,1,0:T(8,128)(2,1)S(1)}, u32[]{:S(2)}, u32[]{:S(2)}) collective-permute-start(bf16[2,8,4224]{2,1,0:T(8,128)(2,1)S(1)} %collective-permute-done.5.refs_2_), channel_id=1, source_target_pairs={{0,128},{1,129},{2,130},{3,131},{4,132},{5,133},{6,134},{7,135},{8... | collective-permute-start | bytes 405512 | tf_op jit(solution)/shard_map/ppermute | solution.py:176
  38.2 7.2 %collective-permute-start.12 = (bf16[2,8,4224]{2,1,0:T(8,128)(2,1)}, bf16[2,8,4224]{2,1,0:T(8,128)(2,1)S(1)}, u32[]{:S(2)}, u32[]{:S(2)}) collective-permute-start(bf16[2,8,4224]{2,1,0:T(8,128)(2,1)} %collective-permute-done.7.refs_3_), channel_id=1, source_target_pairs={{0,8},{1,9},{2,10},{3,11},{4,12},{5,13},{6,14},{7,15},{8,0},{9,1},... | collective-permute-start | bytes 405512 | tf_op jit(solution)/shard_map/ppermute | solution.py:176
  38.9 7.2 %collective-permute-start.9 = (bf16[2,8,4224]{2,1,0:T(8,128)(2,1)}, bf16[2,8,4224]{2,1,0:T(8,128)(2,1)}, u32[]{:S(2)}, u32[]{:S(2)}) collective-permute-start(bf16[2,8,4224]{2,1,0:T(8,128)(2,1)} %collective-permute-done.7.refs_3_), channel_id=1, source_target_pairs={{0,16},{1,17},{2,18},{3,19},{4,20},{5,21},{6,22},{7,23},{8,120},{9... | collective-permute-start | bytes 405512 | tf_op jit(solution)/shard_map/ppermute | solution.py:176
  39.7 17.2 %collective-permute-start.2 = (bf16[2,8,4224]{2,1,0:T(8,128)(2,1)S(1)}, bf16[2,8,4224]{2,1,0:T(8,128)(2,1)}, u32[]{:S(2)}, u32[]{:S(2)}) collective-permute-start(bf16[2,8,4224]{2,1,0:T(8,128)(2,1)S(1)} %pad_maximum_fusion.refs_0_), channel_id=1, source_target_pairs={{0,128},{1,129},{2,130},{3,131},{4,132},{5,133},{6,134},{7,135},{8... | collective-permute-start | bytes 405512 | tf_op jit(solution)/shard_map/ppermute | solution.py:176
  43.5 0.7 copy-start.2
  44.1 12.7 %collective-permute-start.14 = (bf16[2,8,4224]{2,1,0:T(8,128)(2,1)S(1)}, bf16[2,8,4224]{2,1,0:T(8,128)(2,1)}, u32[]{:S(2)}, u32[]{:S(2)}) collective-permute-start(bf16[2,8,4224]{2,1,0:T(8,128)(2,1)S(1)} %collective-permute-done.4.refs_1_), channel_id=1, source_target_pairs={{0,8},{1,9},{2,10},{3,11},{4,12},{5,13},{6,14},{7,15},{8,0},{9,1},... | collective-permute-start | bytes 405512 | tf_op jit(solution)/shard_map/ppermute | solution.py:176
  44.1 10.1 %collective-permute-start.8 = (bf16[2,8,4224]{2,1,0:T(8,128)(2,1)}, bf16[2,8,4224]{2,1,0:T(8,128)(2,1)}, u32[]{:S(2)}, u32[]{:S(2)}) collective-permute-start(bf16[2,8,4224]{2,1,0:T(8,128)(2,1)} %collective-permute-done.7.refs_3_), channel_id=1, source_target_pairs={{0,128},{1,129},{2,130},{3,131},{4,132},{5,133},{6,134},{7,135},{8... | collective-permute-start | bytes 405512 | tf_op jit(solution)/shard_map/ppermute | solution.py:176
  46.0 10.8 %collective-permute-start.15 = (bf16[2,8,4224]{2,1,0:T(8,128)(2,1)S(1)}, bf16[2,8,4224]{2,1,0:T(8,128)(2,1)}, u32[]{:S(2)}, u32[]{:S(2)}) collective-permute-start(bf16[2,8,4224]{2,1,0:T(8,128)(2,1)S(1)} %collective-permute-done.6.refs_2_), channel_id=1, source_target_pairs={{0,8},{1,9},{2,10},{3,11},{4,12},{5,13},{6,14},{7,15},{8,0},{9,1},... | collective-permute-start | bytes 405512 | tf_op jit(solution)/shard_map/ppermute | solution.py:176
  46.1 0.9 %copy-start.1 = (bf16[2,8,4224]{2,1,0:T(8,128)(2,1)S(1)}, bf16[2,8,4224]{2,1,0:T(8,128)(2,1)}, u32[]{:S(2)}) copy-start(bf16[2,8,4224]{2,1,0:T(8,128)(2,1)} %copy-done) | copy-start | bytes 405508
  47.0 0.9 %copy-start.3 = (bf16[2,8,4224]{2,1,0:T(8,128)(2,1)S(1)}, bf16[2,8,4224]{2,1,0:T(8,128)(2,1)}, u32[]{:S(2)}) copy-start(bf16[2,8,4224]{2,1,0:T(8,128)(2,1)} %copy-done.2) | copy-start | bytes 405508
  47.9 0.9 %copy-start.5 = (bf16[2,8,4224]{2,1,0:T(8,128)(2,1)S(1)}, bf16[2,8,4224]{2,1,0:T(8,128)(2,1)}, u32[]{:S(2)}) copy-start(bf16[2,8,4224]{2,1,0:T(8,128)(2,1)} %copy-done.4) | copy-start | bytes 405508
  54.2 7.8 %collective-permute-start.13 = (bf16[2,8,4224]{2,1,0:T(8,128)(2,1)}, bf16[2,8,4224]{2,1,0:T(8,128)(2,1)S(1)}, u32[]{:S(2)}, u32[]{:S(2)}) collective-permute-start(bf16[2,8,4224]{2,1,0:T(8,128)(2,1)} %collective-permute-done.9.refs_4_), channel_id=1, source_target_pairs={{0,128},{1,129},{2,130},{3,131},{4,132},{5,133},{6,134},{7,135},{8... | collective-permute-start | bytes 405512 | tf_op jit(solution)/shard_map/ppermute | solution.py:176
  56.8 5.2 %collective-permute-start.16 = (bf16[2,8,4224]{2,1,0:T(8,128)(2,1)}, bf16[2,8,4224]{2,1,0:T(8,128)(2,1)S(1)}, u32[]{:S(2)}, u32[]{:S(2)}) collective-permute-start(bf16[2,8,4224]{2,1,0:T(8,128)(2,1)} %collective-permute-done.8.refs_3_), channel_id=1, source_target_pairs={{0,8},{1,9},{2,10},{3,11},{4,12},{5,13},{6,14},{7,15},{8,0},{9,1},... | collective-permute-start | bytes 405512 | tf_op jit(solution)/shard_map/ppermute | solution.py:176
  (2 other events, 1.3 us)

commit v5 on v4

--- a/solution.py
+++ b/solution.py
@@ -61,25 +61,27 @@
 
 
 def solve_kernel(first, seat_ref, row_ref, *refs):
-    pair_ref, near_refs, fourth_ref, other_refs = refs[0], refs[1:4], refs[4], refs[5:8]
-    left_ref, right_ref, green_ref = refs[8:11]
+    early_ref, late_ref, fourth_ref, other_early_ref, other_late_ref = refs[:5]
+    left_ref, right_ref, green_ref = refs[5:8]
     col_ref, f_ref = refs[-2:]
     out_ref = refs[-3]
     group = seat_ref[0]
     core = jnp.bitwise_and(group, 1)
     z = jnp.bitwise_and(jnp.right_shift(group, 1), 7)
 
-    def place(ref, holder, block):
+    def place(ref, start, holder, block):
         rows = pl.ds(pl.multiple_of(8 * jnp.bitwise_and(block + 8, 7), 8), 8)
         for i in range(2):
-            col_ref[jnp.bitwise_xor(i, holder), rows, :] = ref[i].astype(jnp.float32)
-
-    place(pair_ref, core, z)
-    place(fourth_ref, core, z + 4)
-    for k in (1, 2, 3):
-        step = jnp.where(core == 0, -k, k)
-        place(near_refs[k - 1], core, z + step)
-        place(other_refs[k - 1], 1 - core, z - step)
+            col_ref[jnp.bitwise_xor(i, holder), rows, :] = ref[start + i].astype(jnp.float32)
+
+    place(early_ref, 0, core, z)
+    place(fourth_ref, 0, core, z + 4)
+    sides = ((core, early_ref, late_ref), (1 - core, other_early_ref, other_late_ref))
+    for holder, early, late in sides:
+        sign = jnp.where(holder == 0, -1, 1)
+        place(early, 2, holder, z + sign)
+        place(late, 0, holder, z + 3 * sign)
+        place(late, 2, holder, z + 2 * sign)
 
     left = left_ref[...]
     right = right_ref[...]
@@ -123,7 +125,7 @@
         v2 = jnp.where(low, pltpu.roll(p0, 64, 1), p1)
         term = v1 * (col_ref[0, :, lanes] * occ[0]) + v2 * (col_ref[1, :, lanes] * occ[1])
         if not first:
-            term = refs[11][:, lanes] + term
+            term = refs[8][:, lanes] + term
         out_ref[:, lanes] = term
 
     if not first:
@@ -139,6 +141,26 @@
         out_ref[:, 4096:4224] = jnp.broadcast_to(power[0:1], (GRID, 128))
 
 
+def copies_kernel(x_ref, out_ref, sem):
+    sends = [pltpu.make_async_copy(x_ref, out_ref.at[i], sem.at[i]) for i in range(8)]
+    for send in sends:
+        send.start()
+    for send in sends:
+        send.wait()
+
+
+def copies_of(x):
+    return pl.pallas_call(
+        copies_kernel,
+        out_shape=jax.ShapeDtypeStruct((8, *x.shape), x.dtype),
+        in_specs=[pl.BlockSpec(memory_space=pltpu.VMEM)],
+        out_specs=pl.BlockSpec(memory_space=pl.ANY),
+        scratch_shapes=[pltpu.SemaphoreType.DMA((8,))],
+        compiler_params=pltpu.CompilerParams(vmem_limit_bytes=2**20),
+        name="copies",
+    )(x)
+
+
 def solve(seat, row, mine, other, left, right, green, *more):
     vm = pl.BlockSpec(memory_space=pltpu.VMEM)
     sm = pl.BlockSpec(memory_space=pltpu.SMEM)
@@ -146,7 +168,7 @@
     return pl.pallas_call(
         functools.partial(solve_kernel, not more),
         out_shape=jax.ShapeDtypeStruct((GRID, width), jnp.float32),
-        in_specs=[sm] + [vm] * (12 + len(more)),
+        in_specs=[sm] + [vm] * (9 + len(more)),
         out_specs=vm,
         scratch_shapes=[
             pltpu.VMEM((2, GRID, GRID * GRID + 128), jnp.float32),
@@ -195,7 +217,7 @@
 def exchange(mine, occupation):
     slice_out = jnp.concatenate([mine, jnp.broadcast_to(occupation, (8, 128))], axis=1)
     kept = moved(slice_out, lambda h, z, c, l: (h, l, c, z))
-    copies = jnp.broadcast_to(mine, (8, *mine.shape))
+    copies = copies_of(mine)
     row = lax.all_to_all(copies, "dist", split_axis=0, concat_axis=0, tiled=True)
     row = row.reshape(GRID, GRID * GRID)
     crossed = moved(kept, cores)
@@ -206,22 +228,25 @@
     left = jnp.where(live, left, 0)
     right = jnp.where(live, right, 0)
     green = green_table(live)
-    chain, far, core = [pair], [], [None]
-    for k in range(5):
-        if k == 2:
-            chain[k], left, right, green = lax.optimization_barrier((chain[k], left, right, green))
-        if k < 4:
-            chain.append(moved(chain[k], ring(1)))
-        if k in (1, 2, 3):
-            core.append(moved(chain[k], cores))
-        far.append(moved(chain[k], halves))
-    far_core = []
-    for k in (1, 2):
-        far_core.append(moved(far[k], cores))
-    partial = solve(seat, row, chain, core[1:], left, right, green)
-    far[3], partial = lax.optimization_barrier((far[3], partial))
-    far_core.append(moved(far[3], cores))
-    partial = solve(seat, row, far, far_core, left, right, green, partial)
+    hop = {}
+    for k in (1, 3, 2):
+        hop[k] = moved(pair, ring(k))
+    early = jnp.concatenate([pair, hop[1]])
+    far_early = moved(early, halves)
+    core_early = moved(early, cores)
+    hop[3], left, right, green = lax.optimization_barrier((hop[3], left, right, green))
+    fourth = moved(hop[3], ring(1))
+    late = jnp.concatenate([hop[3], hop[2]])
+    core_late = moved(late, cores)
+    far_late = moved(late, halves)
+    far_fourth = moved(fourth, halves)
+    far_core_early = moved(far_early, cores)
+    mine, other = (early, late, fourth), (core_early, core_late)
+    partial = solve(seat, row, mine, other, left, right, green)
+    far_late, partial = lax.optimization_barrier((far_late, partial))
+    far_core_late = moved(far_late, cores)
+    mine, other = (far_early, far_late, far_fourth), (far_core_early, far_core_late)
+    partial = solve(seat, row, mine, other, left, right, green, partial)
     sent = partial.astype(jnp.float16).reshape(8, 8, GRID * GRID + 128)
     arrived = lax.all_to_all(sent, "dist", split_axis=0, concat_axis=0, tiled=True)
     power = lax.optimization_barrier(arrived[:, 0:1, GRID * GRID : GRID * GRID + 1])

time: 83 us -> 81.9 us (0.987)
  local copies, waits for them, and re-layouts: 7.26 us -> 3.56 us
  waiting for transfers between devices: 19.7 us -> 20.9 us
  Pallas kernels: 11.4 us -> 12.3 us
    unnamed x16 -> x8, local copies, waits for them, and re-layouts: 4.7 us -> 1.77 us
    broadcast_in_dim x1 -> x0, local copies, waits for them, and re-layouts: 1.68 us -> none  [exchange(): copies = jnp.broadcast_to(mine, (8, *mine.shape))]
    ppermute x17 -> x13, waiting for transfers between devices: 19.7 us -> 20.9 us  [moved(): return lax.ppermute(x, AXES, pairs)]
    concatenate x0 -> x2, local copies, waits for them, and re-layouts: none -> 0.94 us  [the longest x1 0.92 us: exchange(): late = jnp.concatenate([hop[3], hop[2]])]
    pallas_call x0 -> x1, Pallas kernels: none -> 0.87 us  [copies_of(): pl.pallas_call(copies_kernel, out_shape=jax.ShapeDtypeStruct((8, *x.shape...]
    ppermute x17 -> x13, starting transfers between devices: 18.8 us -> 18.7 us  [moved(): return lax.ppermute(x, AXES, pairs)]
  transfers between devices with their start and end apart: 18 -> 14, of which waited for: 6 -> 5; matrix products, arithmetic and copies ran while one was open for 3% -> 3% of each run, Pallas kernels for 7% -> 8%
where the time goes in v5:
time: 81.9 us; the launch traced here: 80.7 us
  starting transfers between devices  27.8 us (34%)
  waiting for transfers between devices  20.9 us (26%)
  blocking collectives  13.3 us (16%)
  Pallas kernels  12.3 us (15%)
  local copies, waits for them, and re-layouts  3.56 us (4%)
  other arithmetic  1.85 us (2%)
  between operations  0.85 us (1%)
    ppermute x13, waiting for transfers between devices, moved(): return lax.ppermute(x, AXES, pairs)  20.9 us
    ppermute x13, starting transfers between devices, moved(): return lax.ppermute(x, AXES, pairs)  18.7 us
    all_to_all x1, blocking collectives, exchange(): lax.all_to_all(sent, 'dist', split_axis=0, concat_axis=0, tiled=True)  13.3 us
    pallas_call x2, Pallas kernels, solve(): pl.pallas_call(functools.partial(solve_kernel, not more), out_shape=jax.S...  11.4 us
    all_to_all x1, starting transfers between devices, exchange(): lax.all_to_all(copies, 'dist', split_axis=0, concat_axis=0, tiled=True)  9.19 us
    unnamed x8, local copies, waits for them, and re-layouts  1.77 us
  transfers between devices with their start and end apart: 14, of which 5 were waited for; matrix products, arithmetic and copies ran while one was open for 3% of the time, Pallas kernels for 8%

profile of v5, /device:TPU:8, one launch (start us, length us, event | category | flops | bytes accessed | tf_op | source)
XLA Modules:
  0.0 80.7 jit_solution(12562924483376985843)
XLA Ops:
  0.7 0.8 %concatenate.39 = bf16[8,4224]{1,0:T(8,128)(2,1)S(1)} pad(bf16[8,4096]{1,0:T(8,128)(2,1)} %bitcast.13, bf16[]{:T(256)} %bitcast.10), padding=0_0x0_128 | pad | bytes 133122 | tf_op jit(solution)/shard_map/concatenate | solution.py:218
  1.5 5.1 %collective-permute-start = (bf16[8,4224]{1,0:T(8,128)(2,1)S(1)}, bf16[8,4224]{1,0:T(8,128)(2,1)S(1)}, u32[]{:S(2)}, u32[]{:S(2)}) collective-permute-start(bf16[8,4224]{1,0:T(8,128)(2,1)S(1)} %concatenate.39), channel_id=1, source_target_pairs={{0,0},{1,16},{2,32},{3,48},{4,64},{5,80},{6,96},{7,112},{8,8},{9,2... | collective-permute-start | bytes 202760 | tf_op jit(solution)/shard_map/ppermute | solution.py:198
  6.6 0.8 %copy-done = bf16[1,8,4096]{2,1,0:T(8,128)(2,1)S(1)} copy-done((bf16[1,8,4096]{2,1,0:T(8,128)(2,1)S(1)}, bf16[1,8,4096]{2,1,0:T(8,128)(2,1)}, u32[]{:S(2)}) %copy-start) | copy-done | bytes 65560
  7.5 0.9 %copies.1 = bf16[8,8,4096]{2,1,0:T(8,128)(2,1)} custom-call(bf16[8,4096]{1,0:T(8,128)(2,1)S(1)} %bitcast.14), custom_call_target="tpu_custom_call" | custom-call | tf_op jit(solution)/shard_map/copies/pallas_call | solution.py:153
  8.3 9.2 %all-to-all-start = ((bf16[8,8,4096]{2,1,0:T(8,128)(2,1)}), bf16[8,8,4096]{2,1,0:T(8,128)(2,1)S(1)}, u32[]{:S(2)}, u32[]{:S(2)}) async-start(bf16[8,8,4096]{2,1,0:T(8,128)(2,1)} %copies.1), calls=%async_computation | async-start | bytes 1048576 | tf_op jit(solution)/shard_map/all_to_all | solution.py:221
  17.8 1.2 %collective-permute-done.1 = bf16[8,4224]{1,0:T(8,128)(2,1)S(1)} collective-permute-done((bf16[8,4224]{1,0:T(8,128)(2,1)S(1)}, bf16[8,4224]{1,0:T(8,128)(2,1)S(1)}, u32[]{:S(2)}, u32[]{:S(2)}) %collective-permute-start.1) | collective-permute-done | bytes 67616 | tf_op jit(solution)/shard_map/ppermute | solution.py:198
  19.0 2.3 %collective-permute-start.5 = (bf16[2,8,4224]{2,1,0:T(8,128)(2,1)S(1)}, bf16[2,8,4224]{2,1,0:T(8,128)(2,1)}, u32[]{:S(2)}, u32[]{:S(2)}) collective-permute-start(bf16[2,8,4224]{2,1,0:T(8,128)(2,1)S(1)} %pad_maximum_fusion), channel_id=1, source_target_pairs={{0,32},{1,33},{2,34},{3,35},{4,36},{5,37},{6,38},{7,39},{8,104},{9... | collective-permute-start | bytes 405512 | tf_op jit(solution)/shard_map/ppermute | solution.py:198
  21.3 1.4 %collective-permute-start.4 = (bf16[2,8,4224]{2,1,0:T(8,128)(2,1)S(1)}, bf16[2,8,4224]{2,1,0:T(8,128)(2,1)}, u32[]{:S(2)}, u32[]{:S(2)}) collective-permute-start(bf16[2,8,4224]{2,1,0:T(8,128)(2,1)S(1)} %pad_maximum_fusion), channel_id=1, source_target_pairs={{0,48},{1,49},{2,50},{3,51},{4,52},{5,53},{6,54},{7,55},{8,88},{9,... | collective-permute-start | bytes 405512 | tf_op jit(solution)/shard_map/ppermute | solution.py:198
  22.6 2.0 %collective-permute-start.2 = (bf16[2,8,4224]{2,1,0:T(8,128)(2,1)S(1)}, bf16[2,8,4224]{2,1,0:T(8,128)(2,1)S(1)}, u32[]{:S(2)}, u32[]{:S(2)}) collective-permute-start(bf16[2,8,4224]{2,1,0:T(8,128)(2,1)S(1)} %pad_maximum_fusion), channel_id=1, source_target_pairs={{0,16},{1,17},{2,18},{3,19},{4,20},{5,21},{6,22},{7,23},{8,120},{9... | collective-permute-start | bytes 405512 | tf_op jit(solution)/shard_map/ppermute | solution.py:198
  24.7 0.6 fusion.1.refs_7_
  25.3 8.2 %collective-permute-done.2 = bf16[2,8,4224]{2,1,0:T(8,128)(2,1)S(1)} collective-permute-done((bf16[2,8,4224]{2,1,0:T(8,128)(2,1)S(1)}, bf16[2,8,4224]{2,1,0:T(8,128)(2,1)S(1)}, u32[]{:S(2)}, u32[]{:S(2)}) %collective-permute-start.2) | collective-permute-done | bytes 135200 | tf_op jit(solution)/shard_map/ppermute | solution.py:198
  33.6 0.9 %constant_dynamic-update-slice_fusion.3 = bf16[4,8,4224]{2,1,0:T(8,128)(2,1)S(1)} fusion(bf16[2,8,4224]{2,1,0:T(8,128)(2,1)} %collective-permute-done.4), kind=kLoop, calls=%fused_computation.13 | loop fusion | bytes 270336
  34.5 0.9 %constant_dynamic-update-slice_fusion.2.refs_1_ = bf16[4,8,4224]{2,1,0:T(8,128)(2,1)S(1)} fusion(bf16[4,8,4224]{2,1,0:T(8,128)(2,1)S(1)} %constant_dynamic-update-slice_fusion.3, bf16[2,8,4224]{2,1,0:T(8,128)(2,1)} %collective-permute-done.5), kind=kLoop, calls=%fused_computation.12 | loop fusion | bytes 270336 | tf_op jit(solution)/shard_map/concatenate | solution.py:239
  35.4 0.6 collective-permute-start.9
  36.1 3.1 %collective-permute-start.3 = (bf16[4,8,4224]{2,1,0:T(8,128)(2,1)S(1)}, bf16[4,8,4224]{2,1,0:T(8,128)(2,1)}, u32[]{:S(2)}, u32[]{:S(2)}) collective-permute-start(bf16[4,8,4224]{2,1,0:T(8,128)(2,1)S(1)} %constant_dynamic-update-slice_fusion.refs_0_), channel_id=1, source_target_pairs={{0,128},{1,129},{2,130},{3,131},{4,132},{5,133},{6,134},{7,135},{8... | collective-permute-start | bytes 811016 | tf_op jit(solution)/shard_map/ppermute | solution.py:198
  39.2 0.4 collective-permute-start.6
  39.6 2.9 %collective-permute-done.7.refs_2_ = bf16[2,8,4224]{2,1,0:T(8,128)(2,1)S(1)} collective-permute-done((bf16[2,8,4224]{2,1,0:T(8,128)(2,1)}, bf16[2,8,4224]{2,1,0:T(8,128)(2,1)S(1)}, u32[]{:S(2)}, u32[]{:S(2)}) %collective-permute-start.7) | collective-permute-done | bytes 135200 | tf_op jit(solution)/shard_map/ppermute | solution.py:198
  42.5 5.5 %solve.2.refs_8_ = f32[64,4096]{1,0:T(8,128)S(1)} custom-call(s32[1]{0:T(128)} %bitcast.4.seat_ref, bf16[64,4096]{1,0:T(8,128)(2,1)S(1)} %bitcast.11, bf16[4,8,4224]{2,1,0:T(8,128)(2,1)S(1)} %constant_dynamic-update-slice_fusion.refs_0_, bf16[4,8,4224]{2,1,0:T(8,128)(2,1)S(1)} %constant_dynamic-update-slice_fusion.2.refs_1_, ...), custom_call_target="tpu_custom_call" | custom-call | flops 10000000000 | bytes 10000000 | tf_op jit(solution)/shard_map/solve/pallas_call | solution.py:168
  48.0 4.8 %collective-permute-done.6.refs_1_ = bf16[4,8,4224]{2,1,0:T(8,128)(2,1)} collective-permute-done((bf16[4,8,4224]{2,1,0:T(8,128)(2,1)S(1)}, bf16[4,8,4224]{2,1,0:T(8,128)(2,1)}, u32[]{:S(2)}, u32[]{:S(2)}) %collective-permute-start.6) | collective-permute-done | bytes 270368 | tf_op jit(solution)/shard_map/ppermute | solution.py:198
  53.3 3.1 %collective-permute-start.10 = (bf16[2,8,4224]{2,1,0:T(8,128)(2,1)S(1)}, bf16[2,8,4224]{2,1,0:T(8,128)(2,1)S(1)}, u32[]{:S(2)}, u32[]{:S(2)}) collective-permute-start(bf16[2,8,4224]{2,1,0:T(8,128)(2,1)S(1)} %collective-permute-done.7.refs_2_), channel_id=1, source_target_pairs={{0,128},{1,129},{2,130},{3,131},{4,132},{5,133},{6,134},{7,135},{8... | collective-permute-start | bytes 405512 | tf_op jit(solution)/shard_map/ppermute | solution.py:198
  56.4 4.0 %collective-permute-done.10.refs_2_ = bf16[2,8,4224]{2,1,0:T(8,128)(2,1)S(1)} collective-permute-done((bf16[2,8,4224]{2,1,0:T(8,128)(2,1)S(1)}, bf16[2,8,4224]{2,1,0:T(8,128)(2,1)S(1)}, u32[]{:S(2)}, u32[]{:S(2)}) %collective-permute-start.10) | collective-permute-done | bytes 135200 | tf_op jit(solution)/shard_map/ppermute | solution.py:198
  60.4 5.9 %solve.3 = f32[64,4224]{1,0:T(8,128)S(1)} custom-call(s32[1]{0:T(128)} %bitcast.4.seat_ref, bf16[64,4096]{1,0:T(8,128)(2,1)S(1)} %bitcast.12, bf16[4,8,4224]{2,1,0:T(8,128)(2,1)} %collective-permute-done.3.refs_0_, bf16[4,8,4224]{2,1,0:T(8,128)(2,1)} %collective-permute-done.6.refs_1_, bf16[2,8,4224]{2,1,0:T(8,128)(2,1)S(1)} %collective-permute-done.10.refs_2_, ...), custom_call_target="tpu_custom_call" | custom-call | flops 10000000000 | bytes 10000000 | tf_op jit(solution)/shard_map/solve/pallas_call | solution.py:168
  66.3 13.3 %all_to_all.10 = f16[8,8,4224]{2,1,0:T(8,128)(2,1)S(1)} all-to-all(f16[8,8,4224]{2,1,0:T(8,128)(2,1)S(1)} %convert_bitcast_fusion), channel_id=1, replica_groups=mesh['grp'=32,'dist'=8] {'dist'}, dimensions={0} | all-to-all | bytes 1081344 | tf_op jit(solution)/shard_map/all_to_all | solution.py:251
  79.8 0.8 %multiply_reduce_fusion = f32[8,4096]{1,0:T(8,128)} fusion(f16[8,8,4224]{2,1,0:T(8,128)(2,1)S(1)} %all_to_all.10, f32[8]{0:T(128)S(1)} %exponential_reduce_fusion), kind=kLoop, calls=%fused_computation.4 | loop fusion | flops 753664 | bytes 655392 | tf_op jit(solution)/shard_map/reduce_sum | solution.py:254
  (30 shorter events, 1.2 us)
Async XLA Ops:
  0.0 24.6 %copy-start.1 = (bf16[256,256]{1,0:T(8,128)(2,1)S(1)}, bf16[256,256]{1,0:T(8,128)(2,1)}, u32[]{:S(2)}) copy-start(bf16[256,256]{1,0:T(8,128)(2,1)} %constant.50) | copy-start | bytes 393220
  1.5 16.1 %collective-permute-start = (bf16[8,4224]{1,0:T(8,128)(2,1)S(1)}, bf16[8,4224]{1,0:T(8,128)(2,1)S(1)}, u32[]{:S(2)}, u32[]{:S(2)}) collective-permute-start(bf16[8,4224]{1,0:T(8,128)(2,1)S(1)} %concatenate.39), channel_id=1, source_target_pairs={{0,0},{1,16},{2,32},{3,48},{4,64},{5,80},{6,96},{7,112},{8,8},{9,2... | collective-permute-start | bytes 202760 | tf_op jit(solution)/shard_map/ppermute | solution.py:198
  6.6 0.8 %copy-start = (bf16[1,8,4096]{2,1,0:T(8,128)(2,1)S(1)}, bf16[1,8,4096]{2,1,0:T(8,128)(2,1)}, u32[]{:S(2)}) copy-start(bf16[1,8,4096]{2,1,0:T(8,128)(2,1)} %param.4) | copy-start | bytes 196612
  8.3 16.9 %copy-start.2 = (bf16[64,192]{1,0:T(8,128)(2,1)S(1)}, bf16[64,192]{1,0:T(8,128)(2,1)}, u32[]{:S(2)}) copy-start(bf16[64,192]{1,0:T(8,128)(2,1)} %constant.42) | copy-start | bytes 73732
  8.3 34.1 %all-to-all-start = ((bf16[8,8,4096]{2,1,0:T(8,128)(2,1)}), bf16[8,8,4096]{2,1,0:T(8,128)(2,1)S(1)}, u32[]{:S(2)}, u32[]{:S(2)}) async-start(bf16[8,8,4096]{2,1,0:T(8,128)(2,1)} %copies.1), calls=%async_computation | async-start | bytes 1048576 | tf_op jit(solution)/shard_map/all_to_all | solution.py:221
  17.6 1.3 %collective-permute-start.1 = (bf16[8,4224]{1,0:T(8,128)(2,1)S(1)}, bf16[8,4224]{1,0:T(8,128)(2,1)S(1)}, u32[]{:S(2)}, u32[]{:S(2)}) collective-permute-start(bf16[8,4224]{1,0:T(8,128)(2,1)S(1)} %collective-permute-done), channel_id=1, source_target_pairs={{0,8},{1,9},{2,10},{3,11},{4,12},{5,13},{6,14},{7,15},{8,0},{9,1},... | collective-permute-start | bytes 202760 | tf_op jit(solution)/shard_map/ppermute | solution.py:198
  19.0 15.5 %collective-permute-start.5 = (bf16[2,8,4224]{2,1,0:T(8,128)(2,1)S(1)}, bf16[2,8,4224]{2,1,0:T(8,128)(2,1)}, u32[]{:S(2)}, u32[]{:S(2)}) collective-permute-start(bf16[2,8,4224]{2,1,0:T(8,128)(2,1)S(1)} %pad_maximum_fusion), channel_id=1, source_target_pairs={{0,32},{1,33},{2,34},{3,35},{4,36},{5,37},{6,38},{7,39},{8,104},{9... | collective-permute-start | bytes 405512 | tf_op jit(solution)/shard_map/ppermute | solution.py:198
  21.3 12.3 %collective-permute-start.4 = (bf16[2,8,4224]{2,1,0:T(8,128)(2,1)S(1)}, bf16[2,8,4224]{2,1,0:T(8,128)(2,1)}, u32[]{:S(2)}, u32[]{:S(2)}) collective-permute-start(bf16[2,8,4224]{2,1,0:T(8,128)(2,1)S(1)} %pad_maximum_fusion), channel_id=1, source_target_pairs={{0,48},{1,49},{2,50},{3,51},{4,52},{5,53},{6,54},{7,55},{8,88},{9,... | collective-permute-start | bytes 405512 | tf_op jit(solution)/shard_map/ppermute | solution.py:198
  22.6 10.8 %collective-permute-start.2 = (bf16[2,8,4224]{2,1,0:T(8,128)(2,1)S(1)}, bf16[2,8,4224]{2,1,0:T(8,128)(2,1)S(1)}, u32[]{:S(2)}, u32[]{:S(2)}) collective-permute-start(bf16[2,8,4224]{2,1,0:T(8,128)(2,1)S(1)} %pad_maximum_fusion), channel_id=1, source_target_pairs={{0,16},{1,17},{2,18},{3,19},{4,20},{5,21},{6,22},{7,23},{8,120},{9... | collective-permute-start | bytes 405512 | tf_op jit(solution)/shard_map/ppermute | solution.py:198
  33.5 9.0 %collective-permute-start.8 = (bf16[4,8,4224]{2,1,0:T(8,128)(2,1)S(1)}, bf16[4,8,4224]{2,1,0:T(8,128)(2,1)}, u32[]{:S(2)}, u32[]{:S(2)}) collective-permute-start(bf16[4,8,4224]{2,1,0:T(8,128)(2,1)S(1)} %constant_dynamic-update-slice_fusion.refs_0_), channel_id=1, source_target_pairs={{0,8},{1,9},{2,10},{3,11},{4,12},{5,13},{6,14},{7,15},{8,0},{9,1},... | collective-permute-start | bytes 811016 | tf_op jit(solution)/shard_map/ppermute | solution.py:198
  35.4 7.0 %collective-permute-start.9 = (bf16[4,8,4224]{2,1,0:T(8,128)(2,1)S(1)}, bf16[4,8,4224]{2,1,0:T(8,128)(2,1)}, u32[]{:S(2)}, u32[]{:S(2)}) collective-permute-start(bf16[4,8,4224]{2,1,0:T(8,128)(2,1)S(1)} %constant_dynamic-update-slice_fusion.2.refs_1_), channel_id=1, source_target_pairs={{0,8},{1,9},{2,10},{3,11},{4,12},{5,13},{6,14},{7,15},{8,0},{9,1},... | collective-permute-start | bytes 811016 | tf_op jit(solution)/shard_map/ppermute | solution.py:198
  36.0 6.4 %collective-permute-start.7 = (bf16[2,8,4224]{2,1,0:T(8,128)(2,1)}, bf16[2,8,4224]{2,1,0:T(8,128)(2,1)S(1)}, u32[]{:S(2)}, u32[]{:S(2)}) collective-permute-start(bf16[2,8,4224]{2,1,0:T(8,128)(2,1)} %collective-permute-done.4), channel_id=1, source_target_pairs={{0,16},{1,17},{2,18},{3,19},{4,20},{5,21},{6,22},{7,23},{8,120},{9... | collective-permute-start | bytes 405512 | tf_op jit(solution)/shard_map/ppermute | solution.py:198
  36.1 16.7 %collective-permute-start.3 = (bf16[4,8,4224]{2,1,0:T(8,128)(2,1)S(1)}, bf16[4,8,4224]{2,1,0:T(8,128)(2,1)}, u32[]{:S(2)}, u32[]{:S(2)}) collective-permute-start(bf16[4,8,4224]{2,1,0:T(8,128)(2,1)S(1)} %constant_dynamic-update-slice_fusion.refs_0_), channel_id=1, source_target_pairs={{0,128},{1,129},{2,130},{3,131},{4,132},{5,133},{6,134},{7,135},{8... | collective-permute-start | bytes 811016 | tf_op jit(solution)/shard_map/ppermute | solution.py:198
  39.2 13.6 %collective-permute-start.6 = (bf16[4,8,4224]{2,1,0:T(8,128)(2,1)S(1)}, bf16[4,8,4224]{2,1,0:T(8,128)(2,1)}, u32[]{:S(2)}, u32[]{:S(2)}) collective-permute-start(bf16[4,8,4224]{2,1,0:T(8,128)(2,1)S(1)} %constant_dynamic-update-slice_fusion.2.refs_1_), channel_id=1, source_target_pairs={{0,128},{1,129},{2,130},{3,131},{4,132},{5,133},{6,134},{7,135},{8... | collective-permute-start | bytes 811016 | tf_op jit(solution)/shard_map/ppermute | solution.py:198
  52.7 7.6 %collective-permute-start.11 = (bf16[4,8,4224]{2,1,0:T(8,128)(2,1)}, bf16[4,8,4224]{2,1,0:T(8,128)(2,1)S(1)}, u32[]{:S(2)}, u32[]{:S(2)}) collective-permute-start(bf16[4,8,4224]{2,1,0:T(8,128)(2,1)} %collective-permute-done.3.refs_0_), channel_id=1, source_target_pairs={{0,8},{1,9},{2,10},{3,11},{4,12},{5,13},{6,14},{7,15},{8,0},{9,1},... | collective-permute-start | bytes 811016 | tf_op jit(solution)/shard_map/ppermute | solution.py:198
  52.9 7.5 %collective-permute-start.12 = (bf16[4,8,4224]{2,1,0:T(8,128)(2,1)}, bf16[4,8,4224]{2,1,0:T(8,128)(2,1)S(1)}, u32[]{:S(2)}, u32[]{:S(2)}) collective-permute-start(bf16[4,8,4224]{2,1,0:T(8,128)(2,1)} %collective-permute-done.6.refs_1_), channel_id=1, source_target_pairs={{0,8},{1,9},{2,10},{3,11},{4,12},{5,13},{6,14},{7,15},{8,0},{9,1},... | collective-permute-start | bytes 811016 | tf_op jit(solution)/shard_map/ppermute | solution.py:198
  53.3 7.1 %collective-permute-start.10 = (bf16[2,8,4224]{2,1,0:T(8,128)(2,1)S(1)}, bf16[2,8,4224]{2,1,0:T(8,128)(2,1)S(1)}, u32[]{:S(2)}, u32[]{:S(2)}) collective-permute-start(bf16[2,8,4224]{2,1,0:T(8,128)(2,1)S(1)} %collective-permute-done.7.refs_2_), channel_id=1, source_target_pairs={{0,128},{1,129},{2,130},{3,131},{4,132},{5,133},{6,134},{7,135},{8... | collective-permute-start | bytes 405512 | tf_op jit(solution)/shard_map/ppermute | solution.py:198

commit v6 on v5

--- a/solution.py
+++ b/solution.py
@@ -142,7 +142,8 @@
 
 
 def copies_kernel(x_ref, out_ref, sem):
-    sends = [pltpu.make_async_copy(x_ref, out_ref.at[i], sem.at[i]) for i in range(8)]
+    source = x_ref.at[:, : GRID * GRID]
+    sends = [pltpu.make_async_copy(source, out_ref.at[i], sem.at[i]) for i in range(8)]
     for send in sends:
         send.start()
     for send in sends:
@@ -152,7 +153,7 @@
 def copies_of(x):
     return pl.pallas_call(
         copies_kernel,
-        out_shape=jax.ShapeDtypeStruct((8, *x.shape), x.dtype),
+        out_shape=jax.ShapeDtypeStruct((8, 8, GRID * GRID), x.dtype),
         in_specs=[pl.BlockSpec(memory_space=pltpu.VMEM)],
         out_specs=pl.BlockSpec(memory_space=pl.ANY),
         scratch_shapes=[pltpu.SemaphoreType.DMA((8,))],
@@ -217,7 +218,7 @@
 def exchange(mine, occupation):
     slice_out = jnp.concatenate([mine, jnp.broadcast_to(occupation, (8, 128))], axis=1)
     kept = moved(slice_out, lambda h, z, c, l: (h, l, c, z))
-    copies = copies_of(mine)
+    copies = copies_of(slice_out)
     row = lax.all_to_all(copies, "dist", split_axis=0, concat_axis=0, tiled=True)
     row = row.reshape(GRID, GRID * GRID)
     crossed = moved(kept, cores)
@@ -231,11 +232,11 @@
     hop = {}
     for k in (1, 3, 2):
         hop[k] = moved(pair, ring(k))
-    early = jnp.concatenate([pair, hop[1]])
+    held, first, left, right, green = lax.optimization_barrier((pair, hop[1], left, right, green))
+    early = jnp.concatenate([held, first])
     far_early = moved(early, halves)
     core_early = moved(early, cores)
-    hop[3], left, right, green = lax.optimization_barrier((hop[3], left, right, green))
-    fourth = moved(hop[3], ring(1))
+    fourth = moved(jnp.where(live, hop[3], 0), ring(1))
     late = jnp.concatenate([hop[3], hop[2]])
     core_late = moved(late, cores)
     far_late = moved(late, halves)

time: 81.9 us -> 80.6 us (0.984)
  local copies, waits for them, and re-layouts: 3.56 us -> 1.81 us
    unnamed x8 -> x5, local copies, waits for them, and re-layouts: 1.77 us -> 0.02 us
    concatenate x1, local copies, waits for them, and re-layouts: 0.02 us -> 0.92 us  [exchange(): early = jnp.concatenate([held, first])]
    concatenate x1, local copies, waits for them, and re-layouts: 0.92 us -> 0.02 us  [exchange(): late = jnp.concatenate([hop[3], hop[2]])]
  transfers between devices with their start and end apart: 14 -> 14, of which waited for: 5 -> 5; matrix products, arithmetic and copies ran while one was open for 3% -> 2% of each run, Pallas kernels for 8% -> 8%
where the time goes in v6:
time: 80.6 us; the launch traced here: 79.5 us
  starting transfers between devices  28.5 us (35%)
  waiting for transfers between devices  20.7 us (26%)
  blocking collectives  13.4 us (17%)
  Pallas kernels  12.3 us (15%)
  other arithmetic  1.88 us (2%)
  local copies, waits for them, and re-layouts  1.81 us (2%)
  between operations  0.85 us (1%)
    ppermute x13, waiting for transfers between devices, moved(): return lax.ppermute(x, AXES, pairs)  20.7 us
    ppermute x13, starting transfers between devices, moved(): return lax.ppermute(x, AXES, pairs)  19.3 us
    all_to_all x1, blocking collectives, exchange(): lax.all_to_all(sent, 'dist', split_axis=0, concat_axis=0, tiled=True)  13.4 us
    pallas_call x2, Pallas kernels, solve(): pl.pallas_call(functools.partial(solve_kernel, not more), out_shape=jax.S...  11.4 us
    all_to_all x1, starting transfers between devices, exchange(): lax.all_to_all(copies, 'dist', split_axis=0, concat_axis=0, tiled=True)  9.19 us
  transfers between devices with their start and end apart: 14, of which 5 were waited for; matrix products, arithmetic and copies ran while one was open for 2% of the time, Pallas kernels for 8%

profile of v6, /device:TPU:8, one launch (start us, length us, event | category | flops | bytes accessed | tf_op | source)
XLA Modules:
  0.0 79.5 jit_solution(5022669619792236976)
XLA Ops:
  0.7 0.8 %concatenate.39.x_ref = bf16[8,4224]{1,0:T(8,128)(2,1)S(1)} pad(bf16[8,4096]{1,0:T(8,128)(2,1)} %bitcast.15, bf16[]{:T(256)} %bitcast.10), padding=0_0x0_128 | pad | bytes 133122 | tf_op jit(solution)/shard_map/concatenate | solution.py:219
  1.5 5.2 %collective-permute-start = (bf16[8,4224]{1,0:T(8,128)(2,1)S(1)}, bf16[8,4224]{1,0:T(8,128)(2,1)S(1)}, u32[]{:S(2)}, u32[]{:S(2)}) collective-permute-start(bf16[8,4224]{1,0:T(8,128)(2,1)S(1)} %concatenate.39.x_ref), channel_id=1, source_target_pairs={{0,0},{1,16},{2,32},{3,48},{4,64},{5,80},{6,96},{7,112},{8,8},{9,2... | collective-permute-start | bytes 202760 | tf_op jit(solution)/shard_map/ppermute | solution.py:199
  6.7 0.9 %copies.1 = bf16[8,8,4096]{2,1,0:T(8,128)(2,1)} custom-call(bf16[8,4224]{1,0:T(8,128)(2,1)S(1)} %concatenate.39.x_ref), custom_call_target="tpu_custom_call" | custom-call | tf_op jit(solution)/shard_map/copies/pallas_call | solution.py:154
  7.6 9.2 %all-to-all-start = ((bf16[8,8,4096]{2,1,0:T(8,128)(2,1)}), bf16[8,8,4096]{2,1,0:T(8,128)(2,1)S(1)}, u32[]{:S(2)}, u32[]{:S(2)}) async-start(bf16[8,8,4096]{2,1,0:T(8,128)(2,1)} %copies.1), calls=%async_computation | async-start | bytes 1048576 | tf_op jit(solution)/shard_map/all_to_all | solution.py:222
  17.1 1.2 %collective-permute-done.1 = bf16[8,4224]{1,0:T(8,128)(2,1)S(1)} collective-permute-done((bf16[8,4224]{1,0:T(8,128)(2,1)S(1)}, bf16[8,4224]{1,0:T(8,128)(2,1)S(1)}, u32[]{:S(2)}, u32[]{:S(2)}) %collective-permute-start.1) | collective-permute-done | bytes 67616 | tf_op jit(solution)/shard_map/ppermute | solution.py:199
  18.3 2.3 %collective-permute-start.5 = (bf16[2,8,4224]{2,1,0:T(8,128)(2,1)S(1)}, bf16[2,8,4224]{2,1,0:T(8,128)(2,1)S(1)}, u32[]{:S(2)}, u32[]{:S(2)}) collective-permute-start(bf16[2,8,4224]{2,1,0:T(8,128)(2,1)S(1)} %pad_maximum_fusion), channel_id=1, source_target_pairs={{0,32},{1,33},{2,34},{3,35},{4,36},{5,37},{6,38},{7,39},{8,104},{9... | collective-permute-start | bytes 405512 | tf_op jit(solution)/shard_map/ppermute | solution.py:199
  20.5 2.2 %collective-permute-start.4 = (bf16[2,8,4224]{2,1,0:T(8,128)(2,1)S(1)}, bf16[2,8,4224]{2,1,0:T(8,128)(2,1)S(1)}, u32[]{:S(2)}, u32[]{:S(2)}) collective-permute-start(bf16[2,8,4224]{2,1,0:T(8,128)(2,1)S(1)} %pad_maximum_fusion), channel_id=1, source_target_pairs={{0,48},{1,49},{2,50},{3,51},{4,52},{5,53},{6,54},{7,55},{8,88},{9,... | collective-permute-start | bytes 405512 | tf_op jit(solution)/shard_map/ppermute | solution.py:199
  22.8 2.1 %collective-permute-start.2 = (bf16[2,8,4224]{2,1,0:T(8,128)(2,1)S(1)}, bf16[2,8,4224]{2,1,0:T(8,128)(2,1)}, u32[]{:S(2)}, u32[]{:S(2)}) collective-permute-start(bf16[2,8,4224]{2,1,0:T(8,128)(2,1)S(1)} %pad_maximum_fusion), channel_id=1, source_target_pairs={{0,16},{1,17},{2,18},{3,19},{4,20},{5,21},{6,22},{7,23},{8,120},{9... | collective-permute-start | bytes 405512 | tf_op jit(solution)/shard_map/ppermute | solution.py:199
  24.8 0.6 fusion.1.refs_7_
  25.5 7.8 %collective-permute-done.4 = bf16[2,8,4224]{2,1,0:T(8,128)(2,1)S(1)} collective-permute-done((bf16[2,8,4224]{2,1,0:T(8,128)(2,1)S(1)}, bf16[2,8,4224]{2,1,0:T(8,128)(2,1)S(1)}, u32[]{:S(2)}, u32[]{:S(2)}) %collective-permute-start.4) | collective-permute-done | bytes 135200 | tf_op jit(solution)/shard_map/ppermute | solution.py:199
  33.3 0.1 collective-permute-start.9
  33.4 0.9 %constant_dynamic-update-slice_fusion.refs_0_ = bf16[4,8,4224]{2,1,0:T(8,128)(2,1)S(1)} fusion(bf16[4,8,4224]{2,1,0:T(8,128)(2,1)S(1)} %constant_dynamic-update-slice_fusion.1, bf16[2,8,4224]{2,1,0:T(8,128)(2,1)} %collective-permute-done.2), kind=kLoop, calls=%fused_computation.11 | loop fusion | bytes 270336 | tf_op jit(solution)/shard_map/concatenate | solution.py:236
  34.4 0.6 collective-permute-start.8
  34.9 3.0 %collective-permute-start.6 = (bf16[4,8,4224]{2,1,0:T(8,128)(2,1)S(1)}, bf16[4,8,4224]{2,1,0:T(8,128)(2,1)}, u32[]{:S(2)}, u32[]{:S(2)}) collective-permute-start(bf16[4,8,4224]{2,1,0:T(8,128)(2,1)S(1)} %constant_dynamic-update-slice_fusion.2.refs_1_), channel_id=1, source_target_pairs={{0,128},{1,129},{2,130},{3,131},{4,132},{5,133},{6,134},{7,135},{8... | collective-permute-start | bytes 811016 | tf_op jit(solution)/shard_map/ppermute | solution.py:199
  37.9 0.6 collective-permute-start.3
  38.5 2.7 %collective-permute-done.7.refs_2_ = bf16[2,8,4224]{2,1,0:T(8,128)(2,1)S(1)} collective-permute-done((bf16[2,8,4224]{2,1,0:T(8,128)(2,1)S(1)}, bf16[2,8,4224]{2,1,0:T(8,128)(2,1)S(1)}, u32[]{:S(2)}, u32[]{:S(2)}) %collective-permute-start.7) | collective-permute-done | bytes 135200 | tf_op jit(solution)/shard_map/ppermute | solution.py:199
  41.2 5.5 %solve.2.refs_8_ = f32[64,4096]{1,0:T(8,128)S(1)} custom-call(s32[1]{0:T(128)} %bitcast.4.seat_ref, bf16[64,4096]{1,0:T(8,128)(2,1)S(1)} %bitcast.11, bf16[4,8,4224]{2,1,0:T(8,128)(2,1)S(1)} %constant_dynamic-update-slice_fusion.refs_0_, bf16[4,8,4224]{2,1,0:T(8,128)(2,1)S(1)} %constant_dynamic-update-slice_fusion.2.refs_1_, ...), custom_call_target="tpu_custom_call" | custom-call | flops 10000000000 | bytes 10000000 | tf_op jit(solution)/shard_map/solve/pallas_call | solution.py:169
  46.8 4.8 %collective-permute-done.3.refs_0_ = bf16[4,8,4224]{2,1,0:T(8,128)(2,1)} collective-permute-done((bf16[4,8,4224]{2,1,0:T(8,128)(2,1)S(1)}, bf16[4,8,4224]{2,1,0:T(8,128)(2,1)}, u32[]{:S(2)}, u32[]{:S(2)}) %collective-permute-start.3) | collective-permute-done | bytes 270368 | tf_op jit(solution)/shard_map/ppermute | solution.py:199
  51.6 3.2 %collective-permute-start.10 = (bf16[2,8,4224]{2,1,0:T(8,128)(2,1)S(1)}, bf16[2,8,4224]{2,1,0:T(8,128)(2,1)S(1)}, u32[]{:S(2)}, u32[]{:S(2)}) collective-permute-start(bf16[2,8,4224]{2,1,0:T(8,128)(2,1)S(1)} %collective-permute-done.7.refs_2_), channel_id=1, source_target_pairs={{0,128},{1,129},{2,130},{3,131},{4,132},{5,133},{6,134},{7,135},{8... | collective-permute-start | bytes 405512 | tf_op jit(solution)/shard_map/ppermute | solution.py:199
  54.8 4.3 %collective-permute-done.10.refs_2_ = bf16[2,8,4224]{2,1,0:T(8,128)(2,1)S(1)} collective-permute-done((bf16[2,8,4224]{2,1,0:T(8,128)(2,1)S(1)}, bf16[2,8,4224]{2,1,0:T(8,128)(2,1)S(1)}, u32[]{:S(2)}, u32[]{:S(2)}) %collective-permute-start.10) | collective-permute-done | bytes 135200 | tf_op jit(solution)/shard_map/ppermute | solution.py:199
  59.1 5.9 %solve.3 = f32[64,4224]{1,0:T(8,128)S(1)} custom-call(s32[1]{0:T(128)} %bitcast.4.seat_ref, bf16[64,4096]{1,0:T(8,128)(2,1)S(1)} %bitcast.12, bf16[4,8,4224]{2,1,0:T(8,128)(2,1)} %collective-permute-done.3.refs_0_, bf16[4,8,4224]{2,1,0:T(8,128)(2,1)} %collective-permute-done.6.refs_1_, bf16[2,8,4224]{2,1,0:T(8,128)(2,1)S(1)} %collective-permute-done.10.refs_2_, ...), custom_call_target="tpu_custom_call" | custom-call | flops 10000000000 | bytes 10000000 | tf_op jit(solution)/shard_map/solve/pallas_call | solution.py:169
  65.1 13.4 %all_to_all.10 = f16[8,8,4224]{2,1,0:T(8,128)(2,1)S(1)} all-to-all(f16[8,8,4224]{2,1,0:T(8,128)(2,1)S(1)} %convert_bitcast_fusion), channel_id=1, replica_groups=mesh['grp'=32,'dist'=8] {'dist'}, dimensions={0} | all-to-all | bytes 1081344 | tf_op jit(solution)/shard_map/all_to_all | solution.py:252
  78.5 0.2 exponential_reduce_fusion
  78.7 0.8 %multiply_reduce_fusion = f32[8,4096]{1,0:T(8,128)} fusion(f16[8,8,4224]{2,1,0:T(8,128)(2,1)S(1)} %all_to_all.10, f32[8]{0:T(128)S(1)} %exponential_reduce_fusion), kind=kLoop, calls=%fused_computation.4 | loop fusion | flops 753664 | bytes 655392 | tf_op jit(solution)/shard_map/reduce_sum | solution.py:255
  (28 shorter events, 0.5 us)
Async XLA Ops:
  0.0 24.8 %copy-start = (bf16[256,256]{1,0:T(8,128)(2,1)S(1)}, bf16[256,256]{1,0:T(8,128)(2,1)}, u32[]{:S(2)}) copy-start(bf16[256,256]{1,0:T(8,128)(2,1)} %constant.50) | copy-start | bytes 393220
  1.5 23.9 %copy-start.1 = (bf16[64,192]{1,0:T(8,128)(2,1)S(1)}, bf16[64,192]{1,0:T(8,128)(2,1)}, u32[]{:S(2)}) copy-start(bf16[64,192]{1,0:T(8,128)(2,1)} %constant.42) | copy-start | bytes 73732
  1.5 15.4 %collective-permute-start = (bf16[8,4224]{1,0:T(8,128)(2,1)S(1)}, bf16[8,4224]{1,0:T(8,128)(2,1)S(1)}, u32[]{:S(2)}, u32[]{:S(2)}) collective-permute-start(bf16[8,4224]{1,0:T(8,128)(2,1)S(1)} %concatenate.39.x_ref), channel_id=1, source_target_pairs={{0,0},{1,16},{2,32},{3,48},{4,64},{5,80},{6,96},{7,112},{8,8},{9,2... | collective-permute-start | bytes 202760 | tf_op jit(solution)/shard_map/ppermute | solution.py:199
  7.6 33.5 %all-to-all-start = ((bf16[8,8,4096]{2,1,0:T(8,128)(2,1)}), bf16[8,8,4096]{2,1,0:T(8,128)(2,1)S(1)}, u32[]{:S(2)}, u32[]{:S(2)}) async-start(bf16[8,8,4096]{2,1,0:T(8,128)(2,1)} %copies.1), calls=%async_computation | async-start | bytes 1048576 | tf_op jit(solution)/shard_map/all_to_all | solution.py:222
  16.9 1.3 %collective-permute-start.1 = (bf16[8,4224]{1,0:T(8,128)(2,1)S(1)}, bf16[8,4224]{1,0:T(8,128)(2,1)S(1)}, u32[]{:S(2)}, u32[]{:S(2)}) collective-permute-start(bf16[8,4224]{1,0:T(8,128)(2,1)S(1)} %collective-permute-done), channel_id=1, source_target_pairs={{0,8},{1,9},{2,10},{3,11},{4,12},{5,13},{6,14},{7,15},{8,0},{9,1},... | collective-permute-start | bytes 202760 | tf_op jit(solution)/shard_map/ppermute | solution.py:199
  18.3 15.0 %collective-permute-start.5 = (bf16[2,8,4224]{2,1,0:T(8,128)(2,1)S(1)}, bf16[2,8,4224]{2,1,0:T(8,128)(2,1)S(1)}, u32[]{:S(2)}, u32[]{:S(2)}) collective-permute-start(bf16[2,8,4224]{2,1,0:T(8,128)(2,1)S(1)} %pad_maximum_fusion), channel_id=1, source_target_pairs={{0,32},{1,33},{2,34},{3,35},{4,36},{5,37},{6,38},{7,39},{8,104},{9... | collective-permute-start | bytes 405512 | tf_op jit(solution)/shard_map/ppermute | solution.py:199
  20.5 12.7 %collective-permute-start.4 = (bf16[2,8,4224]{2,1,0:T(8,128)(2,1)S(1)}, bf16[2,8,4224]{2,1,0:T(8,128)(2,1)S(1)}, u32[]{:S(2)}, u32[]{:S(2)}) collective-permute-start(bf16[2,8,4224]{2,1,0:T(8,128)(2,1)S(1)} %pad_maximum_fusion), channel_id=1, source_target_pairs={{0,48},{1,49},{2,50},{3,51},{4,52},{5,53},{6,54},{7,55},{8,88},{9,... | collective-permute-start | bytes 405512 | tf_op jit(solution)/shard_map/ppermute | solution.py:199
  22.8 10.6 %collective-permute-start.2 = (bf16[2,8,4224]{2,1,0:T(8,128)(2,1)S(1)}, bf16[2,8,4224]{2,1,0:T(8,128)(2,1)}, u32[]{:S(2)}, u32[]{:S(2)}) collective-permute-start(bf16[2,8,4224]{2,1,0:T(8,128)(2,1)S(1)} %pad_maximum_fusion), channel_id=1, source_target_pairs={{0,16},{1,17},{2,18},{3,19},{4,20},{5,21},{6,22},{7,23},{8,120},{9... | collective-permute-start | bytes 405512 | tf_op jit(solution)/shard_map/ppermute | solution.py:199
  33.3 7.9 %collective-permute-start.9 = (bf16[4,8,4224]{2,1,0:T(8,128)(2,1)S(1)}, bf16[4,8,4224]{2,1,0:T(8,128)(2,1)}, u32[]{:S(2)}, u32[]{:S(2)}) collective-permute-start(bf16[4,8,4224]{2,1,0:T(8,128)(2,1)S(1)} %constant_dynamic-update-slice_fusion.2.refs_1_), channel_id=1, source_target_pairs={{0,8},{1,9},{2,10},{3,11},{4,12},{5,13},{6,14},{7,15},{8,0},{9,1},... | collective-permute-start | bytes 811016 | tf_op jit(solution)/shard_map/ppermute | solution.py:199
  34.4 6.8 %collective-permute-start.8 = (bf16[4,8,4224]{2,1,0:T(8,128)(2,1)S(1)}, bf16[4,8,4224]{2,1,0:T(8,128)(2,1)}, u32[]{:S(2)}, u32[]{:S(2)}) collective-permute-start(bf16[4,8,4224]{2,1,0:T(8,128)(2,1)S(1)} %constant_dynamic-update-slice_fusion.refs_0_), channel_id=1, source_target_pairs={{0,8},{1,9},{2,10},{3,11},{4,12},{5,13},{6,14},{7,15},{8,0},{9,1},... | collective-permute-start | bytes 811016 | tf_op jit(solution)/shard_map/ppermute | solution.py:199
  34.9 6.2 %collective-permute-start.7 = (bf16[2,8,4224]{2,1,0:T(8,128)(2,1)S(1)}, bf16[2,8,4224]{2,1,0:T(8,128)(2,1)S(1)}, u32[]{:S(2)}, u32[]{:S(2)}) collective-permute-start(bf16[2,8,4224]{2,1,0:T(8,128)(2,1)S(1)} %get-tuple-element.23), channel_id=1, source_target_pairs={{0,16},{1,17},{2,18},{3,19},{4,20},{5,21},{6,22},{7,23},{8,120},{9... | collective-permute-start | bytes 405512 | tf_op jit(solution)/shard_map/ppermute | solution.py:199
  34.9 11.7 %collective-permute-start.6 = (bf16[4,8,4224]{2,1,0:T(8,128)(2,1)S(1)}, bf16[4,8,4224]{2,1,0:T(8,128)(2,1)}, u32[]{:S(2)}, u32[]{:S(2)}) collective-permute-start(bf16[4,8,4224]{2,1,0:T(8,128)(2,1)S(1)} %constant_dynamic-update-slice_fusion.2.refs_1_), channel_id=1, source_target_pairs={{0,128},{1,129},{2,130},{3,131},{4,132},{5,133},{6,134},{7,135},{8... | collective-permute-start | bytes 811016 | tf_op jit(solution)/shard_map/ppermute | solution.py:199
  37.9 13.7 %collective-permute-start.3 = (bf16[4,8,4224]{2,1,0:T(8,128)(2,1)S(1)}, bf16[4,8,4224]{2,1,0:T(8,128)(2,1)}, u32[]{:S(2)}, u32[]{:S(2)}) collective-permute-start(bf16[4,8,4224]{2,1,0:T(8,128)(2,1)S(1)} %constant_dynamic-update-slice_fusion.refs_0_), channel_id=1, source_target_pairs={{0,128},{1,129},{2,130},{3,131},{4,132},{5,133},{6,134},{7,135},{8... | collective-permute-start | bytes 811016 | tf_op jit(solution)/shard_map/ppermute | solution.py:199
  46.7 12.4 %collective-permute-start.12 = (bf16[4,8,4224]{2,1,0:T(8,128)(2,1)}, bf16[4,8,4224]{2,1,0:T(8,128)(2,1)S(1)}, u32[]{:S(2)}, u32[]{:S(2)}) collective-permute-start(bf16[4,8,4224]{2,1,0:T(8,128)(2,1)} %collective-permute-done.6.refs_1_), channel_id=1, source_target_pairs={{0,8},{1,9},{2,10},{3,11},{4,12},{5,13},{6,14},{7,15},{8,0},{9,1},... | collective-permute-start | bytes 811016 | tf_op jit(solution)/shard_map/ppermute | solution.py:199
  51.6 7.5 %collective-permute-start.11 = (bf16[4,8,4224]{2,1,0:T(8,128)(2,1)}, bf16[4,8,4224]{2,1,0:T(8,128)(2,1)S(1)}, u32[]{:S(2)}, u32[]{:S(2)}) collective-permute-start(bf16[4,8,4224]{2,1,0:T(8,128)(2,1)} %collective-permute-done.3.refs_0_), channel_id=1, source_target_pairs={{0,8},{1,9},{2,10},{3,11},{4,12},{5,13},{6,14},{7,15},{8,0},{9,1},... | collective-permute-start | bytes 811016 | tf_op jit(solution)/shard_map/ppermute | solution.py:199
  51.6 7.5 %collective-permute-start.10 = (bf16[2,8,4224]{2,1,0:T(8,128)(2,1)S(1)}, bf16[2,8,4224]{2,1,0:T(8,128)(2,1)S(1)}, u32[]{:S(2)}, u32[]{:S(2)}) collective-permute-start(bf16[2,8,4224]{2,1,0:T(8,128)(2,1)S(1)} %collective-permute-done.7.refs_2_), channel_id=1, source_target_pairs={{0,128},{1,129},{2,130},{3,131},{4,132},{5,133},{6,134},{7,135},{8... | collective-permute-start | bytes 405512 | tf_op jit(solution)/shard_map/ppermute | solution.py:199

commit v7 on v6

--- a/solution.py
+++ b/solution.py
@@ -79,9 +79,9 @@
     sides = ((core, early_ref, late_ref), (1 - core, other_early_ref, other_late_ref))
     for holder, early, late in sides:
         sign = jnp.where(holder == 0, -1, 1)
-        place(early, 2, holder, z + sign)
-        place(late, 0, holder, z + 3 * sign)
-        place(late, 2, holder, z + 2 * sign)
+        place(early, 2, holder, z + 3 * sign)
+        place(late, 0, holder, z + 2 * sign)
+        place(late, 2, holder, z + sign)
 
     left = left_ref[...]
     right = right_ref[...]
@@ -230,14 +230,14 @@
     right = jnp.where(live, right, 0)
     green = green_table(live)
     hop = {}
-    for k in (1, 3, 2):
+    for k in (3, 2, 1):
         hop[k] = moved(pair, ring(k))
-    held, first, left, right, green = lax.optimization_barrier((pair, hop[1], left, right, green))
-    early = jnp.concatenate([held, first])
+    fourth = moved(jnp.where(live, hop[3], 0), ring(1))
+    held, third, left, right, green = lax.optimization_barrier((pair, hop[3], left, right, green))
+    early = jnp.concatenate([held, third])
     far_early = moved(early, halves)
     core_early = moved(early, cores)
-    fourth = moved(jnp.where(live, hop[3], 0), ring(1))
-    late = jnp.concatenate([hop[3], hop[2]])
+    late = jnp.concatenate([hop[2], hop[1]])
     core_late = moved(late, cores)
     far_late = moved(late, halves)
     far_fourth = moved(fourth, halves)

time: 80.6 us -> 81.5 us (1.011)
  starting transfers between devices: 28.5 us -> 31.8 us
  waiting for transfers between devices: 20.7 us -> 18 us
  other arithmetic: 1.88 us -> 2.78 us
    ppermute x13, starting transfers between devices: 19.3 us -> 22.7 us  [moved(): return lax.ppermute(x, AXES, pairs)]
    ppermute x13, waiting for transfers between devices: 20.7 us -> 18 us  [moved(): return lax.ppermute(x, AXES, pairs)]
    select_n x1, other arithmetic: 0.03 us -> 0.93 us  [exchange(): fourth = moved(jnp.where(live, hop[3], 0), ring(1))]
  transfers between devices with their start and end apart: 14 -> 14, of which waited for: 5 -> 7; matrix products, arithmetic and copies ran while one was open for 2% -> 3% of each run, Pallas kernels for 8% -> 8%
where the time goes in v7:
time: 81.5 us; the launch traced here: 80.2 us
  starting transfers between devices  31.8 us (39%)
  waiting for transfers between devices  18 us (22%)
  blocking collectives  12.7 us (16%)
  Pallas kernels  12.3 us (15%)
  other arithmetic  2.78 us (3%)
  local copies, waits for them, and re-layouts  1.82 us (2%)
  between operations  0.83 us (1%)
    ppermute x13, starting transfers between devices, moved(): return lax.ppermute(x, AXES, pairs)  22.7 us
    ppermute x13, waiting for transfers between devices, moved(): return lax.ppermute(x, AXES, pairs)  18 us
    all_to_all x1, blocking collectives, exchange(): lax.all_to_all(sent, 'dist', split_axis=0, concat_axis=0, tiled=True)  12.7 us
    pallas_call x2, Pallas kernels, solve(): pl.pallas_call(functools.partial(solve_kernel, not more), out_shape=jax.S...  11.4 us
    all_to_all x1, starting transfers between devices, exchange(): lax.all_to_all(copies, 'dist', split_axis=0, concat_axis=0, tiled=True)  9.19 us
  transfers between devices with their start and end apart: 14, of which 7 were waited for; matrix products, arithmetic and copies ran while one was open for 3% of the time, Pallas kernels for 8%

profile of v7, /device:TPU:8, one launch (start us, length us, event | category | flops | bytes accessed | tf_op | source)
XLA Modules:
  0.0 80.2 jit_solution(9306805230062906829)
XLA Ops:
  0.7 0.8 %concatenate.39.x_ref = bf16[8,4224]{1,0:T(8,128)(2,1)S(1)} pad(bf16[8,4096]{1,0:T(8,128)(2,1)} %bitcast.15, bf16[]{:T(256)} %bitcast.10), padding=0_0x0_128 | pad | bytes 133122 | tf_op jit(solution)/shard_map/concatenate | solution.py:219
  1.5 5.2 %collective-permute-start = (bf16[8,4224]{1,0:T(8,128)(2,1)S(1)}, bf16[8,4224]{1,0:T(8,128)(2,1)S(1)}, u32[]{:S(2)}, u32[]{:S(2)}) collective-permute-start(bf16[8,4224]{1,0:T(8,128)(2,1)S(1)} %concatenate.39.x_ref), channel_id=1, source_target_pairs={{0,0},{1,16},{2,32},{3,48},{4,64},{5,80},{6,96},{7,112},{8,8},{9,2... | collective-permute-start | bytes 202760 | tf_op jit(solution)/shard_map/ppermute | solution.py:199
  6.7 0.9 %copies.1 = bf16[8,8,4096]{2,1,0:T(8,128)(2,1)} custom-call(bf16[8,4224]{1,0:T(8,128)(2,1)S(1)} %concatenate.39.x_ref), custom_call_target="tpu_custom_call" | custom-call | tf_op jit(solution)/shard_map/copies/pallas_call | solution.py:154
  7.6 9.2 %all-to-all-start = ((bf16[8,8,4096]{2,1,0:T(8,128)(2,1)}), bf16[8,8,4096]{2,1,0:T(8,128)(2,1)S(1)}, u32[]{:S(2)}, u32[]{:S(2)}) async-start(bf16[8,8,4096]{2,1,0:T(8,128)(2,1)} %copies.1), calls=%async_computation | async-start | bytes 1048576 | tf_op jit(solution)/shard_map/all_to_all | solution.py:222
  17.1 1.2 %collective-permute-done.1 = bf16[8,4224]{1,0:T(8,128)(2,1)S(1)} collective-permute-done((bf16[8,4224]{1,0:T(8,128)(2,1)S(1)}, bf16[8,4224]{1,0:T(8,128)(2,1)S(1)}, u32[]{:S(2)}, u32[]{:S(2)}) %collective-permute-start.1) | collective-permute-done | bytes 67616 | tf_op jit(solution)/shard_map/ppermute | solution.py:199
  18.2 1.6 %collective-permute-start.5 = (bf16[2,8,4224]{2,1,0:T(8,128)(2,1)S(1)}, bf16[2,8,4224]{2,1,0:T(8,128)(2,1)S(1)}, u32[]{:S(2)}, u32[]{:S(2)}) collective-permute-start(bf16[2,8,4224]{2,1,0:T(8,128)(2,1)S(1)} %pad_maximum_fusion), channel_id=1, source_target_pairs={{0,16},{1,17},{2,18},{3,19},{4,20},{5,21},{6,22},{7,23},{8,120},{9... | collective-permute-start | bytes 405512 | tf_op jit(solution)/shard_map/ppermute | solution.py:199
  19.8 2.2 %collective-permute-start.4 = (bf16[2,8,4224]{2,1,0:T(8,128)(2,1)S(1)}, bf16[2,8,4224]{2,1,0:T(8,128)(2,1)S(1)}, u32[]{:S(2)}, u32[]{:S(2)}) collective-permute-start(bf16[2,8,4224]{2,1,0:T(8,128)(2,1)S(1)} %pad_maximum_fusion), channel_id=1, source_target_pairs={{0,32},{1,33},{2,34},{3,35},{4,36},{5,37},{6,38},{7,39},{8,104},{9... | collective-permute-start | bytes 405512 | tf_op jit(solution)/shard_map/ppermute | solution.py:199
  22.0 2.8 %collective-permute-start.2 = (bf16[2,8,4224]{2,1,0:T(8,128)(2,1)S(1)}, bf16[2,8,4224]{2,1,0:T(8,128)(2,1)}, u32[]{:S(2)}, u32[]{:S(2)}) collective-permute-start(bf16[2,8,4224]{2,1,0:T(8,128)(2,1)S(1)} %pad_maximum_fusion), channel_id=1, source_target_pairs={{0,48},{1,49},{2,50},{3,51},{4,52},{5,53},{6,54},{7,55},{8,88},{9,... | collective-permute-start | bytes 405512 | tf_op jit(solution)/shard_map/ppermute | solution.py:199
  24.8 0.6 fusion.1.refs_7_
  25.5 6.1 %collective-permute-done.4 = bf16[2,8,4224]{2,1,0:T(8,128)(2,1)S(1)} collective-permute-done((bf16[2,8,4224]{2,1,0:T(8,128)(2,1)S(1)}, bf16[2,8,4224]{2,1,0:T(8,128)(2,1)S(1)}, u32[]{:S(2)}, u32[]{:S(2)}) %collective-permute-start.4) | collective-permute-done | bytes 135200 | tf_op jit(solution)/shard_map/ppermute | solution.py:199
  32.3 0.9 %constant_dynamic-update-slice_fusion.refs_0_ = bf16[4,8,4224]{2,1,0:T(8,128)(2,1)S(1)} fusion(bf16[4,8,4224]{2,1,0:T(8,128)(2,1)S(1)} %constant_dynamic-update-slice_fusion.1, bf16[2,8,4224]{2,1,0:T(8,128)(2,1)} %collective-permute-done.2), kind=kLoop, calls=%fused_computation.11 | loop fusion | bytes 270336 | tf_op jit(solution)/shard_map/concatenate | solution.py:237
  33.3 0.9 %broadcast_select_fusion = bf16[2,8,4224]{2,1,0:T(8,128)(2,1)S(1)} fusion(bf16[2,8,4224]{2,1,0:T(8,128)(2,1)} %collective-permute-done.2, pred[]{:T(512)} %bitcast.6), kind=kLoop, calls=%fused_computation.7 | loop fusion | flops 67584 | bytes 270337 | tf_op jit(solution)/shard_map/jit(_where)/select_n | solution.py:235
  34.2 2.4 %collective-permute-start.7 = (bf16[2,8,4224]{2,1,0:T(8,128)(2,1)S(1)}, bf16[2,8,4224]{2,1,0:T(8,128)(2,1)S(1)}, u32[]{:S(2)}, u32[]{:S(2)}) collective-permute-start(bf16[2,8,4224]{2,1,0:T(8,128)(2,1)S(1)} %broadcast_select_fusion), channel_id=1, source_target_pairs={{0,16},{1,17},{2,18},{3,19},{4,20},{5,21},{6,22},{7,23},{8,120},{9... | collective-permute-start | bytes 405512 | tf_op jit(solution)/shard_map/ppermute | solution.py:199
  36.7 3.1 %collective-permute-start.6 = (bf16[4,8,4224]{2,1,0:T(8,128)(2,1)S(1)}, bf16[4,8,4224]{2,1,0:T(8,128)(2,1)}, u32[]{:S(2)}, u32[]{:S(2)}) collective-permute-start(bf16[4,8,4224]{2,1,0:T(8,128)(2,1)S(1)} %constant_dynamic-update-slice_fusion.2.refs_1_), channel_id=1, source_target_pairs={{0,128},{1,129},{2,130},{3,131},{4,132},{5,133},{6,134},{7,135},{8... | collective-permute-start | bytes 811016 | tf_op jit(solution)/shard_map/ppermute | solution.py:199
  40.2 0.8 collective-permute-done.7.refs_2_
  40.9 5.5 %solve.2.refs_8_ = f32[64,4096]{1,0:T(8,128)S(1)} custom-call(s32[1]{0:T(128)} %bitcast.4.seat_ref, bf16[64,4096]{1,0:T(8,128)(2,1)S(1)} %bitcast.11, bf16[4,8,4224]{2,1,0:T(8,128)(2,1)S(1)} %constant_dynamic-update-slice_fusion.refs_0_, bf16[4,8,4224]{2,1,0:T(8,128)(2,1)S(1)} %constant_dynamic-update-slice_fusion.2.refs_1_, ...), custom_call_target="tpu_custom_call" | custom-call | flops 10000000000 | bytes 10000000 | tf_op jit(solution)/shard_map/solve/pallas_call | solution.py:169
  46.5 0.6 collective-permute-done.6.refs_1_
  47.1 1.2 %collective-permute-start.12 = (bf16[4,8,4224]{2,1,0:T(8,128)(2,1)}, bf16[4,8,4224]{2,1,0:T(8,128)(2,1)S(1)}, u32[]{:S(2)}, u32[]{:S(2)}) collective-permute-start(bf16[4,8,4224]{2,1,0:T(8,128)(2,1)} %collective-permute-done.6.refs_1_), channel_id=1, source_target_pairs={{0,8},{1,9},{2,10},{3,11},{4,12},{5,13},{6,14},{7,15},{8,0},{9,1},... | collective-permute-start | bytes 811016 | tf_op jit(solution)/shard_map/ppermute | solution.py:199
  48.3 4.6 %collective-permute-done.3.refs_0_ = bf16[4,8,4224]{2,1,0:T(8,128)(2,1)} collective-permute-done((bf16[4,8,4224]{2,1,0:T(8,128)(2,1)S(1)}, bf16[4,8,4224]{2,1,0:T(8,128)(2,1)}, u32[]{:S(2)}, u32[]{:S(2)}) %collective-permute-start.3) | collective-permute-done | bytes 270368 | tf_op jit(solution)/shard_map/ppermute | solution.py:199
  53.2 3.2 %collective-permute-start.10 = (bf16[2,8,4224]{2,1,0:T(8,128)(2,1)S(1)}, bf16[2,8,4224]{2,1,0:T(8,128)(2,1)S(1)}, u32[]{:S(2)}, u32[]{:S(2)}) collective-permute-start(bf16[2,8,4224]{2,1,0:T(8,128)(2,1)S(1)} %collective-permute-done.7.refs_2_), channel_id=1, source_target_pairs={{0,128},{1,129},{2,130},{3,131},{4,132},{5,133},{6,134},{7,135},{8... | collective-permute-start | bytes 405512 | tf_op jit(solution)/shard_map/ppermute | solution.py:199
  56.4 4.1 %collective-permute-done.10.refs_2_ = bf16[2,8,4224]{2,1,0:T(8,128)(2,1)S(1)} collective-permute-done((bf16[2,8,4224]{2,1,0:T(8,128)(2,1)S(1)}, bf16[2,8,4224]{2,1,0:T(8,128)(2,1)S(1)}, u32[]{:S(2)}, u32[]{:S(2)}) %collective-permute-start.10) | collective-permute-done | bytes 135200 | tf_op jit(solution)/shard_map/ppermute | solution.py:199
  60.5 5.9 %solve.3 = f32[64,4224]{1,0:T(8,128)S(1)} custom-call(s32[1]{0:T(128)} %bitcast.4.seat_ref, bf16[64,4096]{1,0:T(8,128)(2,1)S(1)} %bitcast.12, bf16[4,8,4224]{2,1,0:T(8,128)(2,1)} %collective-permute-done.3.refs_0_, bf16[4,8,4224]{2,1,0:T(8,128)(2,1)} %collective-permute-done.6.refs_1_, bf16[2,8,4224]{2,1,0:T(8,128)(2,1)S(1)} %collective-permute-done.10.refs_2_, ...), custom_call_target="tpu_custom_call" | custom-call | flops 10000000000 | bytes 10000000 | tf_op jit(solution)/shard_map/solve/pallas_call | solution.py:169
  66.5 12.7 %all_to_all.10 = f16[8,8,4224]{2,1,0:T(8,128)(2,1)S(1)} all-to-all(f16[8,8,4224]{2,1,0:T(8,128)(2,1)S(1)} %convert_bitcast_fusion), channel_id=1, replica_groups=mesh['grp'=32,'dist'=8] {'dist'}, dimensions={0} | all-to-all | bytes 1081344 | tf_op jit(solution)/shard_map/all_to_all | solution.py:252
  79.3 0.8 %multiply_reduce_fusion = f32[8,4096]{1,0:T(8,128)} fusion(f16[8,8,4224]{2,1,0:T(8,128)(2,1)S(1)} %all_to_all.10, f32[8]{0:T(128)S(1)} %exponential_reduce_fusion), kind=kLoop, calls=%fused_computation.4 | loop fusion | flops 753664 | bytes 655392 | tf_op jit(solution)/shard_map/reduce_sum | solution.py:255
  (29 shorter events, 2.1 us)
Async XLA Ops:
  0.0 24.8 %copy-start = (bf16[256,256]{1,0:T(8,128)(2,1)S(1)}, bf16[256,256]{1,0:T(8,128)(2,1)}, u32[]{:S(2)}) copy-start(bf16[256,256]{1,0:T(8,128)(2,1)} %constant.50) | copy-start | bytes 393220
  1.5 23.9 %copy-start.1 = (bf16[64,192]{1,0:T(8,128)(2,1)S(1)}, bf16[64,192]{1,0:T(8,128)(2,1)}, u32[]{:S(2)}) copy-start(bf16[64,192]{1,0:T(8,128)(2,1)} %constant.42) | copy-start | bytes 73732
  1.5 15.3 %collective-permute-start = (bf16[8,4224]{1,0:T(8,128)(2,1)S(1)}, bf16[8,4224]{1,0:T(8,128)(2,1)S(1)}, u32[]{:S(2)}, u32[]{:S(2)}) collective-permute-start(bf16[8,4224]{1,0:T(8,128)(2,1)S(1)} %concatenate.39.x_ref), channel_id=1, source_target_pairs={{0,0},{1,16},{2,32},{3,48},{4,64},{5,80},{6,96},{7,112},{8,8},{9,2... | collective-permute-start | bytes 202760 | tf_op jit(solution)/shard_map/ppermute | solution.py:199
  7.6 33.3 %all-to-all-start = ((bf16[8,8,4096]{2,1,0:T(8,128)(2,1)}), bf16[8,8,4096]{2,1,0:T(8,128)(2,1)S(1)}, u32[]{:S(2)}, u32[]{:S(2)}) async-start(bf16[8,8,4096]{2,1,0:T(8,128)(2,1)} %copies.1), calls=%async_computation | async-start | bytes 1048576 | tf_op jit(solution)/shard_map/all_to_all | solution.py:222
  16.9 1.3 %collective-permute-start.1 = (bf16[8,4224]{1,0:T(8,128)(2,1)S(1)}, bf16[8,4224]{1,0:T(8,128)(2,1)S(1)}, u32[]{:S(2)}, u32[]{:S(2)}) collective-permute-start(bf16[8,4224]{1,0:T(8,128)(2,1)S(1)} %collective-permute-done), channel_id=1, source_target_pairs={{0,8},{1,9},{2,10},{3,11},{4,12},{5,13},{6,14},{7,15},{8,0},{9,1},... | collective-permute-start | bytes 202760 | tf_op jit(solution)/shard_map/ppermute | solution.py:199
  18.2 13.3 %collective-permute-start.5 = (bf16[2,8,4224]{2,1,0:T(8,128)(2,1)S(1)}, bf16[2,8,4224]{2,1,0:T(8,128)(2,1)S(1)}, u32[]{:S(2)}, u32[]{:S(2)}) collective-permute-start(bf16[2,8,4224]{2,1,0:T(8,128)(2,1)S(1)} %pad_maximum_fusion), channel_id=1, source_target_pairs={{0,16},{1,17},{2,18},{3,19},{4,20},{5,21},{6,22},{7,23},{8,120},{9... | collective-permute-start | bytes 405512 | tf_op jit(solution)/shard_map/ppermute | solution.py:199
  19.8 11.7 %collective-permute-start.4 = (bf16[2,8,4224]{2,1,0:T(8,128)(2,1)S(1)}, bf16[2,8,4224]{2,1,0:T(8,128)(2,1)S(1)}, u32[]{:S(2)}, u32[]{:S(2)}) collective-permute-start(bf16[2,8,4224]{2,1,0:T(8,128)(2,1)S(1)} %pad_maximum_fusion), channel_id=1, source_target_pairs={{0,32},{1,33},{2,34},{3,35},{4,36},{5,37},{6,38},{7,39},{8,104},{9... | collective-permute-start | bytes 405512 | tf_op jit(solution)/shard_map/ppermute | solution.py:199
  22.0 10.3 %collective-permute-start.2 = (bf16[2,8,4224]{2,1,0:T(8,128)(2,1)S(1)}, bf16[2,8,4224]{2,1,0:T(8,128)(2,1)}, u32[]{:S(2)}, u32[]{:S(2)}) collective-permute-start(bf16[2,8,4224]{2,1,0:T(8,128)(2,1)S(1)} %pad_maximum_fusion), channel_id=1, source_target_pairs={{0,48},{1,49},{2,50},{3,51},{4,52},{5,53},{6,54},{7,55},{8,88},{9,... | collective-permute-start | bytes 405512 | tf_op jit(solution)/shard_map/ppermute | solution.py:199
  31.6 9.3 %collective-permute-start.9 = (bf16[4,8,4224]{2,1,0:T(8,128)(2,1)S(1)}, bf16[4,8,4224]{2,1,0:T(8,128)(2,1)}, u32[]{:S(2)}, u32[]{:S(2)}) collective-permute-start(bf16[4,8,4224]{2,1,0:T(8,128)(2,1)S(1)} %constant_dynamic-update-slice_fusion.2.refs_1_), channel_id=1, source_target_pairs={{0,8},{1,9},{2,10},{3,11},{4,12},{5,13},{6,14},{7,15},{8,0},{9,1},... | collective-permute-start | bytes 811016 | tf_op jit(solution)/shard_map/ppermute | solution.py:199
  33.2 7.7 %collective-permute-start.8 = (bf16[4,8,4224]{2,1,0:T(8,128)(2,1)S(1)}, bf16[4,8,4224]{2,1,0:T(8,128)(2,1)}, u32[]{:S(2)}, u32[]{:S(2)}) collective-permute-start(bf16[4,8,4224]{2,1,0:T(8,128)(2,1)S(1)} %constant_dynamic-update-slice_fusion.refs_0_), channel_id=1, source_target_pairs={{0,8},{1,9},{2,10},{3,11},{4,12},{5,13},{6,14},{7,15},{8,0},{9,1},... | collective-permute-start | bytes 811016 | tf_op jit(solution)/shard_map/ppermute | solution.py:199
  34.2 6.7 %collective-permute-start.7 = (bf16[2,8,4224]{2,1,0:T(8,128)(2,1)S(1)}, bf16[2,8,4224]{2,1,0:T(8,128)(2,1)S(1)}, u32[]{:S(2)}, u32[]{:S(2)}) collective-permute-start(bf16[2,8,4224]{2,1,0:T(8,128)(2,1)S(1)} %broadcast_select_fusion), channel_id=1, source_target_pairs={{0,16},{1,17},{2,18},{3,19},{4,20},{5,21},{6,22},{7,23},{8,120},{9... | collective-permute-start | bytes 405512 | tf_op jit(solution)/shard_map/ppermute | solution.py:199
  36.7 10.4 %collective-permute-start.6 = (bf16[4,8,4224]{2,1,0:T(8,128)(2,1)S(1)}, bf16[4,8,4224]{2,1,0:T(8,128)(2,1)}, u32[]{:S(2)}, u32[]{:S(2)}) collective-permute-start(bf16[4,8,4224]{2,1,0:T(8,128)(2,1)S(1)} %constant_dynamic-update-slice_fusion.2.refs_1_), channel_id=1, source_target_pairs={{0,128},{1,129},{2,130},{3,131},{4,132},{5,133},{6,134},{7,135},{8... | collective-permute-start | bytes 811016 | tf_op jit(solution)/shard_map/ppermute | solution.py:199
  39.7 13.2 %collective-permute-start.3 = (bf16[4,8,4224]{2,1,0:T(8,128)(2,1)S(1)}, bf16[4,8,4224]{2,1,0:T(8,128)(2,1)}, u32[]{:S(2)}, u32[]{:S(2)}) collective-permute-start(bf16[4,8,4224]{2,1,0:T(8,128)(2,1)S(1)} %constant_dynamic-update-slice_fusion.refs_0_), channel_id=1, source_target_pairs={{0,128},{1,129},{2,130},{3,131},{4,132},{5,133},{6,134},{7,135},{8... | collective-permute-start | bytes 811016 | tf_op jit(solution)/shard_map/ppermute | solution.py:199
  47.1 13.5 %collective-permute-start.12 = (bf16[4,8,4224]{2,1,0:T(8,128)(2,1)}, bf16[4,8,4224]{2,1,0:T(8,128)(2,1)S(1)}, u32[]{:S(2)}, u32[]{:S(2)}) collective-permute-start(bf16[4,8,4224]{2,1,0:T(8,128)(2,1)} %collective-permute-done.6.refs_1_), channel_id=1, source_target_pairs={{0,8},{1,9},{2,10},{3,11},{4,12},{5,13},{6,14},{7,15},{8,0},{9,1},... | collective-permute-start | bytes 811016 | tf_op jit(solution)/shard_map/ppermute | solution.py:199
  52.9 7.7 %collective-permute-start.11 = (bf16[4,8,4224]{2,1,0:T(8,128)(2,1)}, bf16[4,8,4224]{2,1,0:T(8,128)(2,1)S(1)}, u32[]{:S(2)}, u32[]{:S(2)}) collective-permute-start(bf16[4,8,4224]{2,1,0:T(8,128)(2,1)} %collective-permute-done.3.refs_0_), channel_id=1, source_target_pairs={{0,8},{1,9},{2,10},{3,11},{4,12},{5,13},{6,14},{7,15},{8,0},{9,1},... | collective-permute-start | bytes 811016 | tf_op jit(solution)/shard_map/ppermute | solution.py:199
  53.2 7.3 %collective-permute-start.10 = (bf16[2,8,4224]{2,1,0:T(8,128)(2,1)S(1)}, bf16[2,8,4224]{2,1,0:T(8,128)(2,1)S(1)}, u32[]{:S(2)}, u32[]{:S(2)}) collective-permute-start(bf16[2,8,4224]{2,1,0:T(8,128)(2,1)S(1)} %collective-permute-done.7.refs_2_), channel_id=1, source_target_pairs={{0,128},{1,129},{2,130},{3,131},{4,132},{5,133},{6,134},{7,135},{8... | collective-permute-start | bytes 405512 | tf_op jit(solution)/shard_map/ppermute | solution.py:199

commit v8 on v6

--- a/solution.py
+++ b/solution.py
@@ -40,7 +40,7 @@
     p = jnp.arange(GRID, dtype=jnp.int32)
     f = jnp.minimum(p, GRID - p)
     sq = (f * f).astype(jnp.float32)
-    tot = sq[:, None, None] + sq[None, :, None] + jnp.concatenate([sq, sq])[None, None, :]
+    tot = sq[: GRID // 2 + 1, None, None] + sq[None, :, None] + jnp.concatenate([sq, sq])[None, None, :]
     c = jnp.where(live, box_length**2 / (math.pi * GRID**3), 0.0)
     return jnp.where(tot > 0.5, c / jnp.maximum(tot, 1.0), 0.0)
 
@@ -105,7 +105,8 @@
         kx = step * GM
         parts = [f_ref[pl.ds(kx + i, 64, stride=PITCH), :] for i in range(GM)]
         h = along_rows(left, jnp.concatenate(parts, axis=1))
-        h = h * jnp.concatenate([green_ref[kx + i] for i in range(GM)], axis=1)
+        folded = [jnp.minimum(kx + i, GRID - kx - i) for i in range(GM)]
+        h = h * jnp.concatenate([green_ref[k] for k in folded], axis=1)
         u = along_rows(left, h)
         for i in range(GM):
             f_ref[pl.ds(kx + i, 64, stride=PITCH), :] = u[:, 128 * i : 128 * i + 128]
@@ -230,7 +231,7 @@
     right = jnp.where(live, right, 0)
     green = green_table(live)
     hop = {}
-    for k in (1, 3, 2):
+    for k in (3, 1, 2):
         hop[k] = moved(pair, ring(k))
     held, first, left, right, green = lax.optimization_barrier((pair, hop[1], left, right, green))
     early = jnp.concatenate([held, first])

time: 80.6 us -> 78.2 us (0.970)
  Pallas kernels: 12.3 us -> 10.2 us
  waiting for transfers between devices: 20.7 us -> 22 us
  local copies, waits for them, and re-layouts: 1.81 us -> 0.91 us
    pallas_call x2, Pallas kernels: 11.4 us -> 9.33 us  [solve(): pl.pallas_call(functools.partial(solve_kernel, not more), out_shape=jax.S...]
    ppermute x13, waiting for transfers between devices: 20.7 us -> 22 us  [moved(): return lax.ppermute(x, AXES, pairs)]
    concatenate x1, local copies, waits for them, and re-layouts: 0.92 us -> 0.02 us  [exchange(): early = jnp.concatenate([held, first])]
  transfers between devices with their start and end apart: 14 -> 14, of which waited for: 5 -> 6; matrix products, arithmetic and copies ran while one was open for 2% -> 1% of each run, Pallas kernels for 8% -> 7%
where the time goes in v8:
time: 78.2 us; the launch traced here: 77.2 us
  starting transfers between devices  28.2 us (36%)
  waiting for transfers between devices  22 us (28%)
  blocking collectives  13.4 us (17%)
  Pallas kernels  10.2 us (13%)
  other arithmetic  1.61 us (2%)
  local copies, waits for them, and re-layouts  0.91 us (1%)
  between operations  0.84 us (1%)
    ppermute x13, waiting for transfers between devices, moved(): return lax.ppermute(x, AXES, pairs)  22 us
    ppermute x13, starting transfers between devices, moved(): return lax.ppermute(x, AXES, pairs)  19 us
    all_to_all x1, blocking collectives, exchange(): lax.all_to_all(sent, 'dist', split_axis=0, concat_axis=0, tiled=True)  13.4 us
    pallas_call x2, Pallas kernels, solve(): pl.pallas_call(functools.partial(solve_kernel, not more), out_shape=jax.S...  9.33 us
    all_to_all x1, starting transfers between devices, exchange(): lax.all_to_all(copies, 'dist', split_axis=0, concat_axis=0, tiled=True)  9.19 us
  transfers between devices with their start and end apart: 14, of which 6 were waited for; matrix products, arithmetic and copies ran while one was open for 1% of the time, Pallas kernels for 7%

profile of v8, /device:TPU:8, one launch (start us, length us, event | category | flops | bytes accessed | tf_op | source)
XLA Modules:
  0.0 77.2 jit_solution(12620758103411609309)
XLA Ops:
  0.7 0.8 %concatenate.39.x_ref = bf16[8,4224]{1,0:T(8,128)(2,1)S(1)} pad(bf16[8,4096]{1,0:T(8,128)(2,1)} %bitcast.16, bf16[]{:T(256)} %bitcast.11), padding=0_0x0_128 | pad | bytes 133122 | tf_op jit(solution)/shard_map/concatenate | solution.py:220
  1.5 5.1 %collective-permute-start = (bf16[8,4224]{1,0:T(8,128)(2,1)S(1)}, bf16[8,4224]{1,0:T(8,128)(2,1)S(1)}, u32[]{:S(2)}, u32[]{:S(2)}) collective-permute-start(bf16[8,4224]{1,0:T(8,128)(2,1)S(1)} %concatenate.39.x_ref), channel_id=1, source_target_pairs={{0,0},{1,16},{2,32},{3,48},{4,64},{5,80},{6,96},{7,112},{8,8},{9,2... | collective-permute-start | bytes 202760 | tf_op jit(solution)/shard_map/ppermute | solution.py:200
  6.6 0.9 %copies.1 = bf16[8,8,4096]{2,1,0:T(8,128)(2,1)} custom-call(bf16[8,4224]{1,0:T(8,128)(2,1)S(1)} %concatenate.39.x_ref), custom_call_target="tpu_custom_call" | custom-call | tf_op jit(solution)/shard_map/copies/pallas_call | solution.py:155
  7.5 9.2 %all-to-all-start = ((bf16[8,8,4096]{2,1,0:T(8,128)(2,1)}), bf16[8,8,4096]{2,1,0:T(8,128)(2,1)S(1)}, u32[]{:S(2)}, u32[]{:S(2)}) async-start(bf16[8,8,4096]{2,1,0:T(8,128)(2,1)} %copies.1), calls=%async_computation | async-start | bytes 1048576 | tf_op jit(solution)/shard_map/all_to_all | solution.py:223
  16.9 1.2 %collective-permute-done.1 = bf16[8,4224]{1,0:T(8,128)(2,1)S(1)} collective-permute-done((bf16[8,4224]{1,0:T(8,128)(2,1)S(1)}, bf16[8,4224]{1,0:T(8,128)(2,1)S(1)}, u32[]{:S(2)}, u32[]{:S(2)}) %collective-permute-start.1) | collective-permute-done | bytes 67616 | tf_op jit(solution)/shard_map/ppermute | solution.py:200
  18.1 2.3 %collective-permute-start.5 = (bf16[2,8,4224]{2,1,0:T(8,128)(2,1)S(1)}, bf16[2,8,4224]{2,1,0:T(8,128)(2,1)S(1)}, u32[]{:S(2)}, u32[]{:S(2)}) collective-permute-start(bf16[2,8,4224]{2,1,0:T(8,128)(2,1)S(1)} %pad_maximum_fusion), channel_id=1, source_target_pairs={{0,32},{1,33},{2,34},{3,35},{4,36},{5,37},{6,38},{7,39},{8,104},{9... | collective-permute-start | bytes 405512 | tf_op jit(solution)/shard_map/ppermute | solution.py:200
  20.4 2.3 %collective-permute-start.4 = (bf16[2,8,4224]{2,1,0:T(8,128)(2,1)S(1)}, bf16[2,8,4224]{2,1,0:T(8,128)(2,1)S(1)}, u32[]{:S(2)}, u32[]{:S(2)}) collective-permute-start(bf16[2,8,4224]{2,1,0:T(8,128)(2,1)S(1)} %pad_maximum_fusion), channel_id=1, source_target_pairs={{0,48},{1,49},{2,50},{3,51},{4,52},{5,53},{6,54},{7,55},{8,88},{9,... | collective-permute-start | bytes 405512 | tf_op jit(solution)/shard_map/ppermute | solution.py:200
  22.6 2.1 %collective-permute-start.2 = (bf16[2,8,4224]{2,1,0:T(8,128)(2,1)S(1)}, bf16[2,8,4224]{2,1,0:T(8,128)(2,1)S(1)}, u32[]{:S(2)}, u32[]{:S(2)}) collective-permute-start(bf16[2,8,4224]{2,1,0:T(8,128)(2,1)S(1)} %pad_maximum_fusion), channel_id=1, source_target_pairs={{0,16},{1,17},{2,18},{3,19},{4,20},{5,21},{6,22},{7,23},{8,120},{9... | collective-permute-start | bytes 405512 | tf_op jit(solution)/shard_map/ppermute | solution.py:200
  24.7 0.4 fusion.1.refs_7_
  25.1 8.0 %collective-permute-done.4 = bf16[2,8,4224]{2,1,0:T(8,128)(2,1)S(1)} collective-permute-done((bf16[2,8,4224]{2,1,0:T(8,128)(2,1)S(1)}, bf16[2,8,4224]{2,1,0:T(8,128)(2,1)S(1)}, u32[]{:S(2)}, u32[]{:S(2)}) %collective-permute-start.4) | collective-permute-done | bytes 135200 | tf_op jit(solution)/shard_map/ppermute | solution.py:200
  33.2 0.1 collective-permute-start.9
  33.3 0.6 collective-permute-start.8
  33.9 2.9 %collective-permute-start.6 = (bf16[4,8,4224]{2,1,0:T(8,128)(2,1)S(1)}, bf16[4,8,4224]{2,1,0:T(8,128)(2,1)S(1)}, u32[]{:S(2)}, u32[]{:S(2)}) collective-permute-start(bf16[4,8,4224]{2,1,0:T(8,128)(2,1)S(1)} %constant_dynamic-update-slice_fusion.2.refs_1_), channel_id=1, source_target_pairs={{0,128},{1,129},{2,130},{3,131},{4,132},{5,133},{6,134},{7,135},{8... | collective-permute-start | bytes 811016 | tf_op jit(solution)/shard_map/ppermute | solution.py:200
  36.8 0.7 collective-permute-start.3
  37.4 2.7 %collective-permute-done.7.refs_2_ = bf16[2,8,4224]{2,1,0:T(8,128)(2,1)S(1)} collective-permute-done((bf16[2,8,4224]{2,1,0:T(8,128)(2,1)S(1)}, bf16[2,8,4224]{2,1,0:T(8,128)(2,1)S(1)}, u32[]{:S(2)}, u32[]{:S(2)}) %collective-permute-start.7) | collective-permute-done | bytes 135200 | tf_op jit(solution)/shard_map/ppermute | solution.py:200
  40.1 4.5 %solve.2.refs_8_ = f32[64,4096]{1,0:T(8,128)S(1)} custom-call(s32[1]{0:T(128)} %bitcast.4.seat_ref, bf16[64,4096]{1,0:T(8,128)(2,1)S(1)} %bitcast.12, bf16[4,8,4224]{2,1,0:T(8,128)(2,1)S(1)} %constant_dynamic-update-slice_fusion.refs_0_, bf16[4,8,4224]{2,1,0:T(8,128)(2,1)S(1)} %constant_dynamic-update-slice_fusion.2.refs_1_, ...), custom_call_target="tpu_custom_call" | custom-call | flops 10000000000 | bytes 10000000 | tf_op jit(solution)/shard_map/solve/pallas_call | solution.py:170
  44.6 0.1 collective-permute-done.6.refs_1_
  44.8 5.6 %collective-permute-done.3.refs_0_ = bf16[4,8,4224]{2,1,0:T(8,128)(2,1)S(1)} collective-permute-done((bf16[4,8,4224]{2,1,0:T(8,128)(2,1)S(1)}, bf16[4,8,4224]{2,1,0:T(8,128)(2,1)S(1)}, u32[]{:S(2)}, u32[]{:S(2)}) %collective-permute-start.3) | collective-permute-done | bytes 270368 | tf_op jit(solution)/shard_map/ppermute | solution.py:200
  50.3 3.1 %collective-permute-start.10 = (bf16[2,8,4224]{2,1,0:T(8,128)(2,1)S(1)}, bf16[2,8,4224]{2,1,0:T(8,128)(2,1)S(1)}, u32[]{:S(2)}, u32[]{:S(2)}) collective-permute-start(bf16[2,8,4224]{2,1,0:T(8,128)(2,1)S(1)} %collective-permute-done.7.refs_2_), channel_id=1, source_target_pairs={{0,128},{1,129},{2,130},{3,131},{4,132},{5,133},{6,134},{7,135},{8... | collective-permute-start | bytes 405512 | tf_op jit(solution)/shard_map/ppermute | solution.py:200
  53.5 4.4 %collective-permute-done.10.refs_2_ = bf16[2,8,4224]{2,1,0:T(8,128)(2,1)S(1)} collective-permute-done((bf16[2,8,4224]{2,1,0:T(8,128)(2,1)S(1)}, bf16[2,8,4224]{2,1,0:T(8,128)(2,1)S(1)}, u32[]{:S(2)}, u32[]{:S(2)}) %collective-permute-start.10) | collective-permute-done | bytes 135200 | tf_op jit(solution)/shard_map/ppermute | solution.py:200
  57.8 4.9 %solve.3 = f32[64,4224]{1,0:T(8,128)S(1)} custom-call(s32[1]{0:T(128)} %bitcast.4.seat_ref, bf16[64,4096]{1,0:T(8,128)(2,1)S(1)} %bitcast.13, bf16[4,8,4224]{2,1,0:T(8,128)(2,1)S(1)} %collective-permute-done.3.refs_0_, bf16[4,8,4224]{2,1,0:T(8,128)(2,1)S(1)} %collective-permute-done.6.refs_1_, bf16[2,8,4224]{2,1,0:T(8,128)(2,1)S(1)} %collective-permute-done.10.refs_2_, ...), custom_call_target="tpu_custom_call" | custom-call | flops 10000000000 | bytes 10000000 | tf_op jit(solution)/shard_map/solve/pallas_call | solution.py:170
  62.8 13.4 %all_to_all.10 = f16[8,8,4224]{2,1,0:T(8,128)(2,1)S(1)} all-to-all(f16[8,8,4224]{2,1,0:T(8,128)(2,1)S(1)} %convert_bitcast_fusion), channel_id=1, replica_groups=mesh['grp'=32,'dist'=8] {'dist'}, dimensions={0} | all-to-all | bytes 1081344 | tf_op jit(solution)/shard_map/all_to_all | solution.py:253
  76.2 0.2 exponential_reduce_fusion
  76.4 0.8 %multiply_reduce_fusion = f32[8,4096]{1,0:T(8,128)} fusion(f16[8,8,4224]{2,1,0:T(8,128)(2,1)S(1)} %all_to_all.10, f32[8]{0:T(128)S(1)} %exponential_reduce_fusion), kind=kLoop, calls=%fused_computation.4 | loop fusion | flops 753664 | bytes 655392 | tf_op jit(solution)/shard_map/reduce_sum | solution.py:256
  (28 shorter events, 0.4 us)
Async XLA Ops:
  0.0 24.7 %copy-start = (bf16[256,256]{1,0:T(8,128)(2,1)S(1)}, bf16[256,256]{1,0:T(8,128)(2,1)}, u32[]{:S(2)}) copy-start(bf16[256,256]{1,0:T(8,128)(2,1)} %constant.50) | copy-start | bytes 393220
  1.5 15.2 %collective-permute-start = (bf16[8,4224]{1,0:T(8,128)(2,1)S(1)}, bf16[8,4224]{1,0:T(8,128)(2,1)S(1)}, u32[]{:S(2)}, u32[]{:S(2)}) collective-permute-start(bf16[8,4224]{1,0:T(8,128)(2,1)S(1)} %concatenate.39.x_ref), channel_id=1, source_target_pairs={{0,0},{1,16},{2,32},{3,48},{4,64},{5,80},{6,96},{7,112},{8,8},{9,2... | collective-permute-start | bytes 202760 | tf_op jit(solution)/shard_map/ppermute | solution.py:200
  7.5 32.6 %all-to-all-start = ((bf16[8,8,4096]{2,1,0:T(8,128)(2,1)}), bf16[8,8,4096]{2,1,0:T(8,128)(2,1)S(1)}, u32[]{:S(2)}, u32[]{:S(2)}) async-start(bf16[8,8,4096]{2,1,0:T(8,128)(2,1)} %copies.1), calls=%async_computation | async-start | bytes 1048576 | tf_op jit(solution)/shard_map/all_to_all | solution.py:223
  16.7 8.4 %copy-start.1 = (bf16[64,192]{1,0:T(8,128)(2,1)S(1)}, bf16[64,192]{1,0:T(8,128)(2,1)}, u32[]{:S(2)}) copy-start(bf16[64,192]{1,0:T(8,128)(2,1)} %constant.42) | copy-start | bytes 73732
  16.8 1.3 %collective-permute-start.1 = (bf16[8,4224]{1,0:T(8,128)(2,1)S(1)}, bf16[8,4224]{1,0:T(8,128)(2,1)S(1)}, u32[]{:S(2)}, u32[]{:S(2)}) collective-permute-start(bf16[8,4224]{1,0:T(8,128)(2,1)S(1)} %collective-permute-done), channel_id=1, source_target_pairs={{0,8},{1,9},{2,10},{3,11},{4,12},{5,13},{6,14},{7,15},{8,0},{9,1},... | collective-permute-start | bytes 202760 | tf_op jit(solution)/shard_map/ppermute | solution.py:200
  18.1 15.0 %collective-permute-start.5 = (bf16[2,8,4224]{2,1,0:T(8,128)(2,1)S(1)}, bf16[2,8,4224]{2,1,0:T(8,128)(2,1)S(1)}, u32[]{:S(2)}, u32[]{:S(2)}) collective-permute-start(bf16[2,8,4224]{2,1,0:T(8,128)(2,1)S(1)} %pad_maximum_fusion), channel_id=1, source_target_pairs={{0,32},{1,33},{2,34},{3,35},{4,36},{5,37},{6,38},{7,39},{8,104},{9... | collective-permute-start | bytes 405512 | tf_op jit(solution)/shard_map/ppermute | solution.py:200
  20.4 12.7 %collective-permute-start.4 = (bf16[2,8,4224]{2,1,0:T(8,128)(2,1)S(1)}, bf16[2,8,4224]{2,1,0:T(8,128)(2,1)S(1)}, u32[]{:S(2)}, u32[]{:S(2)}) collective-permute-start(bf16[2,8,4224]{2,1,0:T(8,128)(2,1)S(1)} %pad_maximum_fusion), channel_id=1, source_target_pairs={{0,48},{1,49},{2,50},{3,51},{4,52},{5,53},{6,54},{7,55},{8,88},{9,... | collective-permute-start | bytes 405512 | tf_op jit(solution)/shard_map/ppermute | solution.py:200
  22.6 10.6 %collective-permute-start.2 = (bf16[2,8,4224]{2,1,0:T(8,128)(2,1)S(1)}, bf16[2,8,4224]{2,1,0:T(8,128)(2,1)S(1)}, u32[]{:S(2)}, u32[]{:S(2)}) collective-permute-start(bf16[2,8,4224]{2,1,0:T(8,128)(2,1)S(1)} %pad_maximum_fusion), channel_id=1, source_target_pairs={{0,16},{1,17},{2,18},{3,19},{4,20},{5,21},{6,22},{7,23},{8,120},{9... | collective-permute-start | bytes 405512 | tf_op jit(solution)/shard_map/ppermute | solution.py:200
  33.2 7.0 %collective-permute-start.9 = (bf16[4,8,4224]{2,1,0:T(8,128)(2,1)S(1)}, bf16[4,8,4224]{2,1,0:T(8,128)(2,1)S(1)}, u32[]{:S(2)}, u32[]{:S(2)}) collective-permute-start(bf16[4,8,4224]{2,1,0:T(8,128)(2,1)S(1)} %constant_dynamic-update-slice_fusion.2.refs_1_), channel_id=1, source_target_pairs={{0,8},{1,9},{2,10},{3,11},{4,12},{5,13},{6,14},{7,15},{8,0},{9,1},... | collective-permute-start | bytes 811016 | tf_op jit(solution)/shard_map/ppermute | solution.py:200
  33.3 6.8 %collective-permute-start.8 = (bf16[4,8,4224]{2,1,0:T(8,128)(2,1)S(1)}, bf16[4,8,4224]{2,1,0:T(8,128)(2,1)S(1)}, u32[]{:S(2)}, u32[]{:S(2)}) collective-permute-start(bf16[4,8,4224]{2,1,0:T(8,128)(2,1)S(1)} %constant_dynamic-update-slice_fusion.refs_0_), channel_id=1, source_target_pairs={{0,8},{1,9},{2,10},{3,11},{4,12},{5,13},{6,14},{7,15},{8,0},{9,1},... | collective-permute-start | bytes 811016 | tf_op jit(solution)/shard_map/ppermute | solution.py:200
  33.9 6.2 %collective-permute-start.7 = (bf16[2,8,4224]{2,1,0:T(8,128)(2,1)S(1)}, bf16[2,8,4224]{2,1,0:T(8,128)(2,1)S(1)}, u32[]{:S(2)}, u32[]{:S(2)}) collective-permute-start(bf16[2,8,4224]{2,1,0:T(8,128)(2,1)S(1)} %get-tuple-element.23), channel_id=1, source_target_pairs={{0,16},{1,17},{2,18},{3,19},{4,20},{5,21},{6,22},{7,23},{8,120},{9... | collective-permute-start | bytes 405512 | tf_op jit(solution)/shard_map/ppermute | solution.py:200
  33.9 10.9 %collective-permute-start.6 = (bf16[4,8,4224]{2,1,0:T(8,128)(2,1)S(1)}, bf16[4,8,4224]{2,1,0:T(8,128)(2,1)S(1)}, u32[]{:S(2)}, u32[]{:S(2)}) collective-permute-start(bf16[4,8,4224]{2,1,0:T(8,128)(2,1)S(1)} %constant_dynamic-update-slice_fusion.2.refs_1_), channel_id=1, source_target_pairs={{0,128},{1,129},{2,130},{3,131},{4,132},{5,133},{6,134},{7,135},{8... | collective-permute-start | bytes 811016 | tf_op jit(solution)/shard_map/ppermute | solution.py:200
  36.8 13.6 %collective-permute-start.3 = (bf16[4,8,4224]{2,1,0:T(8,128)(2,1)S(1)}, bf16[4,8,4224]{2,1,0:T(8,128)(2,1)S(1)}, u32[]{:S(2)}, u32[]{:S(2)}) collective-permute-start(bf16[4,8,4224]{2,1,0:T(8,128)(2,1)S(1)} %constant_dynamic-update-slice_fusion.refs_0_), channel_id=1, source_target_pairs={{0,128},{1,129},{2,130},{3,131},{4,132},{5,133},{6,134},{7,135},{8... | collective-permute-start | bytes 811016 | tf_op jit(solution)/shard_map/ppermute | solution.py:200
  44.8 13.1 %collective-permute-start.12 = (bf16[4,8,4224]{2,1,0:T(8,128)(2,1)S(1)}, bf16[4,8,4224]{2,1,0:T(8,128)(2,1)S(1)}, u32[]{:S(2)}, u32[]{:S(2)}) collective-permute-start(bf16[4,8,4224]{2,1,0:T(8,128)(2,1)S(1)} %collective-permute-done.6.refs_1_), channel_id=1, source_target_pairs={{0,8},{1,9},{2,10},{3,11},{4,12},{5,13},{6,14},{7,15},{8,0},{9,1},... | collective-permute-start | bytes 811016 | tf_op jit(solution)/shard_map/ppermute | solution.py:200
  50.3 7.5 %collective-permute-start.11 = (bf16[4,8,4224]{2,1,0:T(8,128)(2,1)S(1)}, bf16[4,8,4224]{2,1,0:T(8,128)(2,1)S(1)}, u32[]{:S(2)}, u32[]{:S(2)}) collective-permute-start(bf16[4,8,4224]{2,1,0:T(8,128)(2,1)S(1)} %collective-permute-done.3.refs_0_), channel_id=1, source_target_pairs={{0,8},{1,9},{2,10},{3,11},{4,12},{5,13},{6,14},{7,15},{8,0},{9,1},... | collective-permute-start | bytes 811016 | tf_op jit(solution)/shard_map/ppermute | solution.py:200
  50.3 7.5 %collective-permute-start.10 = (bf16[2,8,4224]{2,1,0:T(8,128)(2,1)S(1)}, bf16[2,8,4224]{2,1,0:T(8,128)(2,1)S(1)}, u32[]{:S(2)}, u32[]{:S(2)}) collective-permute-start(bf16[2,8,4224]{2,1,0:T(8,128)(2,1)S(1)} %collective-permute-done.7.refs_2_), channel_id=1, source_target_pairs={{0,128},{1,129},{2,130},{3,131},{4,132},{5,133},{6,134},{7,135},{8... | collective-permute-start | bytes 405512 | tf_op jit(solution)/shard_map/ppermute | solution.py:200

commit v9 on v8

--- a/solution.py
+++ b/solution.py
@@ -76,10 +76,10 @@
 
     place(early_ref, 0, core, z)
     place(fourth_ref, 0, core, z + 4)
-    sides = ((core, early_ref, late_ref), (1 - core, other_early_ref, other_late_ref))
-    for holder, early, late in sides:
+    sides = ((core, early_ref, 2, late_ref), (1 - core, other_early_ref, 0, other_late_ref))
+    for holder, early, start, late in sides:
         sign = jnp.where(holder == 0, -1, 1)
-        place(early, 2, holder, z + sign)
+        place(early, start, holder, z + sign)
         place(late, 0, holder, z + 3 * sign)
         place(late, 2, holder, z + 2 * sign)
 
@@ -231,21 +231,21 @@
     right = jnp.where(live, right, 0)
     green = green_table(live)
     hop = {}
-    for k in (3, 1, 2):
+    for k in (1, 3, 2):
         hop[k] = moved(pair, ring(k))
     held, first, left, right, green = lax.optimization_barrier((pair, hop[1], left, right, green))
     early = jnp.concatenate([held, first])
     far_early = moved(early, halves)
-    core_early = moved(early, cores)
+    core_early = moved(first, cores)
     fourth = moved(jnp.where(live, hop[3], 0), ring(1))
     late = jnp.concatenate([hop[3], hop[2]])
     core_late = moved(late, cores)
     far_late = moved(late, halves)
     far_fourth = moved(fourth, halves)
-    far_core_early = moved(far_early, cores)
     mine, other = (early, late, fourth), (core_early, core_late)
     partial = solve(seat, row, mine, other, left, right, green)
-    far_late, partial = lax.optimization_barrier((far_late, partial))
+    far_early, far_late, partial = lax.optimization_barrier((far_early, far_late, partial))
+    far_core_early = moved(far_early[2:], cores)
     far_core_late = moved(far_late, cores)
     mine, other = (far_early, far_late, far_fourth), (far_core_early, far_core_late)
     partial = solve(seat, row, mine, other, left, right, green, partial)

time: 78.2 us -> 76.7 us (0.981)
  waiting for transfers between devices: 22 us -> 21.2 us
  transfers between devices with their start and end apart: 14 -> 14, of which waited for: 6 -> 5; matrix products, arithmetic and copies ran while one was open for 1% -> 1% of each run, Pallas kernels for 7% -> 7%
where the time goes in v9:
time: 76.7 us; the launch traced here: 75.6 us
  starting transfers between devices  28.1 us (37%)
  waiting for transfers between devices  21.2 us (28%)
  blocking collectives  12.7 us (17%)
  Pallas kernels  10.2 us (13%)
  other arithmetic  1.61 us (2%)
  local copies, waits for them, and re-layouts  0.92 us (1%)
  between operations  0.84 us (1%)
    ppermute x13, waiting for transfers between devices, moved(): return lax.ppermute(x, AXES, pairs)  21.2 us
    ppermute x13, starting transfers between devices, moved(): return lax.ppermute(x, AXES, pairs)  18.9 us
    all_to_all x1, blocking collectives, exchange(): lax.all_to_all(sent, 'dist', split_axis=0, concat_axis=0, tiled=True)  12.7 us
    pallas_call x2, Pallas kernels, solve(): pl.pallas_call(functools.partial(solve_kernel, not more), out_shape=jax.S...  9.35 us
    all_to_all x1, starting transfers between devices, exchange(): lax.all_to_all(copies, 'dist', split_axis=0, concat_axis=0, tiled=True)  9.19 us
  transfers between devices with their start and end apart: 14, of which 5 were waited for; matrix products, arithmetic and copies ran while one was open for 1% of the time, Pallas kernels for 7%

profile of v9, /device:TPU:8, one launch (start us, length us, event | category | flops | bytes accessed | tf_op | source)
XLA Modules:
  0.0 75.6 jit_solution(12547995459052932957)
XLA Ops:
  0.7 0.8 %concatenate.39.x_ref = bf16[8,4224]{1,0:T(8,128)(2,1)S(1)} pad(bf16[8,4096]{1,0:T(8,128)(2,1)} %bitcast.16, bf16[]{:T(256)} %bitcast.11), padding=0_0x0_128 | pad | bytes 133122 | tf_op jit(solution)/shard_map/concatenate | solution.py:220
  1.5 5.1 %collective-permute-start = (bf16[8,4224]{1,0:T(8,128)(2,1)S(1)}, bf16[8,4224]{1,0:T(8,128)(2,1)S(1)}, u32[]{:S(2)}, u32[]{:S(2)}) collective-permute-start(bf16[8,4224]{1,0:T(8,128)(2,1)S(1)} %concatenate.39.x_ref), channel_id=1, source_target_pairs={{0,0},{1,16},{2,32},{3,48},{4,64},{5,80},{6,96},{7,112},{8,8},{9,2... | collective-permute-start | bytes 202760 | tf_op jit(solution)/shard_map/ppermute | solution.py:200
  6.6 0.9 %copies.1 = bf16[8,8,4096]{2,1,0:T(8,128)(2,1)} custom-call(bf16[8,4224]{1,0:T(8,128)(2,1)S(1)} %concatenate.39.x_ref), custom_call_target="tpu_custom_call" | custom-call | tf_op jit(solution)/shard_map/copies/pallas_call | solution.py:155
  7.5 9.2 %all-to-all-start = ((bf16[8,8,4096]{2,1,0:T(8,128)(2,1)}), bf16[8,8,4096]{2,1,0:T(8,128)(2,1)S(1)}, u32[]{:S(2)}, u32[]{:S(2)}) async-start(bf16[8,8,4096]{2,1,0:T(8,128)(2,1)} %copies.1), calls=%async_computation | async-start | bytes 1048576 | tf_op jit(solution)/shard_map/all_to_all | solution.py:223
  16.9 1.2 %collective-permute-done.1 = bf16[8,4224]{1,0:T(8,128)(2,1)S(1)} collective-permute-done((bf16[8,4224]{1,0:T(8,128)(2,1)S(1)}, bf16[8,4224]{1,0:T(8,128)(2,1)S(1)}, u32[]{:S(2)}, u32[]{:S(2)}) %collective-permute-start.1) | collective-permute-done | bytes 67616 | tf_op jit(solution)/shard_map/ppermute | solution.py:200
  18.1 2.3 %collective-permute-start.5 = (bf16[2,8,4224]{2,1,0:T(8,128)(2,1)S(1)}, bf16[2,8,4224]{2,1,0:T(8,128)(2,1)S(1)}, u32[]{:S(2)}, u32[]{:S(2)}) collective-permute-start(bf16[2,8,4224]{2,1,0:T(8,128)(2,1)S(1)} %pad_maximum_fusion), channel_id=1, source_target_pairs={{0,32},{1,33},{2,34},{3,35},{4,36},{5,37},{6,38},{7,39},{8,104},{9... | collective-permute-start | bytes 405512 | tf_op jit(solution)/shard_map/ppermute | solution.py:200
  20.4 2.3 %collective-permute-start.4 = (bf16[2,8,4224]{2,1,0:T(8,128)(2,1)S(1)}, bf16[2,8,4224]{2,1,0:T(8,128)(2,1)S(1)}, u32[]{:S(2)}, u32[]{:S(2)}) collective-permute-start(bf16[2,8,4224]{2,1,0:T(8,128)(2,1)S(1)} %pad_maximum_fusion), channel_id=1, source_target_pairs={{0,48},{1,49},{2,50},{3,51},{4,52},{5,53},{6,54},{7,55},{8,88},{9,... | collective-permute-start | bytes 405512 | tf_op jit(solution)/shard_map/ppermute | solution.py:200
  22.6 2.1 %collective-permute-start.2 = (bf16[2,8,4224]{2,1,0:T(8,128)(2,1)S(1)}, bf16[2,8,4224]{2,1,0:T(8,128)(2,1)S(1)}, u32[]{:S(2)}, u32[]{:S(2)}) collective-permute-start(bf16[2,8,4224]{2,1,0:T(8,128)(2,1)S(1)} %pad_maximum_fusion), channel_id=1, source_target_pairs={{0,16},{1,17},{2,18},{3,19},{4,20},{5,21},{6,22},{7,23},{8,120},{9... | collective-permute-start | bytes 405512 | tf_op jit(solution)/shard_map/ppermute | solution.py:200
  24.7 0.4 fusion.1.refs_7_
  25.1 8.0 %collective-permute-done.4 = bf16[2,8,4224]{2,1,0:T(8,128)(2,1)S(1)} collective-permute-done((bf16[2,8,4224]{2,1,0:T(8,128)(2,1)S(1)}, bf16[2,8,4224]{2,1,0:T(8,128)(2,1)S(1)}, u32[]{:S(2)}, u32[]{:S(2)}) %collective-permute-start.4) | collective-permute-done | bytes 135200 | tf_op jit(solution)/shard_map/ppermute | solution.py:200
  33.2 0.1 collective-permute-start.9
  33.3 2.8 %collective-permute-start.6 = (bf16[4,8,4224]{2,1,0:T(8,128)(2,1)S(1)}, bf16[4,8,4224]{2,1,0:T(8,128)(2,1)S(1)}, u32[]{:S(2)}, u32[]{:S(2)}) collective-permute-start(bf16[4,8,4224]{2,1,0:T(8,128)(2,1)S(1)} %constant_dynamic-update-slice_fusion.2.refs_1_), channel_id=1, source_target_pairs={{0,128},{1,129},{2,130},{3,131},{4,132},{5,133},{6,134},{7,135},{8... | collective-permute-start | bytes 811016 | tf_op jit(solution)/shard_map/ppermute | solution.py:200
  36.0 0.3 collective-permute-start.7
  36.5 0.7 collective-permute-start.3
  37.2 5.0 %collective-permute-done.7.refs_2_ = bf16[2,8,4224]{2,1,0:T(8,128)(2,1)S(1)} collective-permute-done((bf16[2,8,4224]{2,1,0:T(8,128)(2,1)S(1)}, bf16[2,8,4224]{2,1,0:T(8,128)(2,1)S(1)}, u32[]{:S(2)}, u32[]{:S(2)}) %collective-permute-start.7) | collective-permute-done | bytes 135200 | tf_op jit(solution)/shard_map/ppermute | solution.py:200
  42.3 4.5 %solve.2.refs_8_ = f32[64,4096]{1,0:T(8,128)S(1)} custom-call(s32[1]{0:T(128)} %bitcast.4.seat_ref, bf16[64,4096]{1,0:T(8,128)(2,1)S(1)} %bitcast.12, bf16[4,8,4224]{2,1,0:T(8,128)(2,1)S(1)} %constant_dynamic-update-slice_fusion.refs_0_, bf16[4,8,4224]{2,1,0:T(8,128)(2,1)S(1)} %constant_dynamic-update-slice_fusion.2.refs_1_, ...), custom_call_target="tpu_custom_call" | custom-call | flops 10000000000 | bytes 10000000 | tf_op jit(solution)/shard_map/solve/pallas_call | solution.py:170
  46.8 2.7 %collective-permute-done.3.refs_0_ = bf16[4,8,4224]{2,1,0:T(8,128)(2,1)S(1)} collective-permute-done((bf16[4,8,4224]{2,1,0:T(8,128)(2,1)S(1)}, bf16[4,8,4224]{2,1,0:T(8,128)(2,1)S(1)}, u32[]{:S(2)}, u32[]{:S(2)}) %collective-permute-start.3) | collective-permute-done | bytes 270368 | tf_op jit(solution)/shard_map/ppermute | solution.py:200
  49.5 2.7 %collective-permute-start.10 = (bf16[2,8,4224]{2,1,0:T(8,128)(2,1)S(1)}, bf16[2,8,4224]{2,1,0:T(8,128)(2,1)S(1)}, u32[]{:S(2)}, u32[]{:S(2)}) collective-permute-start(bf16[2,8,4224]{2,1,0:T(8,128)(2,1)S(1)} %collective-permute-done.7.refs_2_), channel_id=1, source_target_pairs={{0,128},{1,129},{2,130},{3,131},{4,132},{5,133},{6,134},{7,135},{8... | collective-permute-start | bytes 405512 | tf_op jit(solution)/shard_map/ppermute | solution.py:200
  52.1 0.5 collective-permute-start.11
  52.6 4.3 %collective-permute-done.10.refs_2_ = bf16[2,8,4224]{2,1,0:T(8,128)(2,1)S(1)} collective-permute-done((bf16[2,8,4224]{2,1,0:T(8,128)(2,1)S(1)}, bf16[2,8,4224]{2,1,0:T(8,128)(2,1)S(1)}, u32[]{:S(2)}, u32[]{:S(2)}) %collective-permute-start.10) | collective-permute-done | bytes 135200 | tf_op jit(solution)/shard_map/ppermute | solution.py:200
  57.0 4.9 %solve.3 = f32[64,4224]{1,0:T(8,128)S(1)} custom-call(s32[1]{0:T(128)} %bitcast.4.seat_ref, bf16[64,4096]{1,0:T(8,128)(2,1)S(1)} %bitcast.13, bf16[4,8,4224]{2,1,0:T(8,128)(2,1)S(1)} %collective-permute-done.3.refs_0_, bf16[4,8,4224]{2,1,0:T(8,128)(2,1)S(1)} %collective-permute-done.6.refs_1_, bf16[2,8,4224]{2,1,0:T(8,128)(2,1)S(1)} %collective-permute-done.10.refs_2_, ...), custom_call_target="tpu_custom_call" | custom-call | flops 10000000000 | bytes 10000000 | tf_op jit(solution)/shard_map/solve/pallas_call | solution.py:170
  61.9 12.7 %all_to_all.10 = f16[8,8,4224]{2,1,0:T(8,128)(2,1)S(1)} all-to-all(f16[8,8,4224]{2,1,0:T(8,128)(2,1)S(1)} %convert_bitcast_fusion), channel_id=1, replica_groups=mesh['grp'=32,'dist'=8] {'dist'}, dimensions={0} | all-to-all | bytes 1081344 | tf_op jit(solution)/shard_map/all_to_all | solution.py:253
  74.6 0.2 exponential_reduce_fusion
  74.8 0.8 %multiply_reduce_fusion = f32[8,4096]{1,0:T(8,128)} fusion(f16[8,8,4224]{2,1,0:T(8,128)(2,1)S(1)} %all_to_all.10, f32[8]{0:T(128)S(1)} %exponential_reduce_fusion), kind=kLoop, calls=%fused_computation.4 | loop fusion | flops 753664 | bytes 655392 | tf_op jit(solution)/shard_map/reduce_sum | solution.py:256
  (29 shorter events, 0.5 us)
Async XLA Ops:
  0.0 24.7 %copy-start = (bf16[256,256]{1,0:T(8,128)(2,1)S(1)}, bf16[256,256]{1,0:T(8,128)(2,1)}, u32[]{:S(2)}) copy-start(bf16[256,256]{1,0:T(8,128)(2,1)} %constant.50) | copy-start | bytes 393220
  1.5 15.2 %collective-permute-start = (bf16[8,4224]{1,0:T(8,128)(2,1)S(1)}, bf16[8,4224]{1,0:T(8,128)(2,1)S(1)}, u32[]{:S(2)}, u32[]{:S(2)}) collective-permute-start(bf16[8,4224]{1,0:T(8,128)(2,1)S(1)} %concatenate.39.x_ref), channel_id=1, source_target_pairs={{0,0},{1,16},{2,32},{3,48},{4,64},{5,80},{6,96},{7,112},{8,8},{9,2... | collective-permute-start | bytes 202760 | tf_op jit(solution)/shard_map/ppermute | solution.py:200
  7.5 34.8 %all-to-all-start = ((bf16[8,8,4096]{2,1,0:T(8,128)(2,1)}), bf16[8,8,4096]{2,1,0:T(8,128)(2,1)S(1)}, u32[]{:S(2)}, u32[]{:S(2)}) async-start(bf16[8,8,4096]{2,1,0:T(8,128)(2,1)} %copies.1), calls=%async_computation | async-start | bytes 1048576 | tf_op jit(solution)/shard_map/all_to_all | solution.py:223
  16.7 8.4 %copy-start.1 = (bf16[64,192]{1,0:T(8,128)(2,1)S(1)}, bf16[64,192]{1,0:T(8,128)(2,1)}, u32[]{:S(2)}) copy-start(bf16[64,192]{1,0:T(8,128)(2,1)} %constant.42) | copy-start | bytes 73732
  16.8 1.3 %collective-permute-start.1 = (bf16[8,4224]{1,0:T(8,128)(2,1)S(1)}, bf16[8,4224]{1,0:T(8,128)(2,1)S(1)}, u32[]{:S(2)}, u32[]{:S(2)}) collective-permute-start(bf16[8,4224]{1,0:T(8,128)(2,1)S(1)} %collective-permute-done), channel_id=1, source_target_pairs={{0,8},{1,9},{2,10},{3,11},{4,12},{5,13},{6,14},{7,15},{8,0},{9,1},... | collective-permute-start | bytes 202760 | tf_op jit(solution)/shard_map/ppermute | solution.py:200
  18.1 15.0 %collective-permute-start.5 = (bf16[2,8,4224]{2,1,0:T(8,128)(2,1)S(1)}, bf16[2,8,4224]{2,1,0:T(8,128)(2,1)S(1)}, u32[]{:S(2)}, u32[]{:S(2)}) collective-permute-start(bf16[2,8,4224]{2,1,0:T(8,128)(2,1)S(1)} %pad_maximum_fusion), channel_id=1, source_target_pairs={{0,32},{1,33},{2,34},{3,35},{4,36},{5,37},{6,38},{7,39},{8,104},{9... | collective-permute-start | bytes 405512 | tf_op jit(solution)/shard_map/ppermute | solution.py:200
  20.4 12.7 %collective-permute-start.4 = (bf16[2,8,4224]{2,1,0:T(8,128)(2,1)S(1)}, bf16[2,8,4224]{2,1,0:T(8,128)(2,1)S(1)}, u32[]{:S(2)}, u32[]{:S(2)}) collective-permute-start(bf16[2,8,4224]{2,1,0:T(8,128)(2,1)S(1)} %pad_maximum_fusion), channel_id=1, source_target_pairs={{0,48},{1,49},{2,50},{3,51},{4,52},{5,53},{6,54},{7,55},{8,88},{9,... | collective-permute-start | bytes 405512 | tf_op jit(solution)/shard_map/ppermute | solution.py:200
  22.6 13.7 %collective-permute-start.2 = (bf16[2,8,4224]{2,1,0:T(8,128)(2,1)S(1)}, bf16[2,8,4224]{2,1,0:T(8,128)(2,1)S(1)}, u32[]{:S(2)}, u32[]{:S(2)}) collective-permute-start(bf16[2,8,4224]{2,1,0:T(8,128)(2,1)S(1)} %pad_maximum_fusion), channel_id=1, source_target_pairs={{0,16},{1,17},{2,18},{3,19},{4,20},{5,21},{6,22},{7,23},{8,120},{9... | collective-permute-start | bytes 405512 | tf_op jit(solution)/shard_map/ppermute | solution.py:200
  33.2 9.1 %collective-permute-start.9 = (bf16[4,8,4224]{2,1,0:T(8,128)(2,1)S(1)}, bf16[4,8,4224]{2,1,0:T(8,128)(2,1)S(1)}, u32[]{:S(2)}, u32[]{:S(2)}) collective-permute-start(bf16[4,8,4224]{2,1,0:T(8,128)(2,1)S(1)} %constant_dynamic-update-slice_fusion.2.refs_1_), channel_id=1, source_target_pairs={{0,8},{1,9},{2,10},{3,11},{4,12},{5,13},{6,14},{7,15},{8,0},{9,1},... | collective-permute-start | bytes 811016 | tf_op jit(solution)/shard_map/ppermute | solution.py:200
  33.3 13.5 %collective-permute-start.6 = (bf16[4,8,4224]{2,1,0:T(8,128)(2,1)S(1)}, bf16[4,8,4224]{2,1,0:T(8,128)(2,1)S(1)}, u32[]{:S(2)}, u32[]{:S(2)}) collective-permute-start(bf16[4,8,4224]{2,1,0:T(8,128)(2,1)S(1)} %constant_dynamic-update-slice_fusion.2.refs_1_), channel_id=1, source_target_pairs={{0,128},{1,129},{2,130},{3,131},{4,132},{5,133},{6,134},{7,135},{8... | collective-permute-start | bytes 811016 | tf_op jit(solution)/shard_map/ppermute | solution.py:200
  36.0 6.2 %collective-permute-start.7 = (bf16[2,8,4224]{2,1,0:T(8,128)(2,1)S(1)}, bf16[2,8,4224]{2,1,0:T(8,128)(2,1)S(1)}, u32[]{:S(2)}, u32[]{:S(2)}) collective-permute-start(bf16[2,8,4224]{2,1,0:T(8,128)(2,1)S(1)} %get-tuple-element.25), channel_id=1, source_target_pairs={{0,16},{1,17},{2,18},{3,19},{4,20},{5,21},{6,22},{7,23},{8,120},{9... | collective-permute-start | bytes 405512 | tf_op jit(solution)/shard_map/ppermute | solution.py:200
  36.4 5.9 %collective-permute-start.8 = (bf16[2,8,4224]{2,1,0:T(8,128)(2,1)S(1)}, bf16[2,8,4224]{2,1,0:T(8,128)(2,1)S(1)}, u32[]{:S(2)}, u32[]{:S(2)}) collective-permute-start(bf16[2,8,4224]{2,1,0:T(8,128)(2,1)S(1)} %collective-permute-done.2), channel_id=1, source_target_pairs={{0,8},{1,9},{2,10},{3,11},{4,12},{5,13},{6,14},{7,15},{8,0},{9,1},... | collective-permute-start | bytes 405512 | tf_op jit(solution)/shard_map/ppermute | solution.py:200
  36.5 12.9 %collective-permute-start.3 = (bf16[4,8,4224]{2,1,0:T(8,128)(2,1)S(1)}, bf16[4,8,4224]{2,1,0:T(8,128)(2,1)S(1)}, u32[]{:S(2)}, u32[]{:S(2)}) collective-permute-start(bf16[4,8,4224]{2,1,0:T(8,128)(2,1)S(1)} %constant_dynamic-update-slice_fusion.refs_0_), channel_id=1, source_target_pairs={{0,128},{1,129},{2,130},{3,131},{4,132},{5,133},{6,134},{7,135},{8... | collective-permute-start | bytes 811016 | tf_op jit(solution)/shard_map/ppermute | solution.py:200
  49.4 7.5 %collective-permute-start.12 = (bf16[4,8,4224]{2,1,0:T(8,128)(2,1)S(1)}, bf16[4,8,4224]{2,1,0:T(8,128)(2,1)S(1)}, u32[]{:S(2)}, u32[]{:S(2)}) collective-permute-start(bf16[4,8,4224]{2,1,0:T(8,128)(2,1)S(1)} %collective-permute-done.6.refs_1_), channel_id=1, source_target_pairs={{0,8},{1,9},{2,10},{3,11},{4,12},{5,13},{6,14},{7,15},{8,0},{9,1},... | collective-permute-start | bytes 811016 | tf_op jit(solution)/shard_map/ppermute | solution.py:200
  49.5 7.5 %collective-permute-start.10 = (bf16[2,8,4224]{2,1,0:T(8,128)(2,1)S(1)}, bf16[2,8,4224]{2,1,0:T(8,128)(2,1)S(1)}, u32[]{:S(2)}, u32[]{:S(2)}) collective-permute-start(bf16[2,8,4224]{2,1,0:T(8,128)(2,1)S(1)} %collective-permute-done.7.refs_2_), channel_id=1, source_target_pairs={{0,128},{1,129},{2,130},{3,131},{4,132},{5,133},{6,134},{7,135},{8... | collective-permute-start | bytes 405512 | tf_op jit(solution)/shard_map/ppermute | solution.py:200
  52.1 4.8 %collective-permute-start.11 = (bf16[2,8,4224]{2,1,0:T(8,128)(2,1)S(1)}, bf16[2,8,4224]{2,1,0:T(8,128)(2,1)S(1)}, u32[]{:S(2)}, u32[]{:S(2)}) collective-permute-start(bf16[2,8,4224]{2,1,0:T(8,128)(2,1)S(1)} %slice.13), channel_id=1, source_target_pairs={{0,8},{1,9},{2,10},{3,11},{4,12},{5,13},{6,14},{7,15},{8,0},{9,1},... | collective-permute-start | bytes 405512 | tf_op jit(solution)/shard_map/ppermute | solution.py:200

commit v10 on v9

--- a/solution.py
+++ b/solution.py
@@ -236,7 +236,7 @@
     held, first, left, right, green = lax.optimization_barrier((pair, hop[1], left, right, green))
     early = jnp.concatenate([held, first])
     far_early = moved(early, halves)
-    core_early = moved(first, cores)
+    core_early = moved(jnp.where(live, first, 0), cores)
     fourth = moved(jnp.where(live, hop[3], 0), ring(1))
     late = jnp.concatenate([hop[3], hop[2]])
     core_late = moved(late, cores)
@@ -244,8 +244,10 @@
     far_fourth = moved(fourth, halves)
     mine, other = (early, late, fourth), (core_early, core_late)
     partial = solve(seat, row, mine, other, left, right, green)
-    far_early, far_late, partial = lax.optimization_barrier((far_early, far_late, partial))
-    far_core_early = moved(far_early[2:], cores)
+    far_early, partial = lax.optimization_barrier((far_early, partial))
+    swapped = far_early[2:]
+    far_core_early = moved(swapped, cores)
+    far_late, swapped = lax.optimization_barrier((far_late, swapped))
     far_core_late = moved(far_late, cores)
     mine, other = (far_early, far_late, far_fourth), (far_core_early, far_core_late)
     partial = solve(seat, row, mine, other, left, right, green, partial)

time: 76.7 us -> 77.7 us (1.013)
  no operation moved by 1% of the time
where the time goes in v10:
time: 77.7 us; the launch traced here: 76.7 us
  starting transfers between devices  28.2 us (36%)
  waiting for transfers between devices  21.5 us (28%)
  blocking collectives  13.3 us (17%)
  Pallas kernels  10.2 us (13%)
  other arithmetic  1.64 us (2%)
  local copies, waits for them, and re-layouts  0.9 us (1%)
  between operations  0.86 us (1%)
    ppermute x13, waiting for transfers between devices, moved(): return lax.ppermute(x, AXES, pairs)  21.5 us
    ppermute x13, starting transfers between devices, moved(): return lax.ppermute(x, AXES, pairs)  19 us
    all_to_all x1, blocking collectives, exchange(): lax.all_to_all(sent, 'dist', split_axis=0, concat_axis=0, tiled=True)  13.3 us
    pallas_call x2, Pallas kernels, solve(): pl.pallas_call(functools.partial(solve_kernel, not more), out_shape=jax.S...  9.36 us
    all_to_all x1, starting transfers between devices, exchange(): lax.all_to_all(copies, 'dist', split_axis=0, concat_axis=0, tiled=True)  9.19 us
  transfers between devices with their start and end apart: 14, of which 5 were waited for; matrix products, arithmetic and copies ran while one was open for 1% of the time, Pallas kernels for 7%

profile of v10, /device:TPU:8, one launch (start us, length us, event | category | flops | bytes accessed | tf_op | source)
XLA Modules:
  0.0 76.7 jit_solution(2795436134342609900)
XLA Ops:
  0.7 0.8 %concatenate.39.x_ref = bf16[8,4224]{1,0:T(8,128)(2,1)S(1)} pad(bf16[8,4096]{1,0:T(8,128)(2,1)} %bitcast.16, bf16[]{:T(256)} %bitcast.11), padding=0_0x0_128 | pad | bytes 133122 | tf_op jit(solution)/shard_map/concatenate | solution.py:220
  1.5 5.1 %collective-permute-start = (bf16[8,4224]{1,0:T(8,128)(2,1)S(1)}, bf16[8,4224]{1,0:T(8,128)(2,1)S(1)}, u32[]{:S(2)}, u32[]{:S(2)}) collective-permute-start(bf16[8,4224]{1,0:T(8,128)(2,1)S(1)} %concatenate.39.x_ref), channel_id=1, source_target_pairs={{0,0},{1,16},{2,32},{3,48},{4,64},{5,80},{6,96},{7,112},{8,8},{9,2... | collective-permute-start | bytes 202760 | tf_op jit(solution)/shard_map/ppermute | solution.py:200
  6.6 0.9 %copies.1 = bf16[8,8,4096]{2,1,0:T(8,128)(2,1)} custom-call(bf16[8,4224]{1,0:T(8,128)(2,1)S(1)} %concatenate.39.x_ref), custom_call_target="tpu_custom_call" | custom-call | tf_op jit(solution)/shard_map/copies/pallas_call | solution.py:155
  7.5 9.2 %all-to-all-start = ((bf16[8,8,4096]{2,1,0:T(8,128)(2,1)}), bf16[8,8,4096]{2,1,0:T(8,128)(2,1)S(1)}, u32[]{:S(2)}, u32[]{:S(2)}) async-start(bf16[8,8,4096]{2,1,0:T(8,128)(2,1)} %copies.1), calls=%async_computation | async-start | bytes 1048576 | tf_op jit(solution)/shard_map/all_to_all | solution.py:223
  16.9 1.2 %collective-permute-done.1 = bf16[8,4224]{1,0:T(8,128)(2,1)S(1)} collective-permute-done((bf16[8,4224]{1,0:T(8,128)(2,1)S(1)}, bf16[8,4224]{1,0:T(8,128)(2,1)S(1)}, u32[]{:S(2)}, u32[]{:S(2)}) %collective-permute-start.1) | collective-permute-done | bytes 67616 | tf_op jit(solution)/shard_map/ppermute | solution.py:200
  18.1 2.3 %collective-permute-start.5 = (bf16[2,8,4224]{2,1,0:T(8,128)(2,1)S(1)}, bf16[2,8,4224]{2,1,0:T(8,128)(2,1)S(1)}, u32[]{:S(2)}, u32[]{:S(2)}) collective-permute-start(bf16[2,8,4224]{2,1,0:T(8,128)(2,1)S(1)} %pad_maximum_fusion), channel_id=1, source_target_pairs={{0,32},{1,33},{2,34},{3,35},{4,36},{5,37},{6,38},{7,39},{8,104},{9... | collective-permute-start | bytes 405512 | tf_op jit(solution)/shard_map/ppermute | solution.py:200
  20.4 2.3 %collective-permute-start.4 = (bf16[2,8,4224]{2,1,0:T(8,128)(2,1)S(1)}, bf16[2,8,4224]{2,1,0:T(8,128)(2,1)S(1)}, u32[]{:S(2)}, u32[]{:S(2)}) collective-permute-start(bf16[2,8,4224]{2,1,0:T(8,128)(2,1)S(1)} %pad_maximum_fusion), channel_id=1, source_target_pairs={{0,48},{1,49},{2,50},{3,51},{4,52},{5,53},{6,54},{7,55},{8,88},{9,... | collective-permute-start | bytes 405512 | tf_op jit(solution)/shard_map/ppermute | solution.py:200
  22.6 2.1 %collective-permute-start.2 = (bf16[2,8,4224]{2,1,0:T(8,128)(2,1)S(1)}, bf16[2,8,4224]{2,1,0:T(8,128)(2,1)S(1)}, u32[]{:S(2)}, u32[]{:S(2)}) collective-permute-start(bf16[2,8,4224]{2,1,0:T(8,128)(2,1)S(1)} %pad_maximum_fusion), channel_id=1, source_target_pairs={{0,16},{1,17},{2,18},{3,19},{4,20},{5,21},{6,22},{7,23},{8,120},{9... | collective-permute-start | bytes 405512 | tf_op jit(solution)/shard_map/ppermute | solution.py:200
  24.7 0.4 fusion.1.refs_7_
  25.1 8.0 %collective-permute-done.4 = bf16[2,8,4224]{2,1,0:T(8,128)(2,1)S(1)} collective-permute-done((bf16[2,8,4224]{2,1,0:T(8,128)(2,1)S(1)}, bf16[2,8,4224]{2,1,0:T(8,128)(2,1)S(1)}, u32[]{:S(2)}, u32[]{:S(2)}) %collective-permute-start.4) | collective-permute-done | bytes 135200 | tf_op jit(solution)/shard_map/ppermute | solution.py:200
  33.3 0.1 collective-permute-start.8
  33.4 0.6 collective-permute-start.7
  34.0 2.7 %collective-permute-start.9 = (bf16[4,8,4224]{2,1,0:T(8,128)(2,1)S(1)}, bf16[4,8,4224]{2,1,0:T(8,128)(2,1)S(1)}, u32[]{:S(2)}, u32[]{:S(2)}) collective-permute-start(bf16[4,8,4224]{2,1,0:T(8,128)(2,1)S(1)} %constant_dynamic-update-slice_fusion.2.refs_1_), channel_id=1, source_target_pairs={{0,128},{1,129},{2,130},{3,131},{4,132},{5,133},{6,134},{7,135},{8... | collective-permute-start | bytes 811016 | tf_op jit(solution)/shard_map/ppermute | solution.py:200
  36.7 0.8 %collective-permute-start.3 = (bf16[4,8,4224]{2,1,0:T(8,128)(2,1)S(1)}, bf16[4,8,4224]{2,1,0:T(8,128)(2,1)S(1)}, u32[]{:S(2)}, u32[]{:S(2)}) collective-permute-start(bf16[4,8,4224]{2,1,0:T(8,128)(2,1)S(1)} %get-tuple-element.26.refs_0_), channel_id=1, source_target_pairs={{0,128},{1,129},{2,130},{3,131},{4,132},{5,133},{6,134},{7,135},{8... | collective-permute-start | bytes 811016 | tf_op jit(solution)/shard_map/ppermute | solution.py:200
  37.5 1.9 %collective-permute-done.6.refs_2_ = bf16[2,8,4224]{2,1,0:T(8,128)(2,1)S(1)} collective-permute-done((bf16[2,8,4224]{2,1,0:T(8,128)(2,1)S(1)}, bf16[2,8,4224]{2,1,0:T(8,128)(2,1)S(1)}, u32[]{:S(2)}, u32[]{:S(2)}) %collective-permute-start.6) | collective-permute-done | bytes 135200 | tf_op jit(solution)/shard_map/ppermute | solution.py:200
  39.5 4.5 %solve.2.refs_8_ = f32[64,4096]{1,0:T(8,128)S(1)} custom-call(s32[1]{0:T(128)} %bitcast.4.seat_ref, bf16[64,4096]{1,0:T(8,128)(2,1)S(1)} %bitcast.12, bf16[4,8,4224]{2,1,0:T(8,128)(2,1)S(1)} %get-tuple-element.26.refs_0_, bf16[4,8,4224]{2,1,0:T(8,128)(2,1)S(1)} %constant_dynamic-update-slice_fusion.2.refs_1_, ...), custom_call_target="tpu_custom_call" | custom-call | flops 10000000000 | bytes 10000000 | tf_op jit(solution)/shard_map/solve/pallas_call | solution.py:170
  43.9 5.8 %collective-permute-done.3.refs_0_ = bf16[4,8,4224]{2,1,0:T(8,128)(2,1)S(1)} collective-permute-done((bf16[4,8,4224]{2,1,0:T(8,128)(2,1)S(1)}, bf16[4,8,4224]{2,1,0:T(8,128)(2,1)S(1)}, u32[]{:S(2)}, u32[]{:S(2)}) %collective-permute-start.3) | collective-permute-done | bytes 270368 | tf_op jit(solution)/shard_map/ppermute | solution.py:200
  49.9 2.8 %collective-permute-start.10 = (bf16[2,8,4224]{2,1,0:T(8,128)(2,1)S(1)}, bf16[2,8,4224]{2,1,0:T(8,128)(2,1)S(1)}, u32[]{:S(2)}, u32[]{:S(2)}) collective-permute-start(bf16[2,8,4224]{2,1,0:T(8,128)(2,1)S(1)} %collective-permute-done.6.refs_2_), channel_id=1, source_target_pairs={{0,128},{1,129},{2,130},{3,131},{4,132},{5,133},{6,134},{7,135},{8... | collective-permute-start | bytes 405512 | tf_op jit(solution)/shard_map/ppermute | solution.py:200
  52.7 0.1 collective-permute-start.11
  52.8 4.5 %collective-permute-done.10.refs_2_ = bf16[2,8,4224]{2,1,0:T(8,128)(2,1)S(1)} collective-permute-done((bf16[2,8,4224]{2,1,0:T(8,128)(2,1)S(1)}, bf16[2,8,4224]{2,1,0:T(8,128)(2,1)S(1)}, u32[]{:S(2)}, u32[]{:S(2)}) %collective-permute-start.10) | collective-permute-done | bytes 135200 | tf_op jit(solution)/shard_map/ppermute | solution.py:200
  57.4 4.9 %solve.3 = f32[64,4224]{1,0:T(8,128)S(1)} custom-call(s32[1]{0:T(128)} %bitcast.4.seat_ref, bf16[64,4096]{1,0:T(8,128)(2,1)S(1)} %bitcast.13, bf16[4,8,4224]{2,1,0:T(8,128)(2,1)S(1)} %collective-permute-done.3.refs_0_, bf16[4,8,4224]{2,1,0:T(8,128)(2,1)S(1)} %collective-permute-done.9.refs_1_, bf16[2,8,4224]{2,1,0:T(8,128)(2,1)S(1)} %collective-permute-done.10.refs_2_, ...), custom_call_target="tpu_custom_call" | custom-call | flops 10000000000 | bytes 10000000 | tf_op jit(solution)/shard_map/solve/pallas_call | solution.py:170
  62.4 13.3 %all_to_all.10 = f16[8,8,4224]{2,1,0:T(8,128)(2,1)S(1)} all-to-all(f16[8,8,4224]{2,1,0:T(8,128)(2,1)S(1)} %convert_bitcast_fusion), channel_id=1, replica_groups=mesh['grp'=32,'dist'=8] {'dist'}, dimensions={0} | all-to-all | bytes 1081344 | tf_op jit(solution)/shard_map/all_to_all | solution.py:255
  75.7 0.2 exponential_reduce_fusion
  75.9 0.8 %multiply_reduce_fusion = f32[8,4096]{1,0:T(8,128)} fusion(f16[8,8,4224]{2,1,0:T(8,128)(2,1)S(1)} %all_to_all.10, f32[8]{0:T(128)S(1)} %exponential_reduce_fusion), kind=kLoop, calls=%fused_computation.4 | loop fusion | flops 753664 | bytes 655392 | tf_op jit(solution)/shard_map/reduce_sum | solution.py:258
  (29 shorter events, 0.6 us)
Async XLA Ops:
  0.0 24.7 %copy-start = (bf16[256,256]{1,0:T(8,128)(2,1)S(1)}, bf16[256,256]{1,0:T(8,128)(2,1)}, u32[]{:S(2)}) copy-start(bf16[256,256]{1,0:T(8,128)(2,1)} %constant.50) | copy-start | bytes 393220
  1.5 15.2 %collective-permute-start = (bf16[8,4224]{1,0:T(8,128)(2,1)S(1)}, bf16[8,4224]{1,0:T(8,128)(2,1)S(1)}, u32[]{:S(2)}, u32[]{:S(2)}) collective-permute-start(bf16[8,4224]{1,0:T(8,128)(2,1)S(1)} %concatenate.39.x_ref), channel_id=1, source_target_pairs={{0,0},{1,16},{2,32},{3,48},{4,64},{5,80},{6,96},{7,112},{8,8},{9,2... | collective-permute-start | bytes 202760 | tf_op jit(solution)/shard_map/ppermute | solution.py:200
  7.5 32.0 %all-to-all-start = ((bf16[8,8,4096]{2,1,0:T(8,128)(2,1)}), bf16[8,8,4096]{2,1,0:T(8,128)(2,1)S(1)}, u32[]{:S(2)}, u32[]{:S(2)}) async-start(bf16[8,8,4096]{2,1,0:T(8,128)(2,1)} %copies.1), calls=%async_computation | async-start | bytes 1048576 | tf_op jit(solution)/shard_map/all_to_all | solution.py:223
  16.7 8.4 %copy-start.1 = (bf16[64,192]{1,0:T(8,128)(2,1)S(1)}, bf16[64,192]{1,0:T(8,128)(2,1)}, u32[]{:S(2)}) copy-start(bf16[64,192]{1,0:T(8,128)(2,1)} %constant.42) | copy-start | bytes 73732
  16.8 1.3 %collective-permute-start.1 = (bf16[8,4224]{1,0:T(8,128)(2,1)S(1)}, bf16[8,4224]{1,0:T(8,128)(2,1)S(1)}, u32[]{:S(2)}, u32[]{:S(2)}) collective-permute-start(bf16[8,4224]{1,0:T(8,128)(2,1)S(1)} %collective-permute-done), channel_id=1, source_target_pairs={{0,8},{1,9},{2,10},{3,11},{4,12},{5,13},{6,14},{7,15},{8,0},{9,1},... | collective-permute-start | bytes 202760 | tf_op jit(solution)/shard_map/ppermute | solution.py:200
  18.1 15.1 %collective-permute-start.5 = (bf16[2,8,4224]{2,1,0:T(8,128)(2,1)S(1)}, bf16[2,8,4224]{2,1,0:T(8,128)(2,1)S(1)}, u32[]{:S(2)}, u32[]{:S(2)}) collective-permute-start(bf16[2,8,4224]{2,1,0:T(8,128)(2,1)S(1)} %pad_maximum_fusion), channel_id=1, source_target_pairs={{0,32},{1,33},{2,34},{3,35},{4,36},{5,37},{6,38},{7,39},{8,104},{9... | collective-permute-start | bytes 405512 | tf_op jit(solution)/shard_map/ppermute | solution.py:200
  20.4 12.7 %collective-permute-start.4 = (bf16[2,8,4224]{2,1,0:T(8,128)(2,1)S(1)}, bf16[2,8,4224]{2,1,0:T(8,128)(2,1)S(1)}, u32[]{:S(2)}, u32[]{:S(2)}) collective-permute-start(bf16[2,8,4224]{2,1,0:T(8,128)(2,1)S(1)} %pad_maximum_fusion), channel_id=1, source_target_pairs={{0,48},{1,49},{2,50},{3,51},{4,52},{5,53},{6,54},{7,55},{8,88},{9,... | collective-permute-start | bytes 405512 | tf_op jit(solution)/shard_map/ppermute | solution.py:200
  22.6 10.7 %collective-permute-start.2 = (bf16[2,8,4224]{2,1,0:T(8,128)(2,1)S(1)}, bf16[2,8,4224]{2,1,0:T(8,128)(2,1)S(1)}, u32[]{:S(2)}, u32[]{:S(2)}) collective-permute-start(bf16[2,8,4224]{2,1,0:T(8,128)(2,1)S(1)} %pad_maximum_fusion), channel_id=1, source_target_pairs={{0,16},{1,17},{2,18},{3,19},{4,20},{5,21},{6,22},{7,23},{8,120},{9... | collective-permute-start | bytes 405512 | tf_op jit(solution)/shard_map/ppermute | solution.py:200
  33.1 6.3 %collective-permute-start.6 = (bf16[2,8,4224]{2,1,0:T(8,128)(2,1)S(1)}, bf16[2,8,4224]{2,1,0:T(8,128)(2,1)S(1)}, u32[]{:S(2)}, u32[]{:S(2)}) collective-permute-start(bf16[2,8,4224]{2,1,0:T(8,128)(2,1)S(1)} %get-tuple-element.27), channel_id=1, source_target_pairs={{0,16},{1,17},{2,18},{3,19},{4,20},{5,21},{6,22},{7,23},{8,120},{9... | collective-permute-start | bytes 405512 | tf_op jit(solution)/shard_map/ppermute | solution.py:200
  33.3 6.2 %collective-permute-start.8 = (bf16[4,8,4224]{2,1,0:T(8,128)(2,1)S(1)}, bf16[4,8,4224]{2,1,0:T(8,128)(2,1)S(1)}, u32[]{:S(2)}, u32[]{:S(2)}) collective-permute-start(bf16[4,8,4224]{2,1,0:T(8,128)(2,1)S(1)} %constant_dynamic-update-slice_fusion.2.refs_1_), channel_id=1, source_target_pairs={{0,8},{1,9},{2,10},{3,11},{4,12},{5,13},{6,14},{7,15},{8,0},{9,1},... | collective-permute-start | bytes 811016 | tf_op jit(solution)/shard_map/ppermute | solution.py:200
  33.4 6.0 %collective-permute-start.7 = (bf16[2,8,4224]{2,1,0:T(8,128)(2,1)S(1)}, bf16[2,8,4224]{2,1,0:T(8,128)(2,1)S(1)}, u32[]{:S(2)}, u32[]{:S(2)}) collective-permute-start(bf16[2,8,4224]{2,1,0:T(8,128)(2,1)S(1)} %get-tuple-element.25), channel_id=1, source_target_pairs={{0,8},{1,9},{2,10},{3,11},{4,12},{5,13},{6,14},{7,15},{8,0},{9,1},... | collective-permute-start | bytes 405512 | tf_op jit(solution)/shard_map/ppermute | solution.py:200
  34.0 15.8 %collective-permute-start.9 = (bf16[4,8,4224]{2,1,0:T(8,128)(2,1)S(1)}, bf16[4,8,4224]{2,1,0:T(8,128)(2,1)S(1)}, u32[]{:S(2)}, u32[]{:S(2)}) collective-permute-start(bf16[4,8,4224]{2,1,0:T(8,128)(2,1)S(1)} %constant_dynamic-update-slice_fusion.2.refs_1_), channel_id=1, source_target_pairs={{0,128},{1,129},{2,130},{3,131},{4,132},{5,133},{6,134},{7,135},{8... | collective-permute-start | bytes 811016 | tf_op jit(solution)/shard_map/ppermute | solution.py:200
  36.7 13.1 %collective-permute-start.3 = (bf16[4,8,4224]{2,1,0:T(8,128)(2,1)S(1)}, bf16[4,8,4224]{2,1,0:T(8,128)(2,1)S(1)}, u32[]{:S(2)}, u32[]{:S(2)}) collective-permute-start(bf16[4,8,4224]{2,1,0:T(8,128)(2,1)S(1)} %get-tuple-element.26.refs_0_), channel_id=1, source_target_pairs={{0,128},{1,129},{2,130},{3,131},{4,132},{5,133},{6,134},{7,135},{8... | collective-permute-start | bytes 811016 | tf_op jit(solution)/shard_map/ppermute | solution.py:200
  49.8 7.6 %collective-permute-start.12 = (bf16[4,8,4224]{2,1,0:T(8,128)(2,1)S(1)}, bf16[4,8,4224]{2,1,0:T(8,128)(2,1)S(1)}, u32[]{:S(2)}, u32[]{:S(2)}) collective-permute-start(bf16[4,8,4224]{2,1,0:T(8,128)(2,1)S(1)} %collective-permute-done.9.refs_1_), channel_id=1, source_target_pairs={{0,8},{1,9},{2,10},{3,11},{4,12},{5,13},{6,14},{7,15},{8,0},{9,1},... | collective-permute-start | bytes 811016 | tf_op jit(solution)/shard_map/ppermute | solution.py:200
  49.9 7.5 %collective-permute-start.10 = (bf16[2,8,4224]{2,1,0:T(8,128)(2,1)S(1)}, bf16[2,8,4224]{2,1,0:T(8,128)(2,1)S(1)}, u32[]{:S(2)}, u32[]{:S(2)}) collective-permute-start(bf16[2,8,4224]{2,1,0:T(8,128)(2,1)S(1)} %collective-permute-done.6.refs_2_), channel_id=1, source_target_pairs={{0,128},{1,129},{2,130},{3,131},{4,132},{5,133},{6,134},{7,135},{8... | collective-permute-start | bytes 405512 | tf_op jit(solution)/shard_map/ppermute | solution.py:200
  52.7 4.7 %collective-permute-start.11 = (bf16[2,8,4224]{2,1,0:T(8,128)(2,1)S(1)}, bf16[2,8,4224]{2,1,0:T(8,128)(2,1)S(1)}, u32[]{:S(2)}, u32[]{:S(2)}) collective-permute-start(bf16[2,8,4224]{2,1,0:T(8,128)(2,1)S(1)} %slice.13), channel_id=1, source_target_pairs={{0,8},{1,9},{2,10},{3,11},{4,12},{5,13},{6,14},{7,15},{8,0},{9,1},... | collective-permute-start | bytes 405512 | tf_op jit(solution)/shard_map/ppermute | solution.py:200

commit v11 on v10

--- a/solution.py
+++ b/solution.py
@@ -28,8 +28,8 @@
     hi = t.astype(jnp.bfloat16)
     lo = (t - hi.astype(np.float64)).astype(jnp.bfloat16)
     hi, lo = jnp.asarray(hi), jnp.asarray(lo)
-    left = jnp.concatenate([hi, hi, lo], axis=1)
     zero = jnp.zeros_like(hi)
+    left = jnp.concatenate([jnp.concatenate([hi, hi], 1), jnp.concatenate([lo, zero], 1)], 0)
     two = lambda m: jnp.concatenate([jnp.concatenate([m, zero], 1), jnp.concatenate([zero, m], 1)], 0)
     wide = jnp.concatenate([two(hi), two(lo)], axis=1)
     right = jnp.concatenate([wide, wide], axis=0)
@@ -57,7 +57,8 @@
 
 def along_rows(left, x):
     hi, lo = split(x)
-    return dot(left, jnp.concatenate([hi, lo, hi], axis=0))
+    y = dot(left, jnp.concatenate([hi, lo], axis=0))
+    return y[:GRID] + y[GRID:]
 
 
 def solve_kernel(first, seat_ref, row_ref, *refs):

time: 77.7 us -> 77.6 us (level)
  no operation moved by 1% of the time
where the time goes in v11:
time: 77.6 us; the launch traced here: 76.6 us
  starting transfers between devices  28.2 us (36%)
  waiting for transfers between devices  21.6 us (28%)
  blocking collectives  13.3 us (17%)
  Pallas kernels  9.98 us (13%)
  other arithmetic  1.64 us (2%)
  local copies, waits for them, and re-layouts  0.9 us (1%)
  between operations  0.86 us (1%)
    ppermute x13, waiting for transfers between devices, moved(): return lax.ppermute(x, AXES, pairs)  21.6 us
    ppermute x13, starting transfers between devices, moved(): return lax.ppermute(x, AXES, pairs)  19 us
    all_to_all x1, blocking collectives, exchange(): lax.all_to_all(sent, 'dist', split_axis=0, concat_axis=0, tiled=True)  13.3 us
    all_to_all x1, starting transfers between devices, exchange(): lax.all_to_all(copies, 'dist', split_axis=0, concat_axis=0, tiled=True)  9.19 us
    pallas_call x2, Pallas kernels, solve(): pl.pallas_call(functools.partial(solve_kernel, not more), out_shape=jax.S...  9.11 us
  transfers between devices with their start and end apart: 14, of which 5 were waited for; matrix products, arithmetic and copies ran while one was open for 1% of the time, Pallas kernels for 7%

profile of v11, /device:TPU:8, one launch (start us, length us, event | category | flops | bytes accessed | tf_op | source)
XLA Modules:
  0.0 76.6 jit_solution(9322905092786141461)
XLA Ops:
  0.7 0.8 %concatenate.43.x_ref = bf16[8,4224]{1,0:T(8,128)(2,1)S(1)} pad(bf16[8,4096]{1,0:T(8,128)(2,1)} %bitcast.16, bf16[]{:T(256)} %bitcast.11), padding=0_0x0_128 | pad | bytes 133122 | tf_op jit(solution)/shard_map/concatenate | solution.py:221
  1.5 5.1 %collective-permute-start = (bf16[8,4224]{1,0:T(8,128)(2,1)S(1)}, bf16[8,4224]{1,0:T(8,128)(2,1)S(1)}, u32[]{:S(2)}, u32[]{:S(2)}) collective-permute-start(bf16[8,4224]{1,0:T(8,128)(2,1)S(1)} %concatenate.43.x_ref), channel_id=1, source_target_pairs={{0,0},{1,16},{2,32},{3,48},{4,64},{5,80},{6,96},{7,112},{8,8},{9,2... | collective-permute-start | bytes 202760 | tf_op jit(solution)/shard_map/ppermute | solution.py:201
  6.6 0.9 %copies.1 = bf16[8,8,4096]{2,1,0:T(8,128)(2,1)} custom-call(bf16[8,4224]{1,0:T(8,128)(2,1)S(1)} %concatenate.43.x_ref), custom_call_target="tpu_custom_call" | custom-call | tf_op jit(solution)/shard_map/copies/pallas_call | solution.py:156
  7.5 9.2 %all-to-all-start = ((bf16[8,8,4096]{2,1,0:T(8,128)(2,1)}), bf16[8,8,4096]{2,1,0:T(8,128)(2,1)S(1)}, u32[]{:S(2)}, u32[]{:S(2)}) async-start(bf16[8,8,4096]{2,1,0:T(8,128)(2,1)} %copies.1), calls=%async_computation | async-start | bytes 1048576 | tf_op jit(solution)/shard_map/all_to_all | solution.py:224
  16.9 1.2 %collective-permute-done.1 = bf16[8,4224]{1,0:T(8,128)(2,1)S(1)} collective-permute-done((bf16[8,4224]{1,0:T(8,128)(2,1)S(1)}, bf16[8,4224]{1,0:T(8,128)(2,1)S(1)}, u32[]{:S(2)}, u32[]{:S(2)}) %collective-permute-start.1) | collective-permute-done | bytes 67616 | tf_op jit(solution)/shard_map/ppermute | solution.py:201
  18.1 2.3 %collective-permute-start.5 = (bf16[2,8,4224]{2,1,0:T(8,128)(2,1)S(1)}, bf16[2,8,4224]{2,1,0:T(8,128)(2,1)S(1)}, u32[]{:S(2)}, u32[]{:S(2)}) collective-permute-start(bf16[2,8,4224]{2,1,0:T(8,128)(2,1)S(1)} %pad_maximum_fusion), channel_id=1, source_target_pairs={{0,32},{1,33},{2,34},{3,35},{4,36},{5,37},{6,38},{7,39},{8,104},{9... | collective-permute-start | bytes 405512 | tf_op jit(solution)/shard_map/ppermute | solution.py:201
  20.4 2.3 %collective-permute-start.4 = (bf16[2,8,4224]{2,1,0:T(8,128)(2,1)S(1)}, bf16[2,8,4224]{2,1,0:T(8,128)(2,1)S(1)}, u32[]{:S(2)}, u32[]{:S(2)}) collective-permute-start(bf16[2,8,4224]{2,1,0:T(8,128)(2,1)S(1)} %pad_maximum_fusion), channel_id=1, source_target_pairs={{0,48},{1,49},{2,50},{3,51},{4,52},{5,53},{6,54},{7,55},{8,88},{9,... | collective-permute-start | bytes 405512 | tf_op jit(solution)/shard_map/ppermute | solution.py:201
  22.6 2.1 %collective-permute-start.2 = (bf16[2,8,4224]{2,1,0:T(8,128)(2,1)S(1)}, bf16[2,8,4224]{2,1,0:T(8,128)(2,1)S(1)}, u32[]{:S(2)}, u32[]{:S(2)}) collective-permute-start(bf16[2,8,4224]{2,1,0:T(8,128)(2,1)S(1)} %pad_maximum_fusion), channel_id=1, source_target_pairs={{0,16},{1,17},{2,18},{3,19},{4,20},{5,21},{6,22},{7,23},{8,120},{9... | collective-permute-start | bytes 405512 | tf_op jit(solution)/shard_map/ppermute | solution.py:201
  24.7 0.4 fusion.1.refs_7_
  25.1 8.0 %collective-permute-done.4 = bf16[2,8,4224]{2,1,0:T(8,128)(2,1)S(1)} collective-permute-done((bf16[2,8,4224]{2,1,0:T(8,128)(2,1)S(1)}, bf16[2,8,4224]{2,1,0:T(8,128)(2,1)S(1)}, u32[]{:S(2)}, u32[]{:S(2)}) %collective-permute-start.4) | collective-permute-done | bytes 135200 | tf_op jit(solution)/shard_map/ppermute | solution.py:201
  33.3 0.1 collective-permute-start.8
  33.4 0.6 collective-permute-start.7
  34.0 2.7 %collective-permute-start.9 = (bf16[4,8,4224]{2,1,0:T(8,128)(2,1)S(1)}, bf16[4,8,4224]{2,1,0:T(8,128)(2,1)S(1)}, u32[]{:S(2)}, u32[]{:S(2)}) collective-permute-start(bf16[4,8,4224]{2,1,0:T(8,128)(2,1)S(1)} %constant_dynamic-update-slice_fusion.2.refs_1_), channel_id=1, source_target_pairs={{0,128},{1,129},{2,130},{3,131},{4,132},{5,133},{6,134},{7,135},{8... | collective-permute-start | bytes 811016 | tf_op jit(solution)/shard_map/ppermute | solution.py:201
  36.7 0.8 %collective-permute-start.3 = (bf16[4,8,4224]{2,1,0:T(8,128)(2,1)S(1)}, bf16[4,8,4224]{2,1,0:T(8,128)(2,1)S(1)}, u32[]{:S(2)}, u32[]{:S(2)}) collective-permute-start(bf16[4,8,4224]{2,1,0:T(8,128)(2,1)S(1)} %get-tuple-element.26.refs_0_), channel_id=1, source_target_pairs={{0,128},{1,129},{2,130},{3,131},{4,132},{5,133},{6,134},{7,135},{8... | collective-permute-start | bytes 811016 | tf_op jit(solution)/shard_map/ppermute | solution.py:201
  37.5 1.9 %collective-permute-done.6.refs_2_ = bf16[2,8,4224]{2,1,0:T(8,128)(2,1)S(1)} collective-permute-done((bf16[2,8,4224]{2,1,0:T(8,128)(2,1)S(1)}, bf16[2,8,4224]{2,1,0:T(8,128)(2,1)S(1)}, u32[]{:S(2)}, u32[]{:S(2)}) %collective-permute-start.6) | collective-permute-done | bytes 135200 | tf_op jit(solution)/shard_map/ppermute | solution.py:201
  39.5 4.4 %solve.2.refs_8_ = f32[64,4096]{1,0:T(8,128)S(1)} custom-call(s32[1]{0:T(128)} %bitcast.4.seat_ref, bf16[64,4096]{1,0:T(8,128)(2,1)S(1)} %bitcast.12, bf16[4,8,4224]{2,1,0:T(8,128)(2,1)S(1)} %get-tuple-element.26.refs_0_, bf16[4,8,4224]{2,1,0:T(8,128)(2,1)S(1)} %constant_dynamic-update-slice_fusion.2.refs_1_, ...), custom_call_target="tpu_custom_call" | custom-call | flops 10000000000 | bytes 10000000 | tf_op jit(solution)/shard_map/solve/pallas_call | solution.py:171
  43.8 6.0 %collective-permute-done.3.refs_0_ = bf16[4,8,4224]{2,1,0:T(8,128)(2,1)S(1)} collective-permute-done((bf16[4,8,4224]{2,1,0:T(8,128)(2,1)S(1)}, bf16[4,8,4224]{2,1,0:T(8,128)(2,1)S(1)}, u32[]{:S(2)}, u32[]{:S(2)}) %collective-permute-start.3) | collective-permute-done | bytes 270368 | tf_op jit(solution)/shard_map/ppermute | solution.py:201
  49.9 2.8 %collective-permute-start.10 = (bf16[2,8,4224]{2,1,0:T(8,128)(2,1)S(1)}, bf16[2,8,4224]{2,1,0:T(8,128)(2,1)S(1)}, u32[]{:S(2)}, u32[]{:S(2)}) collective-permute-start(bf16[2,8,4224]{2,1,0:T(8,128)(2,1)S(1)} %collective-permute-done.6.refs_2_), channel_id=1, source_target_pairs={{0,128},{1,129},{2,130},{3,131},{4,132},{5,133},{6,134},{7,135},{8... | collective-permute-start | bytes 405512 | tf_op jit(solution)/shard_map/ppermute | solution.py:201
  52.7 0.1 collective-permute-start.11
  52.8 4.5 %collective-permute-done.10.refs_2_ = bf16[2,8,4224]{2,1,0:T(8,128)(2,1)S(1)} collective-permute-done((bf16[2,8,4224]{2,1,0:T(8,128)(2,1)S(1)}, bf16[2,8,4224]{2,1,0:T(8,128)(2,1)S(1)}, u32[]{:S(2)}, u32[]{:S(2)}) %collective-permute-start.10) | collective-permute-done | bytes 135200 | tf_op jit(solution)/shard_map/ppermute | solution.py:201
  57.4 4.8 %solve.3 = f32[64,4224]{1,0:T(8,128)S(1)} custom-call(s32[1]{0:T(128)} %bitcast.4.seat_ref, bf16[64,4096]{1,0:T(8,128)(2,1)S(1)} %bitcast.13, bf16[4,8,4224]{2,1,0:T(8,128)(2,1)S(1)} %collective-permute-done.3.refs_0_, bf16[4,8,4224]{2,1,0:T(8,128)(2,1)S(1)} %collective-permute-done.9.refs_1_, bf16[2,8,4224]{2,1,0:T(8,128)(2,1)S(1)} %collective-permute-done.10.refs_2_, ...), custom_call_target="tpu_custom_call" | custom-call | flops 10000000000 | bytes 10000000 | tf_op jit(solution)/shard_map/solve/pallas_call | solution.py:171
  62.2 13.3 %all_to_all.10 = f16[8,8,4224]{2,1,0:T(8,128)(2,1)S(1)} all-to-all(f16[8,8,4224]{2,1,0:T(8,128)(2,1)S(1)} %convert_bitcast_fusion), channel_id=1, replica_groups=mesh['grp'=32,'dist'=8] {'dist'}, dimensions={0} | all-to-all | bytes 1081344 | tf_op jit(solution)/shard_map/all_to_all | solution.py:256
  75.6 0.2 exponential_reduce_fusion
  75.7 0.8 %multiply_reduce_fusion = f32[8,4096]{1,0:T(8,128)} fusion(f16[8,8,4224]{2,1,0:T(8,128)(2,1)S(1)} %all_to_all.10, f32[8]{0:T(128)S(1)} %exponential_reduce_fusion), kind=kLoop, calls=%fused_computation.4 | loop fusion | flops 753664 | bytes 655392 | tf_op jit(solution)/shard_map/reduce_sum | solution.py:259
  (29 shorter events, 0.6 us)
Async XLA Ops:
  0.0 24.7 %copy-start = (bf16[256,256]{1,0:T(8,128)(2,1)S(1)}, bf16[256,256]{1,0:T(8,128)(2,1)}, u32[]{:S(2)}) copy-start(bf16[256,256]{1,0:T(8,128)(2,1)} %constant.51) | copy-start | bytes 393220
  1.5 15.2 %collective-permute-start = (bf16[8,4224]{1,0:T(8,128)(2,1)S(1)}, bf16[8,4224]{1,0:T(8,128)(2,1)S(1)}, u32[]{:S(2)}, u32[]{:S(2)}) collective-permute-start(bf16[8,4224]{1,0:T(8,128)(2,1)S(1)} %concatenate.43.x_ref), channel_id=1, source_target_pairs={{0,0},{1,16},{2,32},{3,48},{4,64},{5,80},{6,96},{7,112},{8,8},{9,2... | collective-permute-start | bytes 202760 | tf_op jit(solution)/shard_map/ppermute | solution.py:201
  7.5 32.0 %all-to-all-start = ((bf16[8,8,4096]{2,1,0:T(8,128)(2,1)}), bf16[8,8,4096]{2,1,0:T(8,128)(2,1)S(1)}, u32[]{:S(2)}, u32[]{:S(2)}) async-start(bf16[8,8,4096]{2,1,0:T(8,128)(2,1)} %copies.1), calls=%async_computation | async-start | bytes 1048576 | tf_op jit(solution)/shard_map/all_to_all | solution.py:224
  16.7 8.4 %copy-start.1 = (bf16[128,128]{1,0:T(8,128)(2,1)S(1)}, bf16[128,128]{1,0:T(8,128)(2,1)}, u32[]{:S(2)}) copy-start(bf16[128,128]{1,0:T(8,128)(2,1)} %constant.44) | copy-start | bytes 98308
  16.8 1.3 %collective-permute-start.1 = (bf16[8,4224]{1,0:T(8,128)(2,1)S(1)}, bf16[8,4224]{1,0:T(8,128)(2,1)S(1)}, u32[]{:S(2)}, u32[]{:S(2)}) collective-permute-start(bf16[8,4224]{1,0:T(8,128)(2,1)S(1)} %collective-permute-done), channel_id=1, source_target_pairs={{0,8},{1,9},{2,10},{3,11},{4,12},{5,13},{6,14},{7,15},{8,0},{9,1},... | collective-permute-start | bytes 202760 | tf_op jit(solution)/shard_map/ppermute | solution.py:201
  18.1 15.1 %collective-permute-start.5 = (bf16[2,8,4224]{2,1,0:T(8,128)(2,1)S(1)}, bf16[2,8,4224]{2,1,0:T(8,128)(2,1)S(1)}, u32[]{:S(2)}, u32[]{:S(2)}) collective-permute-start(bf16[2,8,4224]{2,1,0:T(8,128)(2,1)S(1)} %pad_maximum_fusion), channel_id=1, source_target_pairs={{0,32},{1,33},{2,34},{3,35},{4,36},{5,37},{6,38},{7,39},{8,104},{9... | collective-permute-start | bytes 405512 | tf_op jit(solution)/shard_map/ppermute | solution.py:201
  20.4 12.7 %collective-permute-start.4 = (bf16[2,8,4224]{2,1,0:T(8,128)(2,1)S(1)}, bf16[2,8,4224]{2,1,0:T(8,128)(2,1)S(1)}, u32[]{:S(2)}, u32[]{:S(2)}) collective-permute-start(bf16[2,8,4224]{2,1,0:T(8,128)(2,1)S(1)} %pad_maximum_fusion), channel_id=1, source_target_pairs={{0,48},{1,49},{2,50},{3,51},{4,52},{5,53},{6,54},{7,55},{8,88},{9,... | collective-permute-start | bytes 405512 | tf_op jit(solution)/shard_map/ppermute | solution.py:201
  22.6 10.7 %collective-permute-start.2 = (bf16[2,8,4224]{2,1,0:T(8,128)(2,1)S(1)}, bf16[2,8,4224]{2,1,0:T(8,128)(2,1)S(1)}, u32[]{:S(2)}, u32[]{:S(2)}) collective-permute-start(bf16[2,8,4224]{2,1,0:T(8,128)(2,1)S(1)} %pad_maximum_fusion), channel_id=1, source_target_pairs={{0,16},{1,17},{2,18},{3,19},{4,20},{5,21},{6,22},{7,23},{8,120},{9... | collective-permute-start | bytes 405512 | tf_op jit(solution)/shard_map/ppermute | solution.py:201
  33.1 6.3 %collective-permute-start.6 = (bf16[2,8,4224]{2,1,0:T(8,128)(2,1)S(1)}, bf16[2,8,4224]{2,1,0:T(8,128)(2,1)S(1)}, u32[]{:S(2)}, u32[]{:S(2)}) collective-permute-start(bf16[2,8,4224]{2,1,0:T(8,128)(2,1)S(1)} %get-tuple-element.27), channel_id=1, source_target_pairs={{0,16},{1,17},{2,18},{3,19},{4,20},{5,21},{6,22},{7,23},{8,120},{9... | collective-permute-start | bytes 405512 | tf_op jit(solution)/shard_map/ppermute | solution.py:201
  33.3 6.2 %collective-permute-start.8 = (bf16[4,8,4224]{2,1,0:T(8,128)(2,1)S(1)}, bf16[4,8,4224]{2,1,0:T(8,128)(2,1)S(1)}, u32[]{:S(2)}, u32[]{:S(2)}) collective-permute-start(bf16[4,8,4224]{2,1,0:T(8,128)(2,1)S(1)} %constant_dynamic-update-slice_fusion.2.refs_1_), channel_id=1, source_target_pairs={{0,8},{1,9},{2,10},{3,11},{4,12},{5,13},{6,14},{7,15},{8,0},{9,1},... | collective-permute-start | bytes 811016 | tf_op jit(solution)/shard_map/ppermute | solution.py:201
  33.4 6.0 %collective-permute-start.7 = (bf16[2,8,4224]{2,1,0:T(8,128)(2,1)S(1)}, bf16[2,8,4224]{2,1,0:T(8,128)(2,1)S(1)}, u32[]{:S(2)}, u32[]{:S(2)}) collective-permute-start(bf16[2,8,4224]{2,1,0:T(8,128)(2,1)S(1)} %get-tuple-element.25), channel_id=1, source_target_pairs={{0,8},{1,9},{2,10},{3,11},{4,12},{5,13},{6,14},{7,15},{8,0},{9,1},... | collective-permute-start | bytes 405512 | tf_op jit(solution)/shard_map/ppermute | solution.py:201
  34.0 15.8 %collective-permute-start.9 = (bf16[4,8,4224]{2,1,0:T(8,128)(2,1)S(1)}, bf16[4,8,4224]{2,1,0:T(8,128)(2,1)S(1)}, u32[]{:S(2)}, u32[]{:S(2)}) collective-permute-start(bf16[4,8,4224]{2,1,0:T(8,128)(2,1)S(1)} %constant_dynamic-update-slice_fusion.2.refs_1_), channel_id=1, source_target_pairs={{0,128},{1,129},{2,130},{3,131},{4,132},{5,133},{6,134},{7,135},{8... | collective-permute-start | bytes 811016 | tf_op jit(solution)/shard_map/ppermute | solution.py:201
  36.7 13.1 %collective-permute-start.3 = (bf16[4,8,4224]{2,1,0:T(8,128)(2,1)S(1)}, bf16[4,8,4224]{2,1,0:T(8,128)(2,1)S(1)}, u32[]{:S(2)}, u32[]{:S(2)}) collective-permute-start(bf16[4,8,4224]{2,1,0:T(8,128)(2,1)S(1)} %get-tuple-element.26.refs_0_), channel_id=1, source_target_pairs={{0,128},{1,129},{2,130},{3,131},{4,132},{5,133},{6,134},{7,135},{8... | collective-permute-start | bytes 811016 | tf_op jit(solution)/shard_map/ppermute | solution.py:201
  49.8 7.6 %collective-permute-start.12 = (bf16[4,8,4224]{2,1,0:T(8,128)(2,1)S(1)}, bf16[4,8,4224]{2,1,0:T(8,128)(2,1)S(1)}, u32[]{:S(2)}, u32[]{:S(2)}) collective-permute-start(bf16[4,8,4224]{2,1,0:T(8,128)(2,1)S(1)} %collective-permute-done.9.refs_1_), channel_id=1, source_target_pairs={{0,8},{1,9},{2,10},{3,11},{4,12},{5,13},{6,14},{7,15},{8,0},{9,1},... | collective-permute-start | bytes 811016 | tf_op jit(solution)/shard_map/ppermute | solution.py:201
  49.9 7.5 %collective-permute-start.10 = (bf16[2,8,4224]{2,1,0:T(8,128)(2,1)S(1)}, bf16[2,8,4224]{2,1,0:T(8,128)(2,1)S(1)}, u32[]{:S(2)}, u32[]{:S(2)}) collective-permute-start(bf16[2,8,4224]{2,1,0:T(8,128)(2,1)S(1)} %collective-permute-done.6.refs_2_), channel_id=1, source_target_pairs={{0,128},{1,129},{2,130},{3,131},{4,132},{5,133},{6,134},{7,135},{8... | collective-permute-start | bytes 405512 | tf_op jit(solution)/shard_map/ppermute | solution.py:201
  52.7 4.7 %collective-permute-start.11 = (bf16[2,8,4224]{2,1,0:T(8,128)(2,1)S(1)}, bf16[2,8,4224]{2,1,0:T(8,128)(2,1)S(1)}, u32[]{:S(2)}, u32[]{:S(2)}) collective-permute-start(bf16[2,8,4224]{2,1,0:T(8,128)(2,1)S(1)} %slice.13), channel_id=1, source_target_pairs={{0,8},{1,9},{2,10},{3,11},{4,12},{5,13},{6,14},{7,15},{8,0},{9,1},... | collective-permute-start | bytes 405512 | tf_op jit(solution)/shard_map/ppermute | solution.py:201
